TPU v7x, 32 devices: a whole 2x2x4 slice. The times are simulated.
32 devices in a mesh: seq: 8 (over y, x, core), stream: 4 (over z).
Axes of the slice: x: 2, y: 2, z: 4, core: 2. Of those that a mesh axis runs over, the one named last changes fastest.
Arguments:
- inputs: bfloat16 [4, 8192, 768], P('stream', 'seq'), may hold values from -11 to 11
- resets: int32 [4, 8192], P('stream', 'seq'), may hold values 0 or 1
- norm_gains: bfloat16 [768, 2], P(('seq', 'stream')), may hold values from 0.5 to 1.5
- norm_biases: bfloat16 [768, 2], P(('seq', 'stream')), may hold values from -1.25 to 1.25
- w_qkv: bfloat16 [768, 2304], P(('seq', 'stream')), may hold values from -1 to 1
- w_feat: bfloat16 [768, 128], P(('seq', 'stream')), may hold values from -0.75 to 0.75
- w_out: bfloat16 [768, 768], P(('seq', 'stream')), may hold values from -0.875 to 0.875
- w_fc: bfloat16 [768, 3072], P(('seq', 'stream')), may hold values from -1 to 1
- w_proj: bfloat16 [3072, 768], P(('seq', 'stream')), may hold values from -0.109375 to 0.109375
- cotangent: bfloat16 [4, 8192, 768], P('stream', 'seq'), may hold values from -6 to 6
Outputs:
- outputs: bfloat16 [4, 8192, 768], P('stream', 'seq')
- input_grad: float32 [4, 8192, 768], P('stream', 'seq')
- grad_gains: float32 [768, 2], P(('seq', 'stream'))
- grad_biases: float32 [768, 2], P(('seq', 'stream'))
- grad_qkv: float32 [768, 2304], P(('seq', 'stream'))
- grad_feat: float32 [768, 128], P(('seq', 'stream'))
- grad_out: float32 [768, 768], P(('seq', 'stream'))
- grad_fc: float32 [768, 3072], P(('seq', 'stream'))
- grad_proj: float32 [3072, 768], P(('seq', 'stream'))
- branch_rms: float32 [4, 3], P('stream')
Inputs may be any that keep to these rules, and one draw needn't show every extreme that they name: `resets`: A stream's first token starts a document whether it is marked or not.
All inputs are finite; a program needn't handle non-finite values. No bound on the sum of `resets` on one device may be relied on, other than what follows from the above.
Results may differ from a plain program's by a relative error of at most 0.015.
Values may be sent and summed in bfloat16 or wider, within the bound.
No kernel may reach another device: no remote copies, remote signals or barrier semaphores. Data moves between devices by JAX's collectives and lax.ppermute only.
A program may use at most 256 MiB of HBM per device.

v0:
```python
from functools import partial

import jax
import jax.numpy as jnp
from jax import lax
from jax.sharding import PartitionSpec as P

BLOCK = 64


highest = lax.Precision.HIGHEST
epsilon = 1e-05


def entering(shard, axis, join, neutral):
    place = lax.axis_index(axis)
    gathered = jax.tree.map(
        lambda a, kind: lax.all_gather(a.astype(kind), axis),
        shard,
        (jnp.bfloat16, jnp.bfloat16, jnp.bfloat16),
    )
    state = jax.tree.map(lambda a, e: jnp.zeros_like(a) + jnp.asarray(e, a.dtype), shard, neutral)

    def entering_one(step, state):
        return join(
            state,
            jax.tree.map(
                lambda a, own: lax.dynamic_index_in_dim(a, step, 0, False).astype(own.dtype),
                gathered,
                shard,
            ),
        )

    return lax.fori_loop(0, place, entering_one, state)


def carried_in(shard, axis, join, neutral):
    count = lax.axis_size(axis)
    place = lax.axis_index(axis)
    ahead = count - 1 - place
    gathered = jax.tree.map(
        lambda a, kind: lax.all_gather(a.astype(kind), axis),
        shard,
        jax.tree.map(lambda a: jnp.bfloat16 if a.dtype == jnp.float32 else a.dtype, shard),
    )
    state = jax.tree.map(lambda a, e: jnp.zeros_like(a) + jnp.asarray(e, a.dtype), shard, neutral)

    def carried_one(step, state):
        source = count - 1 - step
        return join(
            state,
            jax.tree.map(
                lambda a, own: lax.dynamic_index_in_dim(a, source, 0, False).astype(own.dtype),
                gathered,
                shard,
            ),
        )

    return lax.fori_loop(0, ahead, carried_one, state)


def layer_norm(values, gain_vec, bias_vec):
    row_mean = jnp.mean(values, axis=-1, keepdims=True)
    centered = values - row_mean
    variance = jnp.mean(centered * centered, axis=-1, keepdims=True)
    return centered * lax.rsqrt(variance + epsilon) * gain_vec + bias_vec


def feature(logits):
    return jnp.concatenate(
        [jax.nn.softmax(logits, axis=-1), jax.nn.softmax(-logits, axis=-1)], axis=-1
    )


def dot_last(left_in, right_in):
    return jnp.dot(left_in, right_in, preferred_element_type=jnp.float32)


def dot_first(left_in, right_in):
    return lax.dot_general(
        left_in, right_in, (((0,), (0,)), ((), ())), preferred_element_type=jnp.float32
    )


def dot_trans(left_in, right_in):
    return lax.dot_general(
        left_in, right_in, (((1,), (1,)), ((), ())), preferred_element_type=jnp.float32
    )


def segmented(earlier, latter):
    return (
        earlier[0] * latter[0],
        latter[0] * earlier[1] + latter[1],
        latter[0] * earlier[2] + latter[2],
    )


def advance(carried, piece_in):
    kv_block, z_block, keep_one = piece_in
    return ((keep_one * carried[0] + kv_block, keep_one * carried[1] + z_block), carried)


def shards(inputs, resets, norm_gains, norm_biases, w_qkv, w_feat, w_out, w_fc, w_proj, cotangent):
    weights = (
        lax.all_gather(norm_gains, ("seq", "stream"), axis=0, tiled=True),
        lax.all_gather(norm_biases, ("seq", "stream"), axis=0, tiled=True),
        lax.all_gather(w_qkv, ("seq", "stream"), axis=0, tiled=True),
        lax.all_gather(w_feat, ("seq", "stream"), axis=0, tiled=True),
        lax.all_gather(w_out, ("seq", "stream"), axis=0, tiled=True),
        lax.all_gather(w_fc, ("seq", "stream"), axis=0, tiled=True),
        lax.all_gather(w_proj, ("seq", "stream"), axis=0, tiled=True),
    )
    gain_full = weights[0].astype(jnp.float32)
    bias_full = weights[1].astype(jnp.float32)
    tokens = inputs.shape[1]
    model_width = inputs.shape[2]
    head_dim = weights[3].shape[1] // 2
    head_count = model_width // head_dim
    feat_dim = 2 * head_dim
    nblocks = tokens // BLOCK
    f32 = jnp.float32
    bf16 = jnp.bfloat16
    x_in = inputs[0].astype(f32)
    normed_one, norm1_back = jax.vjp(layer_norm, x_in, gain_full[:, 0], bias_full[:, 0])
    h_one = normed_one.astype(bf16)
    qkv_rows = dot_last(h_one, weights[2]).astype(bf16)
    queries = qkv_rows[:, :model_width].reshape(tokens, head_count, head_dim)
    keys_in = qkv_rows[:, model_width : 2 * model_width].reshape(tokens, head_count, head_dim)
    value_rows = qkv_rows[:, 2 * model_width :].reshape(tokens, head_count, head_dim)
    feature_maps = weights[3].reshape(head_count, head_dim, feat_dim)
    q_logits = jnp.einsum(
        "thi,hij->thj", queries, feature_maps[:, :, :head_dim], preferred_element_type=f32
    )
    k_logits = jnp.einsum(
        "thi,hij->thj", keys_in, feature_maps[:, :, head_dim:], preferred_element_type=f32
    )
    phi_q_f, phi_q_back = jax.vjp(feature, q_logits)
    phi_k_f, phi_k_back = jax.vjp(feature, k_logits)

    def to_blocks(tensor):
        return tensor.reshape(nblocks, BLOCK, head_count, tensor.shape[-1]).transpose(0, 2, 1, 3)

    def from_blocks(tensor):
        return tensor.transpose(0, 2, 1, 3).reshape(tokens, head_count, tensor.shape[-1])

    phi_qb = to_blocks(phi_q_f.astype(bf16))
    phi_kb = to_blocks(phi_k_f.astype(bf16))
    value_blk = to_blocks(value_rows)
    reset_rows = resets[0].reshape(nblocks, BLOCK)
    counts = jnp.cumsum(reset_rows, axis=1)
    row_ids = jnp.arange(BLOCK)
    doc_mask = (
        (row_ids[None, :, None] >= row_ids[None, None, :])
        & (counts[:, :, None] == counts[:, None, :])
    ).astype(f32)
    before = (counts == 0).astype(f32)
    after_last = (counts == counts[:, -1:]).astype(f32)
    keep_block = (counts[:, -1] == 0).astype(f32)
    before_prod = jnp.cumprod(jnp.concatenate([jnp.ones((1,), f32), keep_block[:-1]]))
    after_prod = jnp.cumprod(jnp.concatenate([keep_block[1:], jnp.ones((1,), f32)])[::-1])[::-1]
    keep_dev = jnp.prod(keep_block)
    scores = (
        jnp.einsum("nhcf,nhsf->nhcs", phi_qb, phi_kb, preferred_element_type=f32)
        * doc_mask[:, None]
    )
    scores_b = scores.astype(bf16)
    intra_num = jnp.einsum("nhcs,nhsd->nhcd", scores_b, value_blk, preferred_element_type=f32)
    intra_den = jnp.sum(scores_b, axis=-1, dtype=f32)
    keyed_phi = phi_kb * after_last[:, None, :, None].astype(bf16)
    block_kv = jnp.einsum("nhsf,nhsd->nhfd", keyed_phi, value_blk, preferred_element_type=f32)
    block_z = jnp.sum(keyed_phi, axis=2, dtype=f32)
    zeros_kv = jnp.zeros((head_count, feat_dim, head_dim), f32)
    zeros_z = jnp.zeros((head_count, feat_dim), f32)
    dev_kv = jnp.einsum("n,nhfd->hfd", after_prod, block_kv, precision=highest)
    dev_z = jnp.einsum("n,nhf->hf", after_prod, block_z, precision=highest)
    incoming = entering(
        (keep_dev, dev_kv, dev_z), "seq", segmented, (jnp.ones((), f32), zeros_kv, zeros_z)
    )
    ignored, (start_kv, start_z) = lax.scan(
        advance, (incoming[1], incoming[2]), (block_kv, block_z, keep_block)
    )
    phi_qf = phi_qb.astype(f32)
    inter_num = jnp.einsum("nhcf,nhfd->nhcd", phi_qf, start_kv, precision=highest)
    inter_den = jnp.einsum("nhcf,nhf->nhc", phi_qf, start_z, precision=highest)
    numerator = intra_num + before[:, None, :, None] * inter_num
    denominator = intra_den + before[:, None, :] * inter_den
    attended = numerator / denominator[..., None]
    att_b = from_blocks(attended).reshape(tokens, model_width).astype(bf16)
    attn_out = dot_last(att_b, weights[4])
    middle = x_in + attn_out
    normed_two, norm2_back = jax.vjp(layer_norm, middle, gain_full[:, 1], bias_full[:, 1])
    h_two = normed_two.astype(bf16)
    fc_pre = dot_last(h_two, weights[5])
    activated, gelu_back = jax.vjp(partial(jax.nn.gelu, approximate=True), fc_pre)
    act_b = activated.astype(bf16)
    mlp_out = dot_last(act_b, weights[6])
    result = middle + mlp_out
    squares = jnp.stack(
        [jnp.sum(attn_out * attn_out), jnp.sum(mlp_out * mlp_out), jnp.sum(result * result)]
    )
    totals = lax.psum(squares, "seq")
    branch_rms = jnp.sqrt(totals / (tokens * lax.axis_size("seq") * model_width)).reshape(1, 3)
    regathered = (
        lax.all_gather(norm_gains, ("seq", "stream"), axis=0, tiled=True),
        lax.all_gather(norm_biases, ("seq", "stream"), axis=0, tiled=True),
        lax.all_gather(w_qkv, ("seq", "stream"), axis=0, tiled=True),
        lax.all_gather(w_feat, ("seq", "stream"), axis=0, tiled=True),
        lax.all_gather(w_out, ("seq", "stream"), axis=0, tiled=True),
        lax.all_gather(w_fc, ("seq", "stream"), axis=0, tiled=True),
        lax.all_gather(w_proj, ("seq", "stream"), axis=0, tiled=True),
    )
    maps_back = regathered[3].reshape(head_count, head_dim, feat_dim)
    d_out_b = cotangent[0]
    d_out = d_out_b.astype(f32)
    grad_proj = dot_first(act_b, d_out_b)
    d_act = dot_trans(d_out_b, regathered[6])
    (d_fc,) = gelu_back(d_act)
    d_fc_b = d_fc.astype(bf16)
    grad_fc = dot_first(h_two, d_fc_b)
    d_h_two = dot_trans(d_fc_b, regathered[5])
    d_mid_ln, d_gain_two, d_bias_two = norm2_back(d_h_two)
    d_middle = d_out + d_mid_ln
    d_attn_b = d_middle.astype(bf16)
    grad_out = dot_first(att_b, d_attn_b)
    d_att = to_blocks(dot_trans(d_attn_b, regathered[4]).reshape(tokens, head_count, head_dim))
    d_num = (d_att / denominator[..., None]).astype(bf16)
    d_num_f = d_num.astype(f32)
    d_den = -jnp.sum(d_att * attended, axis=-1) / denominator
    phi_q_used = phi_qf * before[:, None, :, None]
    g_block_kv = jnp.einsum("nhcf,nhcd->nhfd", phi_q_used, d_num_f, precision=highest)
    g_block_z = jnp.einsum("nhcf,nhc->nhf", phi_q_used, d_den, precision=highest)
    dev_g_kv = jnp.einsum("n,nhfd->hfd", before_prod, g_block_kv, precision=highest)
    dev_g_z = jnp.einsum("n,nhf->hf", before_prod, g_block_z, precision=highest)
    returning = carried_in(
        (keep_dev, dev_g_kv, dev_g_z), "seq", segmented, (jnp.ones((), f32), zeros_kv, zeros_z)
    )
    ignored, (after_dkv, after_dz) = lax.scan(
        advance, (returning[1], returning[2]), (g_block_kv, g_block_z, keep_block), reverse=True
    )
    d_scores = (
        jnp.einsum("nhcd,nhsd->nhcs", d_num, value_blk, preferred_element_type=f32)
        + d_den[..., None]
    )
    d_scores_b = (d_scores * doc_mask[:, None]).astype(bf16)
    d_phi_q = jnp.einsum("nhcs,nhsf->nhcf", d_scores_b, phi_kb, preferred_element_type=f32)
    d_phi_q = d_phi_q + before[:, None, :, None] * (
        jnp.einsum("nhfd,nhcd->nhcf", start_kv, d_num_f, precision=highest)
        + d_den[..., None] * start_z[:, :, None, :]
    )
    d_phi_k = jnp.einsum("nhcs,nhcf->nhsf", d_scores_b, phi_qb, preferred_element_type=f32)
    d_phi_k = d_phi_k + after_last[:, None, :, None] * (
        jnp.einsum("nhfd,nhsd->nhsf", after_dkv, value_blk.astype(f32), precision=highest)
        + after_dz[:, :, None, :]
    )
    d_values = jnp.einsum("nhcs,nhcd->nhsd", scores_b, d_num, preferred_element_type=f32)
    d_values = d_values + jnp.einsum(
        "nhsf,nhfd->nhsd", keyed_phi.astype(f32), after_dkv, precision=highest
    )
    (d_q_logits,) = phi_q_back(from_blocks(d_phi_q))
    (d_k_logits,) = phi_k_back(from_blocks(d_phi_k))
    d_q_b = d_q_logits.astype(bf16)
    d_k_b = d_k_logits.astype(bf16)
    grad_map_q = jnp.einsum("thi,thj->hij", queries, d_q_b, preferred_element_type=f32)
    grad_map_k = jnp.einsum("thi,thj->hij", keys_in, d_k_b, preferred_element_type=f32)
    d_queries = jnp.einsum(
        "thj,hij->thi", d_q_b, maps_back[:, :, :head_dim], preferred_element_type=f32
    )
    d_keys = jnp.einsum(
        "thj,hij->thi", d_k_b, maps_back[:, :, head_dim:], preferred_element_type=f32
    )
    d_qkv = jnp.concatenate(
        [
            d_queries.reshape(tokens, model_width),
            d_keys.reshape(tokens, model_width),
            from_blocks(d_values).reshape(tokens, model_width),
        ],
        axis=1,
    ).astype(bf16)
    grad_qkv = dot_first(h_one, d_qkv)
    d_h_one = dot_trans(d_qkv, regathered[2])
    d_x_ln, d_gain_one, d_bias_one = norm1_back(d_h_one)
    input_grad = (d_middle + d_x_ln)[None]
    grad_gains = jnp.stack([d_gain_one, d_gain_two], axis=1)
    grad_biases = jnp.stack([d_bias_one, d_bias_two], axis=1)
    grad_feat = jnp.concatenate([grad_map_q, grad_map_k], axis=-1).reshape(model_width, feat_dim)
    summed = (
        lax.psum_scatter(grad_gains, ("seq", "stream"), scatter_dimension=0, tiled=True),
        lax.psum_scatter(grad_biases, ("seq", "stream"), scatter_dimension=0, tiled=True),
        lax.psum_scatter(grad_qkv, ("seq", "stream"), scatter_dimension=0, tiled=True),
        lax.psum_scatter(grad_feat, ("seq", "stream"), scatter_dimension=0, tiled=True),
        lax.psum_scatter(grad_out, ("seq", "stream"), scatter_dimension=0, tiled=True),
        lax.psum_scatter(grad_fc, ("seq", "stream"), scatter_dimension=0, tiled=True),
        lax.psum_scatter(grad_proj, ("seq", "stream"), scatter_dimension=0, tiled=True),
    )
    return (
        result.astype(bf16)[None],
        input_grad,
        summed[0],
        summed[1],
        summed[2],
        summed[3],
        summed[4],
        summed[5],
        summed[6],
        branch_rms,
    )


def solution(mesh):
    placed = (
        P("stream", "seq", None),
        P("stream", "seq"),
        P(("seq", "stream"), None),
        P(("seq", "stream"), None),
        P(("seq", "stream"), None),
        P(("seq", "stream"), None),
        P(("seq", "stream"), None),
        P(("seq", "stream"), None),
        P(("seq", "stream"), None),
        P("stream", "seq", None),
    )
    return jax.shard_map(
        shards,
        mesh=mesh,
        in_specs=placed,
        out_specs=(
            P("stream", "seq", None),
            P("stream", "seq", None),
            P(("seq", "stream"), None),
            P(("seq", "stream"), None),
            P(("seq", "stream"), None),
            P(("seq", "stream"), None),
            P(("seq", "stream"), None),
            P(("seq", "stream"), None),
            P(("seq", "stream"), None),
            P("stream", None),
        ),
        check_vma=False,
    )
```

profile of v0, /device:TPU:9, one launch (start us, length us, event | category | flops | bytes accessed | tf_op | source)
XLA Modules:
  0.0 1406.8 jit_solution(17598636936767226499)
XLA Ops:
  9.7 59.1 %all-gather.4 = bf16[32,24,2]{1,2,0:T(2,128)(2,1)S(1)} all-gather(bf16[1,24,2]{1,2,0:T(2,128)(2,1)S(1)} %bitcast.379), channel_id=1, replica_groups=mesh['seq'=8,'stream'=4] {'seq','stream'}, dimensions={0}, use_global_device_ids=true | all-gather | bytes 3168 | tf_op jit(solution)/shard_map/all_gather | solution.py:106
  69.2 68.0 %all-gather.5 = bf16[32,24,2]{1,2,0:T(2,128)(2,1)S(1)} all-gather(bf16[1,24,2]{1,2,0:T(2,128)(2,1)S(1)} %bitcast.380), channel_id=1, replica_groups=mesh['seq'=8,'stream'=4] {'seq','stream'}, dimensions={0}, use_global_device_ids=true | all-gather | bytes 3168 | tf_op jit(solution)/shard_map/all_gather | solution.py:107
  139.7 65.0 %all_gather.61 = bf16[768,128]{1,0:T(8,128)(2,1)S(1)} all-gather(bf16[24,128]{1,0:T(8,128)(2,1)S(1)} %copy-done.73), channel_id=1, replica_groups=mesh['seq'=8,'stream'=4] {'seq','stream'}, dimensions={0}, use_global_device_ids=true | all-gather | bytes 202752 | tf_op jit(solution)/shard_map/all_gather | solution.py:109
  206.9 6.4 convolution_convert_fusion
  219.6 5.7 fusion.134
  226.8 5.2 concatenate.34
  232.1 5.2 copy.169
  246.6 5.9 reshape.364
  252.5 6.5 copy.172
  259.0 5.4 convert_reduce_fusion.1
  265.5 6.6 fusion.18
  277.5 17.7 %all-reduce = bf16[8]{0:T(256)(128)(2,1)} all-reduce(bf16[8]{0:T(256)(128)(2,1)S(1)} %dynamic-update-slice), channel_id=1, replica_groups=mesh['seq'=8,'stream'=4] {'seq'}, use_global_device_ids=true, to_apply=%add | all-reduce | flops 8 | bytes 32
  306.4 5.0 fusion.124
  313.8 9.0 all-gather.6
  326.9 5.2 concatenate.31
  332.1 5.0 copy.165
  341.3 5.2 concatenate.32
  346.5 5.0 copy.166
  351.5 6.5 copy.222
  370.8 6.1 broadcast.202.clone
  376.9 82.7 %while.67 = (s32[]{:T(128)}, f32[12,128,64]{2,1,0:T(8,128)S(1)}, f32[12,128]{1,0:T(8,128)S(1)}, f32[16,12,128,64]{3,2,1,0:T(8,128)}, f32[16,12,128]{2,1,0:T(8,12...) while((s32[]{:T(128)}, f32[12,128,64]{2,1,0:T(8,128)S(1)}, ...), condition=%wide.region_17.18_spmd, body=%wide.region_16.17_spmd.sunk | while | flops 199682 | bytes 3967613 | solution.py:180
  459.7 7.0 fusion.96
  466.8 15.5 %fusion.146 = f32[16,12,64,64]{2,3,1,0:T(8,128)} fusion(bf16[16,12,64,128]{3,2,1,0:T(8,128)(2,1)S(1)} %copy-done.4, f32[16,12,128,64]{3,2,1,0:T(8,128)} %get-tuple-element.388), kind=kOutput, calls=%fused_computation.215 | convolution fusion | flops 1207959552 | bytes 12582912 | tf_op jit(solution)/shard_map/nhcf,nhfd->nhcd/dot_general | solution.py:184
  482.3 6.8 fusion.15
  493.2 5.6 convert_element_type.198
  505.8 11.1 fusion.114
  516.9 15.9 %fusion.10 = bf16[1024,3072]{1,0:T(8,128)(2,1)S(1)} fusion(f32[1024,3072]{1,0:T(8,128)} %fusion.114, bf16[3072,768]{1,0:T(8,128)(2,1)} %all-gather.21.cloned.1.call-done, bf16[1,1024,768]{2,1,0:T(8,128)(2,1)} %param.27), kind=kOutput, calls=%fused_computation.28 | convolution fusion | flops 4894752768 | bytes 25165824 | tf_op jit(solution)/shard_map/dot_general | solution.py:86
  532.8 7.3 fusion.144
  543.7 13.5 multiply_reduce_fusion.1
  560.7 6.2 multiply_reduce_fusion.3
  573.7 5.7 reshape_reshape.12
  579.4 6.4 fusion.14
  586.6 5.7 fusion.21
  592.3 5.1 multiply_convert_fusion.1
  597.5 5.9 fusion.147
  603.4 15.8 %fusion.12 = f32[16,64,12,128]{3,1,2,0:T(8,128)} fusion(f32[16,12,64,128]{3,2,1,0:T(8,128)} %fusion.147, f32[16,12,128]{2,1,0:T(8,128)S(1)} %copy-done.52, f32[16,64,12]{1,2,0:T(8,128)S(1)} %copy-done.50, f32[16,64]{1,0:T(8,128)S(1)} %get-tuple-element.616, bf16[16,12,64,64]{2,3,1,0:T(8,128)(2,1)} %copy-done.6, f32[16,12,128,64]{3,2,1,0:T(8,128)S(1)} %bitcast.350), kind=kOutput, calls=%fused_computation.32 | convolution fusion | flops 1214251008 | bytes 20598784 | tf_op jit(solution)/shard_map/nhfd,nhcd->nhcf/dot_general | solution.py:248
  622.6 6.7 fusion.120
  629.3 6.3 copy.257
  638.9 6.1 copy.258
  649.6 5.9 fusion.20
  656.3 24.4 %all-gather.7 = bf16[8,12,128]{2,1,0:T(8,128)(2,1)S(1)} all-gather(bf16[1,12,128]{2,1,0:T(8,128)(2,1)S(1)} %copy.287), channel_id=5, replica_groups=mesh['seq'=8,'stream'=4] {'seq'}, dimensions={0}, use_global_device_ids=true | all-gather | bytes 27648 | tf_op jit(solution)/shard_map/all_gather | solution.py:42
  680.7 10.0 fusion.16
  691.6 6.5 add_convert_fusion.2
  704.0 5.6 fusion.148
  715.0 17.0 %while.68 = (s32[]{:T(128)}, f32[12,128,64]{2,1,0:T(8,128)S(1)}, f32[12,128]{1,0:T(8,128)S(1)}, s32[]{:T(128)}, bf16[8]{0:T(256)(128)(2,1)S(1)}, /*index=5*/bf16...) while((s32[]{:T(128)}, f32[12,128,64]{2,1,0:T(8,128)S(1)}, ...), condition=%wide.region_28.29_spmd, body=%wide.region_27.28_spmd.sunk | while | flops 299527 | bytes 1785017 | solution.py:59
  732.0 6.2 broadcast.202
  738.3 82.5 %while.69 = (s32[]{:T(128)}, f32[12,128,64]{2,1,0:T(8,128)S(1)}, f32[12,128]{1,0:T(8,128)S(1)}, f32[16,12,128,64]{3,2,1,0:T(8,128)}, f32[16,12,128]{2,1,0:T(8,12...) while((s32[]{:T(128)}, f32[12,128,64]{2,1,0:T(8,128)S(1)}, ...), condition=%wide.region_30.31_spmd, body=%wide.region_29.30_spmd.sunk | while | flops 199683 | bytes 3967125 | solution.py:238
  820.8 16.4 %add_bitcast_fusion = f32[16,64,12,128]{3,1,2,0:T(8,128)S(1)} fusion(f32[16,12,64,128]{3,2,1,0:T(8,128)} %fusion.148, f32[16,12,128]{2,1,0:T(8,128)S(1)} %get-tuple-element.393, f32[16,64]{1,0:T(8,128)S(1)} %copy-done.71, bf16[16,12,64,64]{2,3,1,0:T(8,128)(2,1)} %copy.222, f32[16,12,128,64]{3,2,1,0:T(8,128)} %get-tuple-element.392), kind=kOutput, calls=%fused_computation.44 | convolution fusion | flops 1212678144 | bytes 20549632 | tf_op jit(solution)/shard_map/nhfd,nhsd->nhsf/dot_general | solution.py:253
  838.0 6.7 fusion.121
  844.7 6.3 copy.259
  854.3 6.3 copy.260
  864.2 12.4 fusion.35
  876.6 5.3 copy.205
  881.8 5.4 reshape_reshape.13
  887.3 5.6 add_convert_fusion.1
  896.9 8.9 fusion.57
  906.4 10.8 fusion.113
  918.6 12.3 fusion.59
  933.2 14.3 %psum.7 = f32[3]{0:T(128)S(1)} all-reduce(f32[3]{0:T(128)S(1)} %pad_maximum_fusion.7), channel_id=1, replica_groups=mesh['seq'=8,'stream'=4] {'seq'}, use_global_device_ids=true, to_apply=%region_49.50 | all-reduce | flops 3 | bytes 24 | tf_op jit(solution)/shard_map/psum | solution.py:202
  949.6 9.0 fusion.145
  973.8 39.1 %all-reduce.4 = (f32[768,2]{0,1:T(2,128)S(1)}, f32[768,2]{0,1:T(2,128)S(1)}) all-reduce(f32[768,2]{0,1:T(2,128)S(1)} %pad_maximum_fusion.4, f32[768,2]{0,1:T(2,128)S(1)} %pad_maximum_fusion.5), channel_id=6, replica_groups=mesh['seq'=8,'stream'=4] {'seq','stream'}, use_global_device_ids=true, to_apply=%region_37.38.clone | all-reduce | flops 3072 | bytes 24576
  1013.6 103.3 %reduce-scatter.10.cloned.1.call-done = f32[24,2304]{1,0:T(8,128)} async-done(((f32[768,2304]{1,0:T(8,128)}), f32[24,2304]{1,0:T(8,128)}) %reduce-scatter.10.cloned.1.call-update) | async-done | bytes 221200 | tf_op jit(solution)/shard_map/reduce_scatter | solution.py:290
  1116.9 141.5 %reduce-scatter.14.cloned.1.call-done = f32[24,3072]{1,0:T(8,128)} async-done(((f32[768,3072]{1,0:T(8,128)}), f32[24,3072]{1,0:T(8,128)}) %reduce-scatter.14.cloned.1.call-update) | async-done | bytes 294928 | tf_op jit(solution)/shard_map/reduce_scatter | solution.py:293
  1258.4 141.7 %reduce-scatter.16.cloned.1.call-done = f32[96,768]{1,0:T(8,128)} async-done(((f32[3072,768]{1,0:T(8,128)}), f32[96,768]{1,0:T(8,128)}) %reduce-scatter.16.cloned.1.call-update) | async-done | bytes 294928 | tf_op jit(solution)/shard_map/reduce_scatter | solution.py:294
  (595 shorter events, 328.1 us)
Async XLA Ops:
  7.2 62.0 %copy-start.84 = (bf16[24,2]{0,1:T(2,128)(2,1)S(1)}, bf16[24,2]{0,1:T(2,128)(2,1)}, u32[]{:S(2)}) copy-start(bf16[24,2]{0,1:T(2,128)(2,1)} %param.21) | copy-start | bytes 292
  7.2 130.8 %copy-start.78 = (s32[1,1024]{1,0:T(1,128)S(1)}, s32[1,1024]{1,0:T(1,128)}, u32[]{:S(2)}) copy-start(s32[1,1024]{1,0:T(1,128)} %param.19) | copy-start | bytes 12292
  7.2 132.5 %copy-start.73 = (bf16[24,128]{1,0:T(8,128)(2,1)S(1)}, bf16[24,128]{1,0:T(8,128)(2,1)}, u32[]{:S(2)}) copy-start(bf16[24,128]{1,0:T(8,128)(2,1)} %param.23) | copy-start | bytes 18436
  7.2 199.7 %all-gather.15.cloned.1.call-start = ((), (), s32[]{:S(2)}) async-start(), calls=%async_computation.5 | async-start | bytes 3649536 | tf_op jit(solution)/shard_map/all_gather | solution.py:108
  8.0 360.0 %all-gather.23.cloned.1.call-start = ((), (), s32[]{:S(2)}) async-start(), calls=%async_computation.13 | async-start | bytes 1769472 | tf_op jit(solution)/shard_map/all_gather | solution.py:18
  9.7 203.6 %copy-start.8 = (bf16[1,1024,768]{1,2,0:T(8,128)(2,1)}, bf16[1,1024,768]{1,2,0:T(8,128)(2,1)S(1)}, u32[]{:S(2)}) copy-start(bf16[1,1024,768]{1,2,0:T(8,128)(2,1)S(1)} %copy.158) | copy-start | bytes 4718596
  139.1 65.6 %copy-start.79 = (f32[16]{0:T(128)}, f32[16]{0:T(128)S(1)}, u32[]{:S(2)}) copy-start(f32[16]{0:T(128)S(1)} %compare_convert_fusion.2) | copy-start | bytes 196
  139.7 125.8 %copy-start.82 = (f32[16]{0:T(128)}, f32[16]{0:T(128)S(1)}, u32[]{:S(2)}) copy-start(f32[16]{0:T(128)S(1)} %rev.7) | copy-start | bytes 196
  204.8 101.7 %copy-start.30 = (bf16[768,128]{1,0:T(8,128)(2,1)}, bf16[768,128]{1,0:T(8,128)(2,1)S(1)}, u32[]{:S(2)}) copy-start(bf16[768,128]{1,0:T(8,128)(2,1)S(1)} %all_gather.61) | copy-start | bytes 589828
  204.8 8.5 copy-start.61
  204.9 8.5 copy-start.75
  204.9 300.9 %copy-start.53 = (f32[768]{0:T(1024)}, f32[768]{0:T(1024)S(1)}, u32[]{:S(2)}) copy-start(f32[768]{0:T(1024)S(1)} %get-tuple-element.533) | copy-start | bytes 9220
  205.1 8.2 copy-start.59
  206.2 7.1 copy-start.65
  206.9 57.5 %copy-start.63 = (bf16[16,64]{1,0:T(8,128)(2,1)}, bf16[16,64]{1,0:T(8,128)(2,1)S(1)}, u32[]{:S(2)}) copy-start(bf16[16,64]{1,0:T(8,128)(2,1)S(1)} %get-tuple-element.603) | copy-start | bytes 6148
  219.5 7.3 copy-start.10
  219.5 92.5 %copy-start.42 = (f32[1024,12]{0,1:T(8,128)}, f32[1024,12]{0,1:T(8,128)S(1)}, u32[]{:S(2)}) copy-start(f32[1024,12]{0,1:T(8,128)S(1)} %get-tuple-element.625) | copy-start | bytes 147460
  225.2 86.2 %copy-start.44 = (f32[1024,12]{0,1:T(8,128)}, f32[1024,12]{0,1:T(8,128)S(1)}, u32[]{:S(2)}) copy-start(f32[1024,12]{0,1:T(8,128)S(1)} %get-tuple-element.623) | copy-start | bytes 147460
  264.4 98.3 %copy-start = (bf16[16,12,64,128]{3,2,1,0:T(8,128)(2,1)}, bf16[16,12,64,128]{3,2,1,0:T(8,128)(2,1)S(1)}, u32[]{:S(2)}) copy-start(bf16[16,12,64,128]{3,2,1,0:T(8,128)(2,1)S(1)} %get-tuple-element.602) | copy-start | bytes 9437188
  265.5 6.6 copy-start.18
  265.5 10.0 copy-start.88
  272.9 225.9 %all-gather.17.cloned.1.call-start = ((), (), s32[]{:S(2)}) async-start(), calls=%async_computation.6 | async-start | bytes 1216512 | tf_op jit(solution)/shard_map/all_gather | solution.py:110
  273.6 232.1 %all-gather.19.cloned.1.call-start = ((), (), s32[]{:S(2)}) async-start(), calls=%async_computation.7 | async-start | bytes 4866048 | tf_op jit(solution)/shard_map/all_gather | solution.py:111
  274.2 242.7 %all-gather.21.cloned.1.call-start = ((), (), s32[]{:S(2)}) async-start(), calls=%async_computation.8 | async-start | bytes 4866048 | tf_op jit(solution)/shard_map/all_gather | solution.py:112
  274.8 440.1 %all-gather.25.cloned.1.call-start = ((), (), s32[]{:S(2)}) async-start(), calls=%async_computation.14 | async-start | bytes 1769472 | tf_op jit(solution)/shard_map/all_gather | solution.py:42
  306.4 20.5 %copy-start.46 = (f32[1024,12]{0,1:T(8,128)}, f32[1024,12]{0,1:T(8,128)S(1)}, u32[]{:S(2)}) copy-start(f32[1024,12]{0,1:T(8,128)S(1)} %get-tuple-element.621) | copy-start | bytes 147460
  358.0 6.4 copy-start.34
  370.8 6.1 copy-start.80
  459.7 7.0 copy-start.51
  459.7 7.0 copy-start.4
  466.7 15.5 %copy-start.26 = (bf16[16,12,64,64]{2,3,1,0:T(8,128)(2,1)S(1)}, bf16[16,12,64,64]{2,3,1,0:T(8,128)(2,1)}, u32[]{:S(2)}) copy-start(bf16[16,12,64,64]{2,3,1,0:T(8,128)(2,1)} %get-tuple-element.628) | copy-start | bytes 4718596
  466.7 15.5 %copy-start.29 = (bf16[16,64,12,64]{1,3,2,0:T(8,128)(2,1)S(1)}, bf16[16,64,12,64]{1,3,2,0:T(8,128)(2,1)}, u32[]{:S(2)}) copy-start(bf16[16,64,12,64]{1,3,2,0:T(8,128)(2,1)} %copy.172) | copy-start | bytes 4718596
  516.9 15.9 %copy-start.33 = (bf16[768,3072]{1,0:T(8,128)(2,1)S(1)}, bf16[768,3072]{1,0:T(8,128)(2,1)}, u32[]{:S(2)}) copy-start(bf16[768,3072]{1,0:T(8,128)(2,1)} %all-gather.19.cloned.1.call-done) | copy-start | bytes 14155780
  532.8 7.4 copy-start.89
  560.7 6.2 copy-start.15
  560.7 6.2 copy-start.21
  585.8 6.5 copy-start.6
  586.6 10.8 copy-start.1
  592.3 11.1 slice-start
  592.3 11.1 slice-start.1
  597.4 5.9 slice-start.2
  597.5 5.9 copy-start.50
  597.5 5.9 copy-start.52
  629.3 6.3 copy-start.16
  629.3 6.3 copy-start.58
  638.9 6.2 copy-start.57
  648.9 7.2 copy-start.74
  680.7 10.9 copy-start.47
  680.7 10.9 copy-start.49
  691.5 6.6 copy-start.31
  691.5 322.1 %reduce-scatter.12.cloned.1.call-start = ((), (), s32[]{:S(2)}) async-start(), calls=%async_computation.10 | async-start | bytes 2433024 | tf_op jit(solution)/shard_map/reduce_scatter | solution.py:292
  714.0 299.6 %reduce-scatter.18.cloned.1.call-start = ((), (), s32[]{:S(2)}) async-start(), calls=%async_computation.15 | async-start | bytes 405504
  732.0 6.2 copy-start.81
  738.2 82.5 %copy-start.71 = (f32[16,64]{1,0:T(8,128)S(1)}, f32[16,64]{1,0:T(8,128)}, u32[]{:S(2)}) copy-start(f32[16,64]{1,0:T(8,128)} %get-tuple-element.604) | copy-start | bytes 12292
  844.7 6.3 copy-start.13
  844.7 6.3 copy-start.56
  854.3 6.3 copy-start.11
  854.3 6.3 copy-start.55
  896.8 220.1 %reduce-scatter.10.cloned.1.call-start = ((), (), s32[]{:S(2)}) async-start(), calls=%async_computation.9 | async-start | bytes 7299072 | tf_op jit(solution)/shard_map/reduce_scatter | solution.py:290
  905.8 352.6 %reduce-scatter.14.cloned.1.call-start = ((), (), s32[]{:S(2)}) async-start(), calls=%async_computation.11 | async-start | bytes 9732096 | tf_op jit(solution)/shard_map/reduce_scatter | solution.py:293
  917.2 482.8 %reduce-scatter.16.cloned.1.call-start = ((), (), s32[]{:S(2)}) async-start(), calls=%async_computation.12 | async-start | bytes 9732096 | tf_op jit(solution)/shard_map/reduce_scatter | solution.py:294
  931.0 16.5 %copy-start.77 = (f32[768]{0:T(1024)S(1)}, f32[768]{0:T(1024)}, u32[]{:S(2)}) copy-start(f32[768]{0:T(1024)} %get-tuple-element.631) | copy-start | bytes 9220
  931.0 16.5 %copy-start.72 = (f32[768]{0:T(1024)S(1)}, f32[768]{0:T(1024)}, u32[]{:S(2)}) copy-start(f32[768]{0:T(1024)} %get-tuple-element.526) | copy-start | bytes 9220
  931.0 16.5 %copy-start.32 = (bf16[1,1024,768]{1,2,0:T(8,128)(2,1)S(1)}, bf16[1,1024,768]{1,2,0:T(8,128)(2,1)}, u32[]{:S(2)}) copy-start(bf16[1,1024,768]{1,2,0:T(8,128)(2,1)} %get-tuple-element.611) | copy-start | bytes 4718596
  (40 other events, 120.5 us)
Sparse Core Ops, SparseCore 0:
  10.8 60.9 all-gather.14
  273.0 29.0 all-gather.22
  305.0 53.0 all-gather.16
  360.7 63.3 all-gather.18
  426.8 61.8 all-gather.20
  691.6 23.2 all-gather.24
  720.8 97.3 reduce-scatter.11
  896.9 94.8 reduce-scatter.17
  998.1 118.7 reduce-scatter.9
  1123.2 135.1 reduce-scatter.13
  1264.9 135.1 reduce-scatter.15
where the time goes:
time: 1430 us; the launch traced here: 1410 us
  waiting for transfers between devices  390 us (27%)
  blocking collectives  297 us (21%)
  local copies, waits for them, and re-layouts  283 us (20%)
  matrix products  258 us (18%)
  other arithmetic  158 us (11%)
  between operations  15.1 us (1%)
    reduce_scatter x1, waiting for transfers between devices, shards(): lax.psum_scatter(grad_proj, ('seq', 'stream'), scatter_dimension=0, tiled...  142 us
    reduce_scatter x1, waiting for transfers between devices, shards(): lax.psum_scatter(grad_fc, ('seq', 'stream'), scatter_dimension=0, tiled=T...  141 us
    reduce_scatter x1, waiting for transfers between devices, shards(): lax.psum_scatter(grad_qkv, ('seq', 'stream'), scatter_dimension=0, tiled=...  103 us
    all_gather x1, blocking collectives, shards(): lax.all_gather(norm_biases, ('seq', 'stream'), axis=0, tiled=True)  68 us
    all_gather x1, blocking collectives, shards(): lax.all_gather(w_feat, ('seq', 'stream'), axis=0, tiled=True)  65 us
    dynamic_slice x96, local copies, waits for them, and re-layouts, shards(): lax.scan(advance, (incoming[1], incoming[2]), (block_kv, block_z, keep_bl...  60.1 us
    all_gather x1, blocking collectives, shards(): lax.all_gather(norm_gains, ('seq', 'stream'), axis=0, tiled=True)  59.1 us
    unnamed x2, blocking collectives  56.8 us
  transfers between devices with their start and end apart: 11, of which 4 were waited for; matrix products, arithmetic and copies ran while one was open for 34% of the time, Pallas kernels for 0%

commit v1 on v0

v1 whole, which is shorter than its diff:
```python
import functools

import jax
import jax.numpy as jnp
from jax import lax
from jax.experimental import pallas as pl
from jax.experimental.pallas import tpu as pltpu
from jax.sharding import PartitionSpec as P

BT = 128
TM = 256
epsilon = 1e-05
f32 = jnp.float32
bf16 = jnp.bfloat16
GC = 0.7978845608028654
GA = 0.044715


def mm(a, b):
    return jnp.dot(a, b, preferred_element_type=f32)


def mm_t(a, b):
    return lax.dot_general(a, b, (((1,), (1,)), ((), ())), preferred_element_type=f32)


def mm_f(a, b):
    return lax.dot_general(a, b, (((0,), (0,)), ((), ())), preferred_element_type=f32)


def xor_send(arr, size, mask):
    return lax.ppermute(arr, "seq", [(i, i ^ mask) for i in range(size)])


def stream_rows(shard, depth):
    pieces = [shard] + [
        lax.ppermute(shard, "stream", [(i, (i + d) % depth) for i in range(depth)])
        for d in range(1, depth)
    ]
    ring = pieces[::-1]
    place = lax.axis_index("stream")
    rows = shard.shape[0]
    both = jnp.concatenate(ring + ring, axis=0)
    return lax.dynamic_slice_in_dim(both, (depth - 1 - place) * rows, depth * rows, 0)


def seq_blocks(block, size, flip):
    bits = [1 << b for b in range(1, size.bit_length() - 1)]
    if flip:
        bits = bits[::-1]
    found = {0: block}
    for bit in bits:
        for r in list(found):
            found[r ^ bit] = xor_send(found[r], size, bit)
    for r in list(found):
        found[r ^ 1] = xor_send(found[r], size, 1)
    return [found[r] for r in range(size)]


def to_owner(grad, size, depth, flip):
    nbits = size.bit_length() - 1
    place = lax.axis_index("seq")
    rest = list(range(nbits))[::-1]
    cols = grad.shape[1]
    cur = grad.reshape([2] * nbits + [grad.shape[0] // size, cols])
    order = [0] + (list(range(1, nbits))[::-1] if flip else list(range(1, nbits)))
    for bit in order:
        axis = rest.index(bit)
        own = (place >> bit) & 1
        send = lax.dynamic_index_in_dim(cur, 1 - own, axis, False)
        keep = lax.dynamic_index_in_dim(cur, own, axis, False)
        got = xor_send(send, size, 1 << bit)
        cur = (keep.astype(f32) + got.astype(f32)).astype(bf16)
        rest.pop(axis)
    level = lax.axis_index("stream")
    cur = cur.reshape(depth, cur.shape[0] // depth, cols)
    total = lax.dynamic_index_in_dim(cur, level, 0, False).astype(f32)
    for d in range(1, depth):
        piece = lax.dynamic_index_in_dim(cur, (level + d) % depth, 0, False)
        total = total + lax.ppermute(
            piece, "stream", [(i, (i + d) % depth) for i in range(depth)]
        ).astype(f32)
    return total


def lanes(shape):
    return lax.broadcasted_iota(jnp.int32, shape, len(shape) - 1)


def block_ones(width, part):
    r = lax.broadcasted_iota(jnp.int32, (width, width), 0) // part
    c = lax.broadcasted_iota(jnp.int32, (width, width), 1) // part
    return jnp.where(r == c, 1.0, 0.0).astype(bf16)


def fetch_start(blocks, dest, me, sems, col=0, width=None):
    rows = dest.shape[0] // len(blocks)
    copies = []
    for r, ref in enumerate(blocks):
        off = pl.multiple_of((me ^ r) * rows, 8)
        src = ref if width is None else ref.at[:, pl.ds(col, width)]
        copy = pltpu.make_async_copy(src, dest.at[pl.ds(off, rows), :], sems.at[r])
        copy.start()
        copies.append(copy)
    return copies


def pair_maps(feat_ref, dest, pairs, which):
    width = 128
    lane = lanes((width, width))
    row = lax.broadcasted_iota(jnp.int32, (width, width), 0)
    for p in range(pairs):
        both = feat_ref[pl.ds(p * width, width), :].astype(f32)
        half = width // 2
        other = pltpu.roll(both, half, 1)
        if which == 0:
            signed = jnp.where(lane < half, both, -other)
        else:
            signed = jnp.where(lane < half, other, -both)
        dest[p, :, pl.ds(0, width)] = jnp.where(row < half, signed, 0.0).astype(bf16)
        dest[p, :, pl.ds(width, width)] = jnp.where(row >= half, signed, 0.0).astype(bf16)


def features(logits, ones):
    parts = []
    for j in range(2):
        one = logits[:, j * 128 : (j + 1) * 128]
        low = lanes(one.shape) < 64
        top_a = jnp.max(jnp.where(low, one, -jnp.inf), axis=1, keepdims=True)
        top_b = jnp.max(jnp.where(low, -jnp.inf, one), axis=1, keepdims=True)
        parts.append(jnp.exp(one - jnp.where(low, top_a, top_b)))
    exps = jnp.concatenate(parts, axis=1)
    return (exps / mm(exps.astype(bf16), ones)).astype(bf16)


def augmented(two):
    low = lanes(two.shape) < 64
    one = jnp.ones_like(two)
    return jnp.where(low, two, one), jnp.where(low, one, two)


def pack_states(get, dest, pairs, zsum):
    shape = (128, 128)
    lane = lanes(shape)
    low = lane < 64
    zt = jnp.zeros(shape, f32)
    for p in range(pairs):
        a, b = get(2 * p), get(2 * p + 1)
        dest[p] = jnp.where(low, a, b).astype(bf16)
        if zsum:
            za = jnp.sum(jnp.where(low, 0.0, a), axis=1, keepdims=True)
            zb = jnp.sum(jnp.where(low, b, 0.0), axis=1, keepdims=True)
        else:
            za, zb = a, b
        zt = jnp.where(lane == 64 + 2 * p, za, zt)
        zt = jnp.where(lane == 2 * p + 1, zb, zt)
    dest[pairs] = zt.astype(bf16)


def unpack_states(coef_ref, blocks, put, pairs, split):
    shape = (128, 128)
    lane = lanes(shape)
    low = lane < 64

    def total(i):
        acc = jnp.zeros(shape, f32)
        for r in range(1, len(blocks)):
            acc = acc + coef_ref[r] * blocks[r][i].astype(f32)
        return acc

    zt = total(pairs)
    for p in range(pairs):
        two = total(p)
        za = jnp.sum(jnp.where(lane == 64 + 2 * p, zt, 0.0), axis=1, keepdims=True)
        zb = jnp.sum(jnp.where(lane == 2 * p + 1, zt, 0.0), axis=1, keepdims=True)
        if split:
            put(2 * p, jnp.where(low, two, jnp.where(lane == 64, za, 0.0)))
            put(2 * p + 1, jnp.where(low, jnp.where(lane == 0, zb, 0.0), two))
        else:
            put(2 * p, jnp.where(low, two, za))
            put(2 * p + 1, jnp.where(low, zb, two))


def normed(values, gain, bias):
    mean = jnp.mean(values, axis=1, keepdims=True)
    cent = values - mean
    rstd = lax.rsqrt(jnp.mean(cent * cent, axis=1, keepdims=True) + epsilon)
    hat = cent * rstd
    return hat * gain + bias, hat, rstd


def normed_back(grad, hat, rstd, gain):
    dhat = grad * gain
    return rstd * (
        dhat
        - jnp.mean(dhat, axis=1, keepdims=True)
        - hat * jnp.mean(dhat * hat, axis=1, keepdims=True)
    )


def keys_body(n_seq, pairs, me_ref, cend_ref, x_ref, cnt_ref, *refs):
    width = x_ref.shape[1]
    wa, wb = refs[:n_seq], refs[n_seq : 2 * n_seq]
    (h_ref, k_ref, v_ref, phi_ref, st_ref, gb_ref, w1, w2, maps, state, sems) = refs[2 * n_seq :]
    step = pl.program_id(0)

    @pl.when(step == 0)
    def _():
        me = me_ref[0]
        copies = fetch_start(wa, w1, me, sems.at[0])
        copies += fetch_start(wb, w2, me, sems.at[1])
        for c in copies:
            c.wait()
        gb_ref[...] = w1[:, pl.ds(width + 128, 128)].astype(f32).T[:8]
        pair_maps(w1.at[:, pl.ds(width, 128)], maps, pairs, 1)
        state[...] = jnp.zeros_like(state)

    gb = gb_ref[...]
    out, _, _ = normed(x_ref[...].astype(f32), gb[0:1], gb[2:3])
    h1 = out.astype(bf16)
    h_ref[...] = h1
    keys = mm(h1, w1[:, pl.ds(0, width)]).astype(bf16)
    vals = mm(h1, w2[...]).astype(bf16)
    k_ref[...] = keys
    v_ref[...] = vals
    ones = block_ones(256, 64)
    last = cend_ref[cend_ref.shape[0] - 1]
    used = jnp.where(cnt_ref[...] == last, 1.0, 0.0).astype(bf16)
    for p in range(pairs):
        two = slice(p * 128, (p + 1) * 128)
        phi = features(mm(keys[:, two], maps[p]), ones)
        phi_ref[:, pl.ds(p * 256, 256)] = phi
        va, vb = augmented(vals[:, two])
        state[2 * p] += mm_f(phi[:, :128], va * used)
        state[2 * p + 1] += mm_f(phi[:, 128:], vb * used)

    @pl.when(step == pl.num_programs(0) - 1)
    def _():
        pack_states(lambda h: state[h], st_ref, pairs, False)


def local_body(n_seq, pairs, me_ref, cend_ref, h_ref, phik_ref, v_ref, cnt_ref, row_ref, feat_ref, *refs):
    wq = refs[:n_seq]
    (q_ref, phiq_ref, num_ref, den_ref, srel_ref, w1, maps, state, sems) = refs[n_seq:]
    step = pl.program_id(0)
    width = h_ref.shape[1]

    @pl.when(step == 0)
    def _():
        for c in fetch_start(wq, w1, me_ref[0], sems, 0, width):
            c.wait()
        pair_maps(feat_ref, maps, pairs, 0)
        state[...] = jnp.zeros_like(state)

    queries = mm(h_ref[...], w1[...]).astype(bf16)
    q_ref[...] = queries
    ones = block_ones(256, 64)
    size = h_ref.shape[0]
    cnt = cnt_ref[...]
    first, last = cend_ref[step], cend_ref[step + 1]
    row_id = lax.broadcasted_iota(jnp.int32, (size, size), 0)
    mask = (row_id >= lanes((size, size))) & (cnt == row_ref[...])
    before = jnp.where(cnt == first, 1.0, 0.0)
    after = jnp.where(cnt == last, 1.0, 0.0).astype(bf16)
    keep = jnp.where(first == last, 1.0, 0.0)
    low = lanes((size, 128)) < 64
    for p in range(pairs):
        two = slice(p * 128, (p + 1) * 128)
        phi = features(mm(queries[:, two], maps[p]), ones)
        phiq_ref[:, pl.ds(p * 256, 256)] = phi
        res = []
        for j, val in enumerate(augmented(v_ref[:, two])):
            h = 2 * p + j
            pq = phi[:, j * 128 : (j + 1) * 128]
            pk = phik_ref[:, pl.ds(h * 128, 128)]
            scores = jnp.where(mask, mm_t(pq, pk), 0.0).astype(bf16)
            st = state[h]
            st_b = st.astype(bf16)
            srel_ref[0, h] = st_b
            res.append(mm(scores, val) + before * mm(pq, st_b))
            state[h] = keep * st + mm_f(pk, val * after)
        num_ref[:, two] = jnp.where(low, res[0], res[1])
        den_ref[:, two] = pltpu.roll(jnp.where(low, res[1], res[0]), 64, 1)


def middle_body(
    n_seq, pairs, me_ref, coef_ref, x_ref, dy_ref, num_ref, den_ref, phiq_ref, cnt_ref, gb_ref, *refs
):
    width = x_ref.shape[1]
    wo, wf, wp, sts = (refs[i * n_seq : (i + 1) * n_seq] for i in range(4))
    (
        y_ref, o_ref, h_ref, a_ref, df_ref, dat_ref, dr_ref, dd_ref, sin_ref, gst_ref, sum_ref,
        w_out, w_fc, w_proj, rden, state, stv, sems,
    ) = refs[4 * n_seq :]
    step = pl.program_id(0)
    chunk = 768
    size = x_ref.shape[0]

    @pl.when(step == 0)
    def _():
        me = me_ref[0]
        st_copies = []
        for r in range(1, n_seq):
            c = pltpu.make_async_copy(sts[r], stv.at[r], sems.at[3, r])
            c.start()
            st_copies.append(c)
        copies = fetch_start(wo, w_out, me, sems.at[0], width, width)
        copies += fetch_start(wf, w_fc, me, sems.at[1])
        copies += fetch_start(wp, w_proj, me, sems.at[2])
        for c in st_copies:
            c.wait()

        def put(h, value):
            sin_ref[h] = value.astype(bf16)

        unpack_states(coef_ref, [stv.at[r] for r in range(n_seq)], put, pairs, False)
        state[...] = jnp.zeros_like(state)
        sum_ref[...] = jnp.zeros_like(sum_ref)
        for c in copies:
            c.wait()

    gb = gb_ref[...]
    low = lanes((size, 128)) < 64
    start = jnp.where(cnt_ref[...] == 0.0, 1.0, 0.0)
    start_b = start.astype(bf16)
    for p in range(pairs):
        two = pl.ds(p * 128, 128)
        ra = mm(phiq_ref[:, pl.ds(p * 256, 128)], sin_ref[2 * p])
        rb = mm(phiq_ref[:, pl.ds(p * 256 + 128, 128)], sin_ref[2 * p + 1])
        num = num_ref[:, two] + start * jnp.where(low, ra, rb)
        den = den_ref[:, two] + start * pltpu.roll(jnp.where(low, rb, ra), 64, 1)
        inv = 1.0 / den
        rden[:, two] = inv
        o_ref[:, two] = (num * inv).astype(bf16)
    x = x_ref[...].astype(f32)
    attn = mm(o_ref[...], w_out[...])
    mid = x + attn
    out, hat, rstd = normed(mid, gb[1:2], gb[3:4])
    h2 = out.astype(bf16)
    h_ref[...] = h2
    dy_b = dy_ref[...]
    branch = jnp.zeros((size, width), f32)
    dh2 = jnp.zeros((size, width), f32)
    for c in range(w_fc.shape[1] // chunk):
        cols = pl.ds(c * chunk, chunk)
        fc = mm(h2, w_fc[:, cols])
        square = fc * fc
        tan = jnp.tanh(fc * (GC + GC * GA * square))
        half = 0.5 + 0.5 * tan
        act = (fc * half).astype(bf16)
        a_ref[:, cols] = act
        branch = branch + mm(act, w_proj[cols, :])
        slope = half + fc * (1.0 - half) * half * (2.0 * GC + 6.0 * GC * GA * square)
        dfc = (mm_t(dy_b, w_proj[cols, :]) * slope).astype(bf16)
        df_ref[:, cols] = dfc
        dh2 = dh2 + mm_t(dfc, w_fc[:, cols])
    y = mid + branch
    y_ref[...] = y.astype(bf16)
    sum_ref[0:1] += jnp.sum(attn * attn, axis=0, keepdims=True)
    sum_ref[1:2] += jnp.sum(branch * branch, axis=0, keepdims=True)
    sum_ref[2:3] += jnp.sum(y * y, axis=0, keepdims=True)
    sum_ref[3:4] += jnp.sum(dh2 * hat, axis=0, keepdims=True)
    sum_ref[4:5] += jnp.sum(dh2, axis=0, keepdims=True)
    dr = dy_b.astype(f32) + normed_back(dh2, hat, rstd, gb[1:2])
    dr_ref[...] = dr
    dat = dr.astype(bf16)
    dat_ref[...] = dat
    d_o = mm_t(dat, w_out[...])
    ones = block_ones(256, 64)
    lane = lanes((size, 128))
    for q in range(pairs // 2):
        four = pl.ds(q * 256, 256)
        inv = rden[:, four]
        d_q = d_o[:, q * 256 : (q + 1) * 256]
        prod = d_q * o_ref[:, four].astype(f32)
        hi = prod.astype(bf16)
        lo = (prod - hi.astype(f32)).astype(bf16)
        dden = -(mm(hi, ones) + mm(lo, ones)) * inv
        dnum = (d_q * inv).astype(bf16)
        for i in range(2):
            p = 2 * q + i
            sub = slice(i * 128, (i + 1) * 128)
            dd = pltpu.roll(dden[:, sub], 64, 1)
            dhi = dd.astype(bf16)
            dlo = (dd - dhi.astype(f32)).astype(bf16)
            near = lane & 63
            aux = jnp.where(near == 0, dhi.astype(f32), jnp.where(near == 1, dlo.astype(f32), 0.0)).astype(bf16)
            dn = dnum[:, sub]
            for j, both in enumerate((jnp.where(low, dn, aux), jnp.where(low, aux, dn))):
                h = 2 * p + j
                dd_ref[:, pl.ds(h * 128, 128)] = both
                state[h] += mm_f(phiq_ref[:, pl.ds(h * 128, 128)], both * start_b)

    @pl.when(step == pl.num_programs(0) - 1)
    def _():
        pack_states(lambda h: state[h], gst_ref, pairs, True)


def back_body(
    n_seq, pairs, coef_ref, cend_ref, q_ref, k_ref, v_ref, phiq_ref, phik_ref, dd_ref, srel_ref, sin_ref,
    cnt_ref, row_ref, feat_ref, *refs
):
    sts = refs[:n_seq]
    (dqkv_ref, gfeat_ref, mapq, mapk, state, gq, gk, stv, sems) = refs[n_seq:]
    step = pl.program_id(0)
    nblk = pl.num_programs(0)
    here = nblk - 1 - step

    @pl.when(step == 0)
    def _():
        copies = []
        for r in range(1, n_seq):
            c = pltpu.make_async_copy(sts[r], stv.at[r], sems.at[r])
            c.start()
            copies.append(c)
        pair_maps(feat_ref, mapq, pairs, 0)
        pair_maps(feat_ref, mapk, pairs, 1)
        gq[...] = jnp.zeros_like(gq)
        gk[...] = jnp.zeros_like(gk)
        for c in copies:
            c.wait()

        def put(h, value):
            state[h] = value

        unpack_states(coef_ref, [stv.at[r] for r in range(n_seq)], put, pairs, True)

    size = q_ref.shape[0]
    width = q_ref.shape[1]
    cnt = cnt_ref[...]
    first, last = cend_ref[here], cend_ref[here + 1]
    row_id = lax.broadcasted_iota(jnp.int32, (size, size), 0)
    col_id = lanes((size, size))
    same = cnt == row_ref[...]
    mask = (row_id >= col_id) & same
    mask_t = (col_id >= row_id) & same
    before = jnp.where(cnt == first, 1.0, 0.0).astype(bf16)
    after = jnp.where(cnt == last, 1.0, 0.0).astype(bf16)
    keep = jnp.where(first == last, 1.0, 0.0)
    opened = jnp.where(first == 0.0, 1.0, 0.0)
    ones = block_ones(256, 64)
    low = lanes((size, 128)) < 64
    for p in range(pairs):
        two = pl.ds(p * 128, 128)
        dphi_q, dphi_k, dvs = [], [], []
        for j, val in enumerate(augmented(v_ref[:, two])):
            h = 2 * p + j
            own = pl.ds(h * 128, 128)
            pq, pk, dd = phiq_ref[:, own], phik_ref[:, own], dd_ref[:, own]
            scores_t = jnp.where(mask_t, mm_t(pk, pq), 0.0).astype(bf16)
            dsc = jnp.where(mask, mm_t(dd, val), 0.0).astype(bf16)
            dsc_t = jnp.where(mask_t, mm_t(val, dd), 0.0).astype(bf16)
            st = (srel_ref[0, h].astype(f32) + opened * sin_ref[h].astype(f32)).astype(bf16)
            dst = state[h]
            dst_b = dst.astype(bf16)
            ddw = dd * before
            dphi_q.append(mm(dsc, pk) + mm_t(ddw, st))
            dphi_k.append(mm(dsc_t, pq) + mm_t(val * after, dst_b))
            dvs.append(mm(scores_t, dd) + mm(pk * after, dst_b))
            state[h] = keep * dst + mm_f(pq, ddw)
        dqkv_ref[:, pl.ds(2 * width + p * 128, 128)] = jnp.where(low, dvs[0], dvs[1]).astype(bf16)
        for phi_ref, dphi, rows_ref, maps, acc, base in (
            (phiq_ref, dphi_q, q_ref, mapq, gq, 0),
            (phik_ref, dphi_k, k_ref, mapk, gk, width),
        ):
            phi = phi_ref[:, pl.ds(p * 256, 256)].astype(f32)
            dphi = jnp.concatenate(dphi, axis=1)
            total = mm((phi * dphi).astype(bf16), ones)
            dlog = (phi * (dphi - total)).astype(bf16)
            dqkv_ref[:, pl.ds(base + p * 128, 128)] = mm_t(dlog, maps[p]).astype(bf16)
            acc[p] += mm_f(rows_ref[:, two], dlog)

    @pl.when(step == nblk - 1)
    def _():
        lane = lanes((128, 128))
        row = lax.broadcasted_iota(jnp.int32, (128, 128), 0)
        for p in range(pairs):
            outs = []
            for acc in (gq, gk):
                one = jnp.where(row < 64, acc[p, :, :128], acc[p, :, 128:])
                outs.append(one - pltpu.roll(one, 64, 1))
            gfeat_ref[pl.ds(p * 128, 128), :] = jnp.where(lane < 64, outs[0], -outs[1]).astype(bf16)


def enter_body(n_seq, me_ref, x_ref, dr_ref, dqkv_ref, gb_ref, *refs):
    width = x_ref.shape[1]
    wq, wk, wv = (refs[i * n_seq : (i + 1) * n_seq] for i in range(3))
    (dx_ref, sum_ref, w1, w2, w3, sems) = refs[3 * n_seq :]

    @pl.when(pl.program_id(0) == 0)
    def _():
        me = me_ref[0]
        copies = fetch_start(wq, w1, me, sems.at[0], 0, width)
        copies += fetch_start(wk, w2, me, sems.at[1], 0, width)
        copies += fetch_start(wv, w3, me, sems.at[2])
        sum_ref[...] = jnp.zeros_like(sum_ref)
        for c in copies:
            c.wait()

    gb = gb_ref[...]
    _, hat, rstd = normed(x_ref[...].astype(f32), gb[0:1], gb[2:3])
    dh = (
        mm_t(dqkv_ref[:, pl.ds(0, width)], w1[...])
        + mm_t(dqkv_ref[:, pl.ds(width, width)], w2[...])
        + mm_t(dqkv_ref[:, pl.ds(2 * width, width)], w3[...])
    )
    dx_ref[...] = dr_ref[...] + normed_back(dh, hat, rstd, gb[0:1])
    sum_ref[0:1] += jnp.sum(dh * hat, axis=0, keepdims=True)
    sum_ref[1:2] += jnp.sum(dh, axis=0, keepdims=True)


def whole(*_):
    return pl.BlockSpec(memory_space=pl.ANY)


def smem():
    return pl.BlockSpec(memory_space=pltpu.SMEM)


def rows_spec(size, cols, back=None):
    if back is None:
        return pl.BlockSpec((size, cols), lambda i: (i, 0))
    return pl.BlockSpec((size, cols), lambda i: (back - 1 - i, 0))


def full_spec(shape):
    zeros = (0,) * len(shape)
    return pl.BlockSpec(shape, lambda i: zeros)


def sds(shape, kind):
    return jax.ShapeDtypeStruct(shape, kind)


def cparams():
    return pltpu.CompilerParams(
        dimension_semantics=("arbitrary",), vmem_limit_bytes=58 * 1024 * 1024
    )


def dma(*shape):
    return pltpu.SemaphoreType.DMA(shape)


def shards(n_seq, depth, inputs, resets, norm_gains, norm_biases, w_qkv, w_feat, w_out, w_fc, w_proj, cotangent):
    tokens, width = inputs.shape[1], inputs.shape[2]
    hidden = w_fc.shape[1]
    head_dim = w_feat.shape[1] // 2
    heads = width // head_dim
    pairs = heads // 2
    rows = w_qkv.shape[0]
    nblk = tokens // BT
    x, dy = inputs[0], cotangent[0]
    me = lax.axis_index("seq")
    me_arr = me.reshape(1).astype(jnp.int32)

    norms = jnp.concatenate(
        [norm_gains, norm_biases, jnp.zeros((rows, 124), bf16)], axis=1
    )
    first = jnp.concatenate([w_qkv[:, width : 2 * width], w_feat, norms], axis=1)
    values_w = w_qkv[:, 2 * width :]
    second = jnp.concatenate([w_qkv[:, :width], w_out], axis=1)
    keys_blocks = seq_blocks(stream_rows(first, depth), n_seq, False)
    vals_blocks = seq_blocks(stream_rows(values_w, depth), n_seq, True)
    second_blocks = seq_blocks(stream_rows(second, depth), n_seq, False)
    fc_blocks = seq_blocks(stream_rows(w_fc, depth), n_seq, True)
    proj_blocks = seq_blocks(stream_rows(w_proj, depth), n_seq, False)

    marks = resets[0].reshape(nblk, BT).astype(bf16)
    upper = jnp.triu(jnp.ones((BT, BT), bf16))
    inner = jnp.dot(marks, upper, preferred_element_type=f32)
    ends = jnp.cumsum(inner[:, -1])
    cend = jnp.concatenate([jnp.zeros((1,), f32), ends])
    counts = inner + cend[:-1, None]
    cnt_col = counts.reshape(tokens, 1)
    cnt_row = counts.reshape(1, tokens)
    keep_dev = jnp.where(ends[-1] == 0.0, 1.0, 0.0).astype(f32)
    tile = jnp.full((8, 128), keep_dev, f32)
    keeps = jnp.stack([xor_send(tile, n_seq, r)[0, 0] if r else keep_dev for r in range(n_seq)])
    index = jnp.arange(n_seq) ^ me
    i_abs, j_abs = index[None, :], index[:, None]
    ahead = jnp.where((i_abs > j_abs) & (i_abs < me), keeps[None, :], 1.0)
    coef_f = jnp.where(index < me, jnp.prod(ahead, axis=1), 0.0)
    behind = jnp.where((i_abs < j_abs) & (i_abs > me), keeps[None, :], 1.0)
    coef_b = jnp.where(index > me, jnp.prod(behind, axis=1), 0.0)

    packed = (pairs + 1, 128, 128)
    full = (heads, 128, 128)
    h_one, keys, vals, phi_k, state, gb = pl.pallas_call(
        functools.partial(keys_body, n_seq, pairs),
        name="keys",
        grid=(tokens // TM,),
        in_specs=[smem(), smem(), rows_spec(TM, width), rows_spec(TM, 1)] + [whole()] * (2 * n_seq),
        out_specs=[rows_spec(TM, width)] * 3
        + [rows_spec(TM, 2 * width), full_spec(packed), full_spec((8, width))],
        out_shape=[sds((tokens, width), bf16)] * 3
        + [sds((tokens, 2 * width), bf16), sds(packed, bf16), sds((8, width), f32)],
        scratch_shapes=[
            pltpu.VMEM((width, width + 256), bf16),
            pltpu.VMEM((width, width), bf16),
            pltpu.VMEM((pairs, 128, 256), bf16),
            pltpu.VMEM(full, f32),
            dma(2, n_seq),
        ],
        compiler_params=cparams(),
    )(me_arr, cend, x, cnt_col, *keys_blocks, *vals_blocks)
    feat_full = assembled([b[:, width : width + 128] for b in keys_blocks], me)
    states = seq_blocks(state, n_seq, False)

    queries, phi_q, num, den, srel = pl.pallas_call(
        functools.partial(local_body, n_seq, pairs),
        name="local",
        grid=(nblk,),
        in_specs=[
            smem(), smem(), rows_spec(BT, width), rows_spec(BT, 2 * width), rows_spec(BT, width),
            rows_spec(BT, 1), pl.BlockSpec((1, BT), lambda i: (0, i)), full_spec((width, 128)),
        ]
        + [whole()] * n_seq,
        out_specs=[
            rows_spec(BT, width), rows_spec(BT, 2 * width), rows_spec(BT, width), rows_spec(BT, width),
            pl.BlockSpec((1,) + full, lambda i: (i, 0, 0, 0)),
        ],
        out_shape=[
            sds((tokens, width), bf16), sds((tokens, 2 * width), bf16), sds((tokens, width), f32),
            sds((tokens, width), f32), sds((nblk,) + full, bf16),
        ],
        scratch_shapes=[
            pltpu.VMEM((width, width), bf16),
            pltpu.VMEM((pairs, 128, 256), bf16),
            pltpu.VMEM(full, f32),
            dma(n_seq),
        ],
        compiler_params=cparams(),
    )(me_arr, cend, h_one, phi_k, vals, cnt_col, cnt_row, feat_full, *second_blocks)

    y, att, h_two, act, d_fc, d_att, d_mid, dd, s_in, g_state, sums = pl.pallas_call(
        functools.partial(middle_body, n_seq, pairs),
        name="middle",
        grid=(tokens // TM,),
        in_specs=[
            smem(), smem(), rows_spec(TM, width), rows_spec(TM, width), rows_spec(TM, width),
            rows_spec(TM, width), rows_spec(TM, 2 * width), rows_spec(TM, 1), full_spec((8, width)),
        ]
        + [whole()] * (4 * n_seq),
        out_specs=[
            rows_spec(TM, width), rows_spec(TM, width), rows_spec(TM, width), rows_spec(TM, hidden),
            rows_spec(TM, hidden), rows_spec(TM, width), rows_spec(TM, width), rows_spec(TM, 2 * width),
            full_spec(full), full_spec(packed), full_spec((8, width)),
        ],
        out_shape=[
            sds((tokens, width), bf16), sds((tokens, width), bf16), sds((tokens, width), bf16),
            sds((tokens, hidden), bf16), sds((tokens, hidden), bf16), sds((tokens, width), bf16),
            sds((tokens, width), f32), sds((tokens, 2 * width), bf16), sds(full, bf16), sds(packed, bf16),
            sds((8, width), f32),
        ],
        scratch_shapes=[
            pltpu.VMEM((width, width), bf16),
            pltpu.VMEM((width, hidden), bf16),
            pltpu.VMEM((hidden, width), bf16),
            pltpu.VMEM((TM, width), f32),
            pltpu.VMEM(full, f32),
            pltpu.VMEM((n_seq,) + packed, bf16),
            dma(4, n_seq),
        ],
        compiler_params=cparams(),
    )(
        me_arr, coef_f, x, dy, num, den, phi_q, cnt_col, gb,
        *second_blocks, *fc_blocks, *proj_blocks, *states,
    )

    g_states = seq_blocks(g_state, n_seq, True)
    squares = jnp.sum(sums[:3], axis=1)
    for b in range(n_seq.bit_length() - 1):
        squares = squares + xor_send(squares, n_seq, 1 << b)
    branch_rms = jnp.sqrt(squares / (tokens * n_seq * width)).reshape(1, 3)

    grad_proj = to_owner(mm_f(act, dy).astype(bf16), n_seq, depth, False)
    grad_fc = to_owner(mm_f(h_two, d_fc).astype(bf16), n_seq, depth, True)
    g_out = mm_f(att, d_att).astype(bf16)

    spec = functools.partial(rows_spec, BT, back=nblk)
    d_qkv, g_feat = pl.pallas_call(
        functools.partial(back_body, n_seq, pairs),
        name="back",
        grid=(nblk,),
        in_specs=[
            smem(), smem(), spec(width), spec(width), spec(width), spec(2 * width), spec(2 * width),
            spec(2 * width), pl.BlockSpec((1,) + full, lambda i: (nblk - 1 - i, 0, 0, 0)), full_spec(full),
            spec(1), pl.BlockSpec((1, BT), lambda i: (0, nblk - 1 - i)), full_spec((width, 128)),
        ]
        + [whole()] * n_seq,
        out_specs=[spec(3 * width), full_spec((width, 128))],
        out_shape=[sds((tokens, 3 * width), bf16), sds((width, 128), bf16)],
        scratch_shapes=[
            pltpu.VMEM((pairs, 128, 256), bf16),
            pltpu.VMEM((pairs, 128, 256), bf16),
            pltpu.VMEM(full, f32),
            pltpu.VMEM((pairs, 128, 256), f32),
            pltpu.VMEM((pairs, 128, 256), f32),
            pltpu.VMEM((n_seq,) + packed, bf16),
            dma(n_seq),
        ],
        compiler_params=cparams(),
    )(
        coef_b, cend, queries, keys, vals, phi_q, phi_k, dd, srel, s_in, cnt_col, cnt_row, feat_full,
        *g_states,
    )

    cut = 3 * width // 2
    grad_left = to_owner(mm_f(h_one, d_qkv[:, :cut]).astype(bf16), n_seq, depth, False)
    grad_right = to_owner(
        jnp.concatenate([mm_f(h_one, d_qkv[:, cut:]).astype(bf16), g_feat], axis=1), n_seq, depth, True
    )
    dx, sums_one = pl.pallas_call(
        functools.partial(enter_body, n_seq),
        name="enter",
        grid=(tokens // TM,),
        in_specs=[
            smem(), rows_spec(TM, width), rows_spec(TM, width), rows_spec(TM, 3 * width), full_spec((8, width)),
        ]
        + [whole()] * (3 * n_seq),
        out_specs=[rows_spec(TM, width), full_spec((8, width))],
        out_shape=[sds((tokens, width), f32), sds((8, width), f32)],
        scratch_shapes=[pltpu.VMEM((width, width), bf16)] * 3 + [dma(3, n_seq)],
        compiler_params=cparams(),
    )(me_arr, x, d_mid, d_qkv, gb, *second_blocks, *keys_blocks, *vals_blocks)
    norm_cols = jnp.stack([sums_one[0], sums[3], sums_one[1], sums[4]], axis=1).astype(bf16)
    last = to_owner(
        jnp.concatenate([g_out, norm_cols, jnp.zeros((width, 124), bf16)], axis=1), n_seq, depth, False
    )
    return (
        y[None],
        dx[None],
        last[:, width : width + 2],
        last[:, width + 2 : width + 4],
        jnp.concatenate([grad_left, grad_right[:, : 3 * width - cut]], axis=1),
        grad_right[:, 3 * width - cut :],
        last[:, :width],
        grad_fc,
        grad_proj,
        branch_rms,
    )


def assembled(blocks, me):
    size = len(blocks)
    rows = blocks[0].shape[0]
    out = jnp.zeros((size * rows, blocks[0].shape[1]), blocks[0].dtype)
    for r, block in enumerate(blocks):
        out = lax.dynamic_update_slice_in_dim(out, block, (me ^ r) * rows, 0)
    return out


def solution(mesh):
    both = P(("seq", "stream"), None)
    acts = P("stream", "seq", None)
    placed = (acts, P("stream", "seq"), both, both, both, both, both, both, both, acts)
    return jax.shard_map(
        functools.partial(shards, mesh.shape["seq"], mesh.shape["stream"]),
        mesh=mesh,
        in_specs=placed,
        out_specs=(acts, acts, both, both, both, both, both, both, both, P("stream", None)),
        check_vma=False,
    )
```

time: 1430 us -> 506 us (0.35); the launches traced: 1410 us -> 498 us
  blocking collectives: 297 us -> 0 us
  waiting for transfers between devices: 390 us -> 140 us
  local copies, waits for them, and re-layouts: 283 us -> 40.4 us
  matrix products: 258 us -> 25.1 us
  Pallas kernels: 0 us -> 160 us
  other arithmetic: 158 us -> 16.5 us
  starting transfers between devices: 0.44 us -> 113 us
    reduce_scatter x4 -> x0, waiting for transfers between devices: 386 us -> none  [the longest x1 142 us: shards(): lax.psum_scatter(grad_proj, ('seq', 'stream'), scatter_dimension=0, tiled...]
    all_gather x5 -> x0, blocking collectives: 226 us -> none  [the longest x1 68 us: shards(): lax.all_gather(norm_biases, ('seq', 'stream'), axis=0, tiled=True)]
    dot_general x34 -> x6, matrix products: 240 us -> 25.1 us  [the longest x5 24.9 us: mm_f(): lax.dot_general(a, b, (((0,), (0,)), ((), ())), preferred_element_type=f32)]
    pallas_call x0 -> x5, Pallas kernels: none -> 160 us  [the longest x1 45 us: shards(): pl.pallas_call(functools.partial(back_body, n_seq, pairs), name='back', g...]
    ppermute x0 -> x104, waiting for transfers between devices: none -> 140 us  [the longest x74 86.1 us: xor_send(): return lax.ppermute(arr, 'seq', [(i, i ^ mask) for i in range(size)])]
    ppermute x0 -> x104, starting transfers between devices: none -> 113 us  [the longest x74 72.7 us: xor_send(): return lax.ppermute(arr, 'seq', [(i, i ^ mask) for i in range(size)])]
    add x79 -> x9, other arithmetic: 76 us -> 1.74 us  [the longest x5 1.65 us: to_owner(): total + lax.ppermute(piece, 'stream', [(i, (i + d) % depth) for i in rang...]
    dynamic_slice x117 -> x5, local copies, waits for them, and re-layouts: 72.5 us -> 0.15 us  [stream_rows(): lax.dynamic_slice_in_dim(both, (depth - 1 - place) * rows, depth * rows, 0)]
  transfers between devices with their start and end apart: 11 -> 104, of which waited for: 4 -> 42; matrix products, arithmetic and copies ran while one was open for 34% -> 15% of each run, Pallas kernels for 0% -> 23%
where the time goes in v1:
time: 506 us; the launch traced here: 498 us
  Pallas kernels  160 us (32%)
  waiting for transfers between devices  140 us (28%)
  starting transfers between devices  113 us (22%)
  local copies, waits for them, and re-layouts  40.4 us (8%)
  matrix products  25.1 us (5%)
  other arithmetic  16.5 us (3%)
    ppermute x74, waiting for transfers between devices, xor_send(): return lax.ppermute(arr, 'seq', [(i, i ^ mask) for i in range(size)])  86.1 us
    ppermute x74, starting transfers between devices, xor_send(): return lax.ppermute(arr, 'seq', [(i, i ^ mask) for i in range(size)])  72.7 us
    pallas_call x1, Pallas kernels, shards(): pl.pallas_call(functools.partial(back_body, n_seq, pairs), name='back', g...  45 us
    pallas_call x1, Pallas kernels, shards(): pl.pallas_call(functools.partial(middle_body, n_seq, pairs), name='middle...  43 us
    pallas_call x1, Pallas kernels, shards(): pl.pallas_call(functools.partial(local_body, n_seq, pairs), name='local',...  38.6 us
    ppermute x15, waiting for transfers between devices, stream_rows(): lax.ppermute(shard, 'stream', [(i, (i + d) % depth) for i in range(depth)])  30.5 us
    dot_general x5, matrix products, mm_f(): lax.dot_general(a, b, (((0,), (0,)), ((), ())), preferred_element_type=f32)  24.9 us
    ppermute x15, starting transfers between devices, stream_rows(): lax.ppermute(shard, 'stream', [(i, (i + d) % depth) for i in range(depth)])  24.5 us
  transfers between devices with their start and end apart: 104, of which 42 were waited for; matrix products, arithmetic and copies ran while one was open for 15% of the time, Pallas kernels for 23%

profile of v1, /device:TPU:9, one launch (start us, length us, event | category | flops | bytes accessed | tf_op | source)
XLA Modules:
  0.0 497.8 jit_solution(9868273598995222035)
XLA Ops:
  1.5 2.5 collective-permute-start.18
  4.0 2.2 collective-permute-start.19
  8.3 3.6 collective-permute-start.6
  14.1 1.9 collective-permute-start.2
  19.2 2.8 collective-permute-done.7
  22.0 2.4 collective-permute-start.8
  24.4 1.6 collective-permute-done.8
  26.0 2.9 collective-permute-done.9
  28.9 2.0 collective-permute-start.27
  32.6 3.5 collective-permute-start.28
  36.2 1.7 collective-permute-done.28
  37.9 4.1 collective-permute-done.29
  42.0 2.2 collective-permute-start.37
  44.3 1.9 collective-permute-done.37
  46.3 3.6 collective-permute-start.38
  49.9 3.0 collective-permute-done.38
  54.0 4.1 collective-permute-done.39
  58.4 12.0 %collective-permute-start.4 = (f32[8,128]{1,0:T(8,128)S(1)}, f32[8,128]{1,0:T(8,128)S(1)}, u32[]{:S(2)}, u32[]{:S(2)}) collective-permute-start(f32[8,128]{1,0:T(8,128)S(1)} %broadcast_in_dim.53), channel_id=1, source_target_pairs={{0,20},{4,16},{8,28},{12,24},{16,4},{20,0},{24,12},{28,8},{1,21},{... | collective-permute-start | bytes 12296 | tf_op jit(solution)/shard_map/ppermute | solution.py:32
  70.9 3.6 collective-permute-start.47
  79.7 4.4 collective-permute-done.48
  84.7 2.6 collective-permute-done.49
  91.4 1.9 collective-permute-done.11.refs_2_.refs_10_
  93.3 2.2 collective-permute-start.24
  96.9 1.8 collective-permute-start.22
  100.1 2.7 collective-permute-done.31.refs_2_
  108.7 16.4 %collective-permute-done.35.refs_6_ = bf16[96,1536]{1,0:T(8,128)(2,1)S(1)} collective-permute-done((bf16[96,1536]{1,0:T(8,128)(2,1)S(1)}, bf16[96,1536]{1,0:T(8,128)(2,1)S(1)}, u32[]{:S(2)}, u32[]{:S(2)}) %collective-permute-start.35) | collective-permute-done | bytes 294944 | tf_op jit(solution)/shard_map/ppermute | solution.py:32
  137.5 4.5 stack.9
  143.4 21.9 %keys.1 = (bf16[1024,768]{1,0:T(8,128)(2,1)}, bf16[1024,768]{1,0:T(8,128)(2,1)}, bf16[1024,768]{1,0:T(8,128)(2,1)}, bf16[1024,1536]{1,0:T(8,128)(2,1)}, bf16[7,128,128]{2,1,0:T(8,128)(2,1)}, /*index=5*/f32[8,768]{1,0:T(8,128)}) custom-call(s32[1]{0:T(128)} %bitcast.me_ref, f32[9]{0:T(128)} %copy-done.61, bf16[1024,768]{1,0:T(8,128)(2,1)} %bitcast.171, ...), custom_call_target="tpu_custom_call" | custom-call | tf_op jit(solution)/shard_map/keys/pallas_call | solution.py:589
  168.6 4.2 collective-permute-done.58.refs_26_
  179.0 2.9 collective-permute-start.42
  184.5 6.0 %collective-permute-done.45.refs_14_ = bf16[96,3072]{1,0:T(8,128)(2,1)S(1)} collective-permute-done((bf16[96,3072]{1,0:T(8,128)(2,1)}, bf16[96,3072]{1,0:T(8,128)(2,1)S(1)}, u32[]{:S(2)}, u32[]{:S(2)}) %collective-permute-start.45) | collective-permute-done | bytes 589856 | tf_op jit(solution)/shard_map/ppermute | solution.py:32
  191.8 1.6 collective-permute-start.56
  196.4 38.6 %local.1 = (bf16[1024,768]{1,0:T(8,128)(2,1)}, bf16[1024,1536]{1,0:T(8,128)(2,1)}, f32[1024,768]{1,0:T(8,128)}, f32[1024,768]{1,0:T(8,128)}, bf16[8,12,128,128]{3,2,1,0:T(8,128)(2,1)}) custom-call(s32[1]{0:T(128)} %bitcast.me_ref, f32[9]{0:T(128)} %copy-done.61, bf16[1024,768]{1,0:T(8,128)(2,1)} %get-tuple-element.36.h_ref, ...), custom_call_target="tpu_custom_call" | custom-call | tf_op jit(solution)/shard_map/local/pallas_call | solution.py:610
  236.2 43.0 %middle.1 = (bf16[1024,768]{1,0:T(8,128)(2,1)}, bf16[1024,768]{1,0:T(8,128)(2,1)}, bf16[1024,768]{1,0:T(8,128)(2,1)}, bf16[1024,3072]{1,0:T(8,128)(2,1)}, bf16[1...) custom-call(s32[1]{0:T(128)} %bitcast.me_ref, ...), custom_call_target="tpu_custom_call" | custom-call | tf_op jit(solution)/shard_map/middle/pallas_call | solution.py:636
  282.5 8.7 %convolution_convert_fusion = bf16[3072,768]{1,0:T(8,128)(2,1)S(1)} fusion(bf16[1024,3072]{1,0:T(8,128)(2,1)} %get-tuple-element.61, bf16[1,1024,768]{2,1,0:T(8,128)(2,1)S(1)} %copy-done.17), kind=kOutput, calls=%fused_computation | convolution fusion | flops 4834197504 | bytes 12582912 | tf_op jit(solution)/shard_map/dot_general | solution.py:28
  291.2 5.9 %convolution_convert_fusion.1 = bf16[768,3072]{1,0:T(8,128)(2,1)S(1)} fusion(bf16[1024,768]{1,0:T(8,128)(2,1)S(1)} %copy-done.65, bf16[1024,3072]{1,0:T(8,128)(2,1)S(1)} %copy-done.62), kind=kOutput, calls=%fused_computation.1 | convolution fusion | flops 4834197504 | bytes 12582912 | tf_op jit(solution)/shard_map/dot_general | solution.py:28
  297.1 1.5 dynamic-slice_bitcast_fusion.1
  298.7 1.9 copy-done.1
  303.9 3.3 collective-permute-done.69.refs_6_
  308.6 1.6 dynamic-slice_bitcast_fusion
  313.4 1.7 collective-permute-done.103
  315.0 2.3 collective-permute-start.95
  318.9 45.0 %back.1 = (bf16[1024,2304]{1,0:T(8,128)(2,1)}, bf16[768,128]{1,0:T(8,128)(2,1)}) custom-call(f32[8]{0:T(128)} %broadcast_select_fusion.coef_ref, f32[9]{0:T(128)} %copy-done.61, bf16[1024,768]{1,0:T(8,128)(2,1)} %get-tuple-element.46.q_ref, bf16[1024,768]{1,0:T(8,128)(2,1)} %get-tuple-element.47.k_ref, bf16[1024,768]{1,0:T(8,128)(2,1)} %get-tuple-element.38.v_ref, ...), custom_call_target="tpu_custom_call" | custom-call | tf_op jit(solution)/shard_map/back/pallas_call | solution.py:682
  363.9 5.3 %convolution_convert_fusion.3 = bf16[768,1152]{1,0:T(8,128)(2,1)} fusion(bf16[1024,768]{1,0:T(8,128)(2,1)S(1)} %copy-done.18, bf16[1024,2304]{1,0:T(8,128)(2,1)} %get-tuple-element.52.dqkv_ref), kind=kOutput, calls=%fused_computation.7 | convolution fusion | flops 1812824064 | bytes 5701632 | tf_op jit(solution)/shard_map/dot_general | solution.py:28
  369.3 3.5 convolution_convert_fusion.2
  372.8 11.0 %enter.1 = (f32[1024,768]{1,0:T(8,128)}, f32[8,768]{1,0:T(8,128)}) custom-call(s32[1]{0:T(128)} %bitcast.me_ref, bf16[1024,768]{1,0:T(8,128)(2,1)} %bitcast.173, f32[1024,768]{1,0:T(8,128)} %get-tuple-element.45.dr_ref, bf16[1024,2304]{1,0:T(8,128)(2,1)} %get-tuple-element.52.dqkv_ref, f32[8,768]{1,0:T(8,128)} %get-tuple-element.42.gb_ref, ...), custom_call_target="tpu_custom_call" | custom-call | tf_op jit(solution)/shard_map/enter/pallas_call | solution.py:714
  390.8 7.8 %collective-permute-done.72 = bf16[2,96,896]{2,1,0:T(8,128)(2,1)S(1)} collective-permute-done((bf16[2,96,896]{2,1,0:T(8,128)(2,1)S(1)}, bf16[2,96,896]{2,1,0:T(8,128)(2,1)S(1)}, u32[]{:S(2)}, u32[]{:S(2)}) %collective-permute-start.72) | collective-permute-done | bytes 344096 | tf_op jit(solution)/shard_map/ppermute | solution.py:32
  399.8 3.8 collective-permute-done.73
  403.7 2.3 collective-permute-start.74
  408.3 1.6 collective-permute-done.75
  412.6 4.1 collective-permute-done.78
  420.6 4.7 collective-permute-done.79
  425.5 2.6 collective-permute-start.81
  428.2 3.1 fusion
  432.0 2.6 fusion.1
  435.6 1.7 collective-permute-start.86
  437.2 1.7 collective-permute-start.87
  439.0 2.2 collective-permute-done.87
  443.0 11.8 %collective-permute-done.96 = bf16[2,384,768]{2,1,0:T(8,128)(2,1)S(1)} collective-permute-done((bf16[2,384,768]{2,1,0:T(8,128)(2,1)S(1)}, bf16[2,384,768]{2,1,0:T(8,128)(2,1)S(1)}, u32[]{:S(2)}, u32[]{:S(2)}) %collective-permute-start.96) | collective-permute-done | bytes 1179680 | tf_op jit(solution)/shard_map/ppermute | solution.py:32
  460.0 10.6 %collective-permute-done.97 = bf16[384,768]{1,0:T(8,128)(2,1)S(1)} collective-permute-done((bf16[384,768]{1,0:T(8,128)(2,1)S(1)}, bf16[384,768]{1,0:T(8,128)(2,1)S(1)}, u32[]{:S(2)}, u32[]{:S(2)}) %collective-permute-start.97) | collective-permute-done | bytes 589856 | tf_op jit(solution)/shard_map/ppermute | solution.py:32
  472.3 3.3 collective-permute-start.99
  477.9 2.0 collective-permute-done.99
  480.7 8.7 %collective-permute-done.92 = bf16[24,3072]{1,0:T(8,128)(2,1)S(1)} collective-permute-done((bf16[24,3072]{1,0:T(8,128)(2,1)S(1)}, bf16[24,3072]{1,0:T(8,128)(2,1)S(1)}, u32[]{:S(2)}, u32[]{:S(2)}) %collective-permute-start.92) | collective-permute-done | bytes 147488 | tf_op jit(solution)/shard_map/ppermute | solution.py:80
  489.3 6.3 %collective-permute-done.93 = bf16[24,3072]{1,0:T(8,128)(2,1)S(1)} collective-permute-done((bf16[24,3072]{1,0:T(8,128)(2,1)S(1)}, bf16[24,3072]{1,0:T(8,128)(2,1)S(1)}, u32[]{:S(2)}, u32[]{:S(2)}) %collective-permute-start.93) | collective-permute-done | bytes 147488 | tf_op jit(solution)/shard_map/ppermute | solution.py:80
  (449 shorter events, 106.0 us)
Async XLA Ops:
  1.5 12.3 %collective-permute-start.17 = (bf16[24,768]{1,0:T(8,128)(2,1)S(1)}, bf16[24,768]{1,0:T(8,128)(2,1)S(1)}, u32[]{:S(2)}, u32[]{:S(2)}) collective-permute-start(bf16[24,768]{1,0:T(8,128)(2,1)S(1)} %slice.115), channel_id=1, source_target_pairs={{0,3},{1,0},{2,1},{3,2},{4,7},{5,4},{6,5},{7,6},{8,11},{9,8},{10,9... | collective-permute-start | bytes 110600 | tf_op jit(solution)/shard_map/ppermute | solution.py:37
  1.5 12.6 %collective-permute-start.18 = (bf16[24,768]{1,0:T(8,128)(2,1)S(1)}, bf16[24,768]{1,0:T(8,128)(2,1)S(1)}, u32[]{:S(2)}, u32[]{:S(2)}) collective-permute-start(bf16[24,768]{1,0:T(8,128)(2,1)S(1)} %slice.115), channel_id=1, source_target_pairs={{0,2},{1,3},{2,0},{3,1},{4,6},{5,7},{6,4},{7,5},{8,10},{9,11},{10,... | collective-permute-start | bytes 110600 | tf_op jit(solution)/shard_map/ppermute | solution.py:37
  4.0 12.0 %collective-permute-start.19 = (bf16[24,768]{1,0:T(8,128)(2,1)S(1)}, bf16[24,768]{1,0:T(8,128)(2,1)S(1)}, u32[]{:S(2)}, u32[]{:S(2)}) collective-permute-start(bf16[24,768]{1,0:T(8,128)(2,1)S(1)} %slice.115), channel_id=1, source_target_pairs={{0,1},{1,2},{2,3},{3,0},{4,5},{5,6},{6,7},{7,4},{8,9},{9,10},{10,1... | collective-permute-start | bytes 110600 | tf_op jit(solution)/shard_map/ppermute | solution.py:37
  8.3 50.1 %collective-permute-start.6 = (f32[8,128]{1,0:T(8,128)S(1)}, f32[8,128]{1,0:T(8,128)S(1)}, u32[]{:S(2)}, u32[]{:S(2)}) collective-permute-start(f32[8,128]{1,0:T(8,128)S(1)} %broadcast_in_dim.53), channel_id=1, source_target_pairs={{0,28},{4,24},{8,20},{12,16},{16,12},{20,8},{24,4},{28,0},{1,29},{... | collective-permute-start | bytes 12296 | tf_op jit(solution)/shard_map/ppermute | solution.py:32
  12.0 58.4 %collective-permute-start = (f32[8,128]{1,0:T(8,128)S(1)}, f32[8,128]{1,0:T(8,128)S(1)}, u32[]{:S(2)}, u32[]{:S(2)}) collective-permute-start(f32[8,128]{1,0:T(8,128)S(1)} %broadcast_in_dim.53), channel_id=1, source_target_pairs={{0,4},{4,0},{8,12},{12,8},{16,20},{20,16},{24,28},{28,24},{1,5},{5... | collective-permute-start | bytes 12296 | tf_op jit(solution)/shard_map/ppermute | solution.py:32
  13.8 57.1 %collective-permute-start.1 = (f32[8,128]{1,0:T(8,128)S(1)}, f32[8,128]{1,0:T(8,128)S(1)}, u32[]{:S(2)}, u32[]{:S(2)}) collective-permute-start(f32[8,128]{1,0:T(8,128)S(1)} %broadcast_in_dim.53), channel_id=1, source_target_pairs={{0,8},{4,12},{8,0},{12,4},{16,24},{20,28},{24,16},{28,20},{1,9},{5... | collective-permute-start | bytes 12296 | tf_op jit(solution)/shard_map/ppermute | solution.py:32
  14.1 60.4 %collective-permute-start.2 = (f32[8,128]{1,0:T(8,128)S(1)}, f32[8,128]{1,0:T(8,128)S(1)}, u32[]{:S(2)}, u32[]{:S(2)}) collective-permute-start(f32[8,128]{1,0:T(8,128)S(1)} %broadcast_in_dim.53), channel_id=1, source_target_pairs={{0,12},{4,8},{8,4},{12,0},{16,28},{20,24},{24,20},{28,16},{1,13},{... | collective-permute-start | bytes 12296 | tf_op jit(solution)/shard_map/ppermute | solution.py:32
  58.1 16.4 %collective-permute-start.3 = (f32[8,128]{1,0:T(8,128)S(1)}, f32[8,128]{1,0:T(8,128)S(1)}, u32[]{:S(2)}, u32[]{:S(2)}) collective-permute-start(f32[8,128]{1,0:T(8,128)S(1)} %broadcast_in_dim.53), channel_id=1, source_target_pairs={{0,16},{4,20},{8,24},{12,28},{16,0},{20,4},{24,8},{28,12},{1,17},{... | collective-permute-start | bytes 12296 | tf_op jit(solution)/shard_map/ppermute | solution.py:32
  58.4 17.6 %collective-permute-start.4 = (f32[8,128]{1,0:T(8,128)S(1)}, f32[8,128]{1,0:T(8,128)S(1)}, u32[]{:S(2)}, u32[]{:S(2)}) collective-permute-start(f32[8,128]{1,0:T(8,128)S(1)} %broadcast_in_dim.53), channel_id=1, source_target_pairs={{0,20},{4,16},{8,28},{12,24},{16,4},{20,0},{24,12},{28,8},{1,21},{... | collective-permute-start | bytes 12296 | tf_op jit(solution)/shard_map/ppermute | solution.py:32
  74.5 9.6 %collective-permute-start.48 = (bf16[96,768]{1,0:T(8,128)(2,1)S(1)}, bf16[96,768]{1,0:T(8,128)(2,1)S(1)}, u32[]{:S(2)}, u32[]{:S(2)}) collective-permute-start(bf16[96,768]{1,0:T(8,128)(2,1)S(1)} %copy-done.42), channel_id=1, source_target_pairs={{0,2},{1,3},{2,0},{3,1},{4,6},{5,7},{6,4},{7,5},{8,10},{9,11},{10,... | collective-permute-start | bytes 442376 | tf_op jit(solution)/shard_map/ppermute | solution.py:37
  74.5 12.8 %collective-permute-start.49 = (bf16[96,768]{1,0:T(8,128)(2,1)S(1)}, bf16[96,768]{1,0:T(8,128)(2,1)S(1)}, u32[]{:S(2)}, u32[]{:S(2)}) collective-permute-start(bf16[96,768]{1,0:T(8,128)(2,1)S(1)} %copy-done.42), channel_id=1, source_target_pairs={{0,1},{1,2},{2,3},{3,0},{4,5},{5,6},{6,7},{7,4},{8,9},{9,10},{10,1... | collective-permute-start | bytes 442376 | tf_op jit(solution)/shard_map/ppermute | solution.py:37
  76.0 12.3 %collective-permute-start.23 = (bf16[96,768]{1,0:T(8,128)(2,1)S(1)}, bf16[96,768]{1,0:T(8,128)(2,1)S(1)}, u32[]{:S(2)}, u32[]{:S(2)}) collective-permute-start(bf16[96,768]{1,0:T(8,128)(2,1)S(1)} %constant_dynamic-slice_fusion.3.refs_8_.refs_16_), channel_id=1, source_target_pairs={{0,16},{4,20},{8,24},{12,28},{16,0},{20,4},{24,8},{28,12},{1,17},{... | collective-permute-start | bytes 442376 | tf_op jit(solution)/shard_map/ppermute | solution.py:32
  77.3 11.8 %collective-permute-start.21 = (bf16[96,768]{1,0:T(8,128)(2,1)S(1)}, bf16[96,768]{1,0:T(8,128)(2,1)S(1)}, u32[]{:S(2)}, u32[]{:S(2)}) collective-permute-start(bf16[96,768]{1,0:T(8,128)(2,1)S(1)} %constant_dynamic-slice_fusion.3.refs_8_.refs_16_), channel_id=1, source_target_pairs={{0,8},{4,12},{8,0},{12,4},{16,24},{20,28},{24,16},{28,20},{1,9},{5... | collective-permute-start | bytes 442376 | tf_op jit(solution)/shard_map/ppermute | solution.py:32
  78.6 11.1 %collective-permute-start.20 = (bf16[96,768]{1,0:T(8,128)(2,1)S(1)}, bf16[96,768]{1,0:T(8,128)(2,1)S(1)}, u32[]{:S(2)}, u32[]{:S(2)}) collective-permute-start(bf16[96,768]{1,0:T(8,128)(2,1)S(1)} %constant_dynamic-slice_fusion.3.refs_8_.refs_16_), channel_id=1, source_target_pairs={{0,4},{4,0},{8,12},{12,8},{16,20},{20,16},{24,28},{28,24},{1,5},{5... | collective-permute-start | bytes 442376 | tf_op jit(solution)/shard_map/ppermute | solution.py:32
  89.2 7.8 %collective-permute-start.25 = (bf16[96,768]{1,0:T(8,128)(2,1)S(1)}, bf16[96,768]{1,0:T(8,128)(2,1)S(1)}, u32[]{:S(2)}, u32[]{:S(2)}) collective-permute-start(bf16[96,768]{1,0:T(8,128)(2,1)S(1)} %collective-permute-done.23.refs_12_.refs_20_), channel_id=1, source_target_pairs={{0,8},{4,12},{8,0},{12,4},{16,24},{20,28},{24,16},{28,20},{1,9},{5... | collective-permute-start | bytes 442376 | tf_op jit(solution)/shard_map/ppermute | solution.py:32
  89.7 13.1 %collective-permute-start.31 = (bf16[96,1536]{1,0:T(8,128)(2,1)S(1)}, bf16[96,1536]{1,0:T(8,128)(2,1)S(1)}, u32[]{:S(2)}, u32[]{:S(2)}) collective-permute-start(bf16[96,1536]{1,0:T(8,128)(2,1)S(1)} %constant_dynamic-slice_fusion.2.refs_0_), channel_id=1, source_target_pairs={{0,8},{4,12},{8,0},{12,4},{16,24},{20,28},{24,16},{28,20},{1,9},{5... | collective-permute-start | bytes 884744 | tf_op jit(solution)/shard_map/ppermute | solution.py:32
  90.7 13.4 %collective-permute-start.33 = (bf16[96,1536]{1,0:T(8,128)(2,1)S(1)}, bf16[96,1536]{1,0:T(8,128)(2,1)S(1)}, u32[]{:S(2)}, u32[]{:S(2)}) collective-permute-start(bf16[96,1536]{1,0:T(8,128)(2,1)S(1)} %constant_dynamic-slice_fusion.2.refs_0_), channel_id=1, source_target_pairs={{0,16},{4,20},{8,24},{12,28},{16,0},{20,4},{24,8},{28,12},{1,17},{... | collective-permute-start | bytes 884744 | tf_op jit(solution)/shard_map/ppermute | solution.py:32
  95.6 8.6 %collective-permute-start.30 = (bf16[96,1536]{1,0:T(8,128)(2,1)S(1)}, bf16[96,1536]{1,0:T(8,128)(2,1)S(1)}, u32[]{:S(2)}, u32[]{:S(2)}) collective-permute-start(bf16[96,1536]{1,0:T(8,128)(2,1)S(1)} %constant_dynamic-slice_fusion.2.refs_0_), channel_id=1, source_target_pairs={{0,4},{4,0},{8,12},{12,8},{16,20},{20,16},{24,28},{28,24},{1,5},{5... | collective-permute-start | bytes 884744 | tf_op jit(solution)/shard_map/ppermute | solution.py:32
  104.2 37.8 %collective-permute-start.43 = (bf16[96,3072]{1,0:T(8,128)(2,1)S(1)}, bf16[96,3072]{1,0:T(8,128)(2,1)}, u32[]{:S(2)}, u32[]{:S(2)}) collective-permute-start(bf16[96,3072]{1,0:T(8,128)(2,1)S(1)} %constant_dynamic-slice_fusion.1.refs_8_), channel_id=1, source_target_pairs={{0,16},{4,20},{8,24},{12,28},{16,0},{20,4},{24,8},{28,12},{1,17},{... | collective-permute-start | bytes 1769480 | tf_op jit(solution)/shard_map/ppermute | solution.py:32
  106.3 18.8 %collective-permute-start.35 = (bf16[96,1536]{1,0:T(8,128)(2,1)S(1)}, bf16[96,1536]{1,0:T(8,128)(2,1)S(1)}, u32[]{:S(2)}, u32[]{:S(2)}) collective-permute-start(bf16[96,1536]{1,0:T(8,128)(2,1)S(1)} %collective-permute-done.31.refs_2_), channel_id=1, source_target_pairs={{0,16},{4,20},{8,24},{12,28},{16,0},{20,4},{24,8},{28,12},{1,17},{... | collective-permute-start | bytes 884744 | tf_op jit(solution)/shard_map/ppermute | solution.py:32
  107.1 19.2 %collective-permute-start.32 = (bf16[96,1536]{1,0:T(8,128)(2,1)S(1)}, bf16[96,1536]{1,0:T(8,128)(2,1)S(1)}, u32[]{:S(2)}, u32[]{:S(2)}) collective-permute-start(bf16[96,1536]{1,0:T(8,128)(2,1)S(1)} %collective-permute-done.31.refs_2_), channel_id=1, source_target_pairs={{0,4},{4,0},{8,12},{12,8},{16,20},{20,16},{24,28},{28,24},{1,5},{5... | collective-permute-start | bytes 884744 | tf_op jit(solution)/shard_map/ppermute | solution.py:32
  107.4 19.9 %collective-permute-start.34 = (bf16[96,1536]{1,0:T(8,128)(2,1)S(1)}, bf16[96,1536]{1,0:T(8,128)(2,1)S(1)}, u32[]{:S(2)}, u32[]{:S(2)}) collective-permute-start(bf16[96,1536]{1,0:T(8,128)(2,1)S(1)} %collective-permute-done.33.refs_4_), channel_id=1, source_target_pairs={{0,4},{4,0},{8,12},{12,8},{16,20},{20,16},{24,28},{28,24},{1,5},{5... | collective-permute-start | bytes 884744 | tf_op jit(solution)/shard_map/ppermute | solution.py:32
  107.7 57.5 %collective-permute-start.41 = (bf16[96,3072]{1,0:T(8,128)(2,1)S(1)}, bf16[96,3072]{1,0:T(8,128)(2,1)}, u32[]{:S(2)}, u32[]{:S(2)}) collective-permute-start(bf16[96,3072]{1,0:T(8,128)(2,1)S(1)} %constant_dynamic-slice_fusion.1.refs_8_), channel_id=1, source_target_pairs={{0,8},{4,12},{8,0},{12,4},{16,24},{20,28},{24,16},{28,20},{1,9},{5... | collective-permute-start | bytes 1769480 | tf_op jit(solution)/shard_map/ppermute | solution.py:32
  125.1 41.3 %collective-permute-start.40 = (bf16[96,3072]{1,0:T(8,128)(2,1)S(1)}, bf16[96,3072]{1,0:T(8,128)(2,1)S(1)}, u32[]{:S(2)}, u32[]{:S(2)}) collective-permute-start(bf16[96,3072]{1,0:T(8,128)(2,1)S(1)} %constant_dynamic-slice_fusion.1.refs_8_), channel_id=1, source_target_pairs={{0,4},{4,0},{8,12},{12,8},{16,20},{20,16},{24,28},{28,24},{1,5},{5... | collective-permute-start | bytes 1769480 | tf_op jit(solution)/shard_map/ppermute | solution.py:32
  126.4 40.8 %collective-permute-start.51 = (bf16[384,768]{1,0:T(8,128)(2,1)S(1)}, bf16[384,768]{1,0:T(8,128)(2,1)}, u32[]{:S(2)}, u32[]{:S(2)}) collective-permute-start(bf16[384,768]{1,0:T(8,128)(2,1)S(1)} %constant_dynamic-slice_fusion.refs_16_), channel_id=1, source_target_pairs={{0,8},{4,12},{8,0},{12,4},{16,24},{20,28},{24,16},{28,20},{1,9},{5... | collective-permute-start | bytes 1769480 | tf_op jit(solution)/shard_map/ppermute | solution.py:32
  127.3 40.4 %collective-permute-start.53 = (bf16[384,768]{1,0:T(8,128)(2,1)S(1)}, bf16[384,768]{1,0:T(8,128)(2,1)}, u32[]{:S(2)}, u32[]{:S(2)}) collective-permute-start(bf16[384,768]{1,0:T(8,128)(2,1)S(1)} %constant_dynamic-slice_fusion.refs_16_), channel_id=1, source_target_pairs={{0,16},{4,20},{8,24},{12,28},{16,0},{20,4},{24,8},{28,12},{1,17},{... | collective-permute-start | bytes 1769480 | tf_op jit(solution)/shard_map/ppermute | solution.py:32
  142.0 31.5 %collective-permute-start.50 = (bf16[384,768]{1,0:T(8,128)(2,1)S(1)}, bf16[384,768]{1,0:T(8,128)(2,1)S(1)}, u32[]{:S(2)}, u32[]{:S(2)}) collective-permute-start(bf16[384,768]{1,0:T(8,128)(2,1)S(1)} %constant_dynamic-slice_fusion.refs_16_), channel_id=1, source_target_pairs={{0,4},{4,0},{8,12},{12,8},{16,20},{20,16},{24,28},{28,24},{1,5},{5... | collective-permute-start | bytes 1769480 | tf_op jit(solution)/shard_map/ppermute | solution.py:32
  166.4 8.9 %collective-permute-start.60 = (bf16[7,128,128]{2,1,0:T(8,128)(2,1)}, bf16[7,128,128]{2,1,0:T(8,128)(2,1)S(1)}, u32[]{:S(2)}, u32[]{:S(2)}) collective-permute-start(bf16[7,128,128]{2,1,0:T(8,128)(2,1)} %get-tuple-element.43.refs_24_), channel_id=1, source_target_pairs={{0,16},{4,20},{8,24},{12,28},{16,0},{20,4},{24,8},{28,12},{1,17},{... | collective-permute-start | bytes 688136 | tf_op jit(solution)/shard_map/ppermute | solution.py:32
  167.1 8.8 %collective-permute-start.57 = (bf16[7,128,128]{2,1,0:T(8,128)(2,1)}, bf16[7,128,128]{2,1,0:T(8,128)(2,1)}, u32[]{:S(2)}, u32[]{:S(2)}) collective-permute-start(bf16[7,128,128]{2,1,0:T(8,128)(2,1)} %get-tuple-element.43.refs_24_), channel_id=1, source_target_pairs={{0,4},{4,0},{8,12},{12,8},{16,20},{20,16},{24,28},{28,24},{1,5},{5... | collective-permute-start | bytes 688136 | tf_op jit(solution)/shard_map/ppermute | solution.py:32
  167.7 8.6 %collective-permute-start.36 = (bf16[96,1536]{1,0:T(8,128)(2,1)S(1)}, bf16[96,1536]{1,0:T(8,128)(2,1)S(1)}, u32[]{:S(2)}, u32[]{:S(2)}) collective-permute-start(bf16[96,1536]{1,0:T(8,128)(2,1)S(1)} %collective-permute-done.35.refs_6_), channel_id=1, source_target_pairs={{0,4},{4,0},{8,12},{12,8},{16,20},{20,16},{24,28},{28,24},{1,5},{5... | collective-permute-start | bytes 884744 | tf_op jit(solution)/shard_map/ppermute | solution.py:32
  173.4 8.5 %collective-permute-start.59 = (bf16[7,128,128]{2,1,0:T(8,128)(2,1)S(1)}, bf16[7,128,128]{2,1,0:T(8,128)(2,1)S(1)}, u32[]{:S(2)}, u32[]{:S(2)}) collective-permute-start(bf16[7,128,128]{2,1,0:T(8,128)(2,1)S(1)} %collective-permute-done.58.refs_26_), channel_id=1, source_target_pairs={{0,4},{4,0},{8,12},{12,8},{16,20},{20,16},{24,28},{28,24},{1,5},{5... | collective-permute-start | bytes 688136 | tf_op jit(solution)/shard_map/ppermute | solution.py:32
  175.3 15.1 %collective-permute-start.45 = (bf16[96,3072]{1,0:T(8,128)(2,1)}, bf16[96,3072]{1,0:T(8,128)(2,1)S(1)}, u32[]{:S(2)}, u32[]{:S(2)}) collective-permute-start(bf16[96,3072]{1,0:T(8,128)(2,1)} %collective-permute-done.43.refs_12_), channel_id=1, source_target_pairs={{0,8},{4,12},{8,0},{12,4},{16,24},{20,28},{24,16},{28,20},{1,9},{5... | collective-permute-start | bytes 1769480 | tf_op jit(solution)/shard_map/ppermute | solution.py:32
  175.9 15.4 %collective-permute-start.44 = (bf16[96,3072]{1,0:T(8,128)(2,1)}, bf16[96,3072]{1,0:T(8,128)(2,1)S(1)}, u32[]{:S(2)}, u32[]{:S(2)}) collective-permute-start(bf16[96,3072]{1,0:T(8,128)(2,1)} %collective-permute-done.43.refs_12_), channel_id=1, source_target_pairs={{0,4},{4,0},{8,12},{12,8},{16,20},{20,16},{24,28},{28,24},{1,5},{5... | collective-permute-start | bytes 1769480 | tf_op jit(solution)/shard_map/ppermute | solution.py:32
  176.3 15.6 %collective-permute-start.55 = (bf16[384,768]{1,0:T(8,128)(2,1)}, bf16[384,768]{1,0:T(8,128)(2,1)S(1)}, u32[]{:S(2)}, u32[]{:S(2)}) collective-permute-start(bf16[384,768]{1,0:T(8,128)(2,1)} %collective-permute-done.51.refs_18_), channel_id=1, source_target_pairs={{0,16},{4,20},{8,24},{12,28},{16,0},{20,4},{24,8},{28,12},{1,17},{... | collective-permute-start | bytes 1769480 | tf_op jit(solution)/shard_map/ppermute | solution.py:32
  179.0 15.1 %collective-permute-start.42 = (bf16[96,3072]{1,0:T(8,128)(2,1)}, bf16[96,3072]{1,0:T(8,128)(2,1)S(1)}, u32[]{:S(2)}, u32[]{:S(2)}) collective-permute-start(bf16[96,3072]{1,0:T(8,128)(2,1)} %collective-permute-done.41.refs_10_), channel_id=1, source_target_pairs={{0,4},{4,0},{8,12},{12,8},{16,20},{20,16},{24,28},{28,24},{1,5},{5... | collective-permute-start | bytes 1769480 | tf_op jit(solution)/shard_map/ppermute | solution.py:32
  184.1 51.1 %collective-permute-start.52 = (bf16[384,768]{1,0:T(8,128)(2,1)}, bf16[384,768]{1,0:T(8,128)(2,1)S(1)}, u32[]{:S(2)}, u32[]{:S(2)}) collective-permute-start(bf16[384,768]{1,0:T(8,128)(2,1)} %collective-permute-done.51.refs_18_), channel_id=1, source_target_pairs={{0,4},{4,0},{8,12},{12,8},{16,20},{20,16},{24,28},{28,24},{1,5},{5... | collective-permute-start | bytes 1769480 | tf_op jit(solution)/shard_map/ppermute | solution.py:32
  190.5 44.7 %collective-permute-start.54 = (bf16[384,768]{1,0:T(8,128)(2,1)}, bf16[384,768]{1,0:T(8,128)(2,1)S(1)}, u32[]{:S(2)}, u32[]{:S(2)}) collective-permute-start(bf16[384,768]{1,0:T(8,128)(2,1)} %collective-permute-done.53.refs_20_), channel_id=1, source_target_pairs={{0,4},{4,0},{8,12},{12,8},{16,20},{20,16},{24,28},{28,24},{1,5},{5... | collective-permute-start | bytes 1769480 | tf_op jit(solution)/shard_map/ppermute | solution.py:32
  191.4 43.9 %collective-permute-start.46 = (bf16[96,3072]{1,0:T(8,128)(2,1)S(1)}, bf16[96,3072]{1,0:T(8,128)(2,1)}, u32[]{:S(2)}, u32[]{:S(2)}) collective-permute-start(bf16[96,3072]{1,0:T(8,128)(2,1)S(1)} %collective-permute-done.45.refs_14_), channel_id=1, source_target_pairs={{0,4},{4,0},{8,12},{12,8},{16,20},{20,16},{24,28},{28,24},{1,5},{5... | collective-permute-start | bytes 1769480 | tf_op jit(solution)/shard_map/ppermute | solution.py:32
  191.8 43.4 %collective-permute-start.56 = (bf16[384,768]{1,0:T(8,128)(2,1)S(1)}, bf16[384,768]{1,0:T(8,128)(2,1)}, u32[]{:S(2)}, u32[]{:S(2)}) collective-permute-start(bf16[384,768]{1,0:T(8,128)(2,1)S(1)} %collective-permute-done.55.refs_22_), channel_id=1, source_target_pairs={{0,4},{4,0},{8,12},{12,8},{16,20},{20,16},{24,28},{28,24},{1,5},{5... | collective-permute-start | bytes 1769480 | tf_op jit(solution)/shard_map/ppermute | solution.py:32
  194.1 41.1 %collective-permute-start.63 = (bf16[7,128,128]{2,1,0:T(8,128)(2,1)S(1)}, bf16[7,128,128]{2,1,0:T(8,128)(2,1)}, u32[]{:S(2)}, u32[]{:S(2)}) collective-permute-start(bf16[7,128,128]{2,1,0:T(8,128)(2,1)S(1)} %collective-permute-done.62.refs_30_), channel_id=1, source_target_pairs={{0,4},{4,0},{8,12},{12,8},{16,20},{20,16},{24,28},{28,24},{1,5},{5... | collective-permute-start | bytes 688136 | tf_op jit(solution)/shard_map/ppermute | solution.py:32
  279.3 21.3 %collective-permute-start.67 = (bf16[7,128,128]{2,1,0:T(8,128)(2,1)}, bf16[7,128,128]{2,1,0:T(8,128)(2,1)S(1)}, u32[]{:S(2)}, u32[]{:S(2)}) collective-permute-start(bf16[7,128,128]{2,1,0:T(8,128)(2,1)} %get-tuple-element.51.refs_0_), channel_id=1, source_target_pairs={{0,16},{4,20},{8,24},{12,28},{16,0},{20,4},{24,8},{28,12},{1,17},{... | collective-permute-start | bytes 688136 | tf_op jit(solution)/shard_map/ppermute | solution.py:32
  280.0 23.8 %collective-permute-start.65 = (bf16[7,128,128]{2,1,0:T(8,128)(2,1)}, bf16[7,128,128]{2,1,0:T(8,128)(2,1)S(1)}, u32[]{:S(2)}, u32[]{:S(2)}) collective-permute-start(bf16[7,128,128]{2,1,0:T(8,128)(2,1)} %get-tuple-element.51.refs_0_), channel_id=1, source_target_pairs={{0,8},{4,12},{8,0},{12,4},{16,24},{20,28},{24,16},{28,20},{1,9},{5... | collective-permute-start | bytes 688136 | tf_op jit(solution)/shard_map/ppermute | solution.py:32
  280.5 37.3 %collective-permute-start.64 = (bf16[7,128,128]{2,1,0:T(8,128)(2,1)}, bf16[7,128,128]{2,1,0:T(8,128)(2,1)S(1)}, u32[]{:S(2)}, u32[]{:S(2)}) collective-permute-start(bf16[7,128,128]{2,1,0:T(8,128)(2,1)} %get-tuple-element.51.refs_0_), channel_id=1, source_target_pairs={{0,4},{4,0},{8,12},{12,8},{16,20},{20,16},{24,28},{28,24},{1,5},{5... | collective-permute-start | bytes 688136 | tf_op jit(solution)/shard_map/ppermute | solution.py:32
  282.4 27.7 %collective-permute-start.101 = (f32[3]{0:T(128)S(1)}, f32[3]{0:T(128)S(1)}, u32[]{:S(2)}, u32[]{:S(2)}) collective-permute-start(f32[3]{0:T(128)S(1)} %slice_reduce_fusion), channel_id=1, source_target_pairs={{0,4},{4,0},{8,12},{12,8},{16,20},{20,16},{24,28},{28,24},{1,5},{5... | collective-permute-start | bytes 44 | tf_op jit(solution)/shard_map/ppermute | solution.py:32
  303.0 14.9 %collective-permute-start.68 = (bf16[7,128,128]{2,1,0:T(8,128)(2,1)S(1)}, bf16[7,128,128]{2,1,0:T(8,128)(2,1)S(1)}, u32[]{:S(2)}, u32[]{:S(2)}) collective-permute-start(bf16[7,128,128]{2,1,0:T(8,128)(2,1)S(1)} %collective-permute-done.67.refs_4_), channel_id=1, source_target_pairs={{0,4},{4,0},{8,12},{12,8},{16,20},{20,16},{24,28},{28,24},{1,5},{5... | collective-permute-start | bytes 688136 | tf_op jit(solution)/shard_map/ppermute | solution.py:32
  303.8 14.1 %collective-permute-start.66 = (bf16[7,128,128]{2,1,0:T(8,128)(2,1)S(1)}, bf16[7,128,128]{2,1,0:T(8,128)(2,1)S(1)}, u32[]{:S(2)}, u32[]{:S(2)}) collective-permute-start(bf16[7,128,128]{2,1,0:T(8,128)(2,1)S(1)} %collective-permute-done.65.refs_2_), channel_id=1, source_target_pairs={{0,4},{4,0},{8,12},{12,8},{16,20},{20,16},{24,28},{28,24},{1,5},{5... | collective-permute-start | bytes 688136 | tf_op jit(solution)/shard_map/ppermute | solution.py:32
  307.2 10.7 %collective-permute-start.70 = (bf16[7,128,128]{2,1,0:T(8,128)(2,1)S(1)}, bf16[7,128,128]{2,1,0:T(8,128)(2,1)S(1)}, u32[]{:S(2)}, u32[]{:S(2)}) collective-permute-start(bf16[7,128,128]{2,1,0:T(8,128)(2,1)S(1)} %collective-permute-done.69.refs_6_), channel_id=1, source_target_pairs={{0,4},{4,0},{8,12},{12,8},{16,20},{20,16},{24,28},{28,24},{1,5},{5... | collective-permute-start | bytes 688136 | tf_op jit(solution)/shard_map/ppermute | solution.py:32
  315.0 113.1 %collective-permute-start.95 = (bf16[2,2,384,768]{3,2,1,0:T(8,128)(2,1)}, bf16[2,2,384,768]{3,2,1,0:T(8,128)(2,1)}, u32[]{:S(2)}, u32[]{:S(2)}) collective-permute-start(bf16[2,2,384,768]{3,2,1,0:T(8,128)(2,1)} %dynamic-slice_bitcast_fusion), channel_id=1, source_target_pairs={{0,4},{4,0},{8,12},{12,8},{16,20},{20,16},{24,28},{28,24},{1,5},{5... | collective-permute-start | bytes 7077896 | tf_op jit(solution)/shard_map/ppermute | solution.py:32
  317.9 113.4 %collective-permute-start.89 = (bf16[2,2,96,3072]{3,2,1,0:T(8,128)(2,1)}, bf16[2,2,96,3072]{3,2,1,0:T(8,128)(2,1)}, u32[]{:S(2)}, u32[]{:S(2)}) collective-permute-start(bf16[2,2,96,3072]{3,2,1,0:T(8,128)(2,1)} %dynamic-slice_bitcast_fusion.1), channel_id=1, source_target_pairs={{0,4},{4,0},{8,12},{12,8},{16,20},{20,16},{24,28},{28,24},{1,5},{5... | collective-permute-start | bytes 7077896 | tf_op jit(solution)/shard_map/ppermute | solution.py:32
  388.5 11.0 %collective-permute-start.83 = (bf16[2,2,96,1280]{3,2,1,0:T(8,128)(2,1)S(1)}, bf16[2,2,96,1280]{3,2,1,0:T(8,128)(2,1)S(1)}, u32[]{:S(2)}, u32[]{:S(2)}) collective-permute-start(bf16[2,2,96,1280]{3,2,1,0:T(8,128)(2,1)S(1)} %dynamic-slice_bitcast_fusion.4), channel_id=1, source_target_pairs={{0,4},{4,0},{8,12},{12,8},{16,20},{20,16},{24,28},{28,24},{1,5},{5... | collective-permute-start | bytes 2949128 | tf_op jit(solution)/shard_map/ppermute | solution.py:32
  389.1 9.5 %collective-permute-start.72 = (bf16[2,96,896]{2,1,0:T(8,128)(2,1)S(1)}, bf16[2,96,896]{2,1,0:T(8,128)(2,1)S(1)}, u32[]{:S(2)}, u32[]{:S(2)}) collective-permute-start(bf16[2,96,896]{2,1,0:T(8,128)(2,1)S(1)} %dynamic-slice_bitcast_fusion.11), channel_id=1, source_target_pairs={{0,8},{4,12},{8,0},{12,4},{16,24},{20,28},{24,16},{28,20},{1,9},{5... | collective-permute-start | bytes 1032200 | tf_op jit(solution)/shard_map/ppermute | solution.py:32
  407.3 9.4 %collective-permute-start.78 = (bf16[2,96,1152]{2,1,0:T(8,128)(2,1)S(1)}, bf16[2,96,1152]{2,1,0:T(8,128)(2,1)}, u32[]{:S(2)}, u32[]{:S(2)}) collective-permute-start(bf16[2,96,1152]{2,1,0:T(8,128)(2,1)S(1)} %dynamic-slice_bitcast_fusion.10), channel_id=1, source_target_pairs={{0,8},{4,12},{8,0},{12,4},{16,24},{20,28},{24,16},{28,20},{1,9},{5... | collective-permute-start | bytes 1327112 | tf_op jit(solution)/shard_map/ppermute | solution.py:32
  409.9 9.6 %collective-permute-start.84 = (bf16[2,96,1280]{2,1,0:T(8,128)(2,1)S(1)}, bf16[2,96,1280]{2,1,0:T(8,128)(2,1)S(1)}, u32[]{:S(2)}, u32[]{:S(2)}) collective-permute-start(bf16[2,96,1280]{2,1,0:T(8,128)(2,1)S(1)} %dynamic-slice_bitcast_fusion.9), channel_id=1, source_target_pairs={{0,16},{4,20},{8,24},{12,28},{16,0},{20,4},{24,8},{28,12},{1,17},{... | collective-permute-start | bytes 1474568 | tf_op jit(solution)/shard_map/ppermute | solution.py:32
  419.6 15.0 %collective-permute-start.85 = (bf16[96,1280]{1,0:T(8,128)(2,1)S(1)}, bf16[96,1280]{1,0:T(8,128)(2,1)S(1)}, u32[]{:S(2)}, u32[]{:S(2)}) collective-permute-start(bf16[96,1280]{1,0:T(8,128)(2,1)S(1)} %dynamic-slice_bitcast_fusion.12), channel_id=1, source_target_pairs={{0,8},{4,12},{8,0},{12,4},{16,24},{20,28},{24,16},{28,20},{1,9},{5... | collective-permute-start | bytes 737288 | tf_op jit(solution)/shard_map/ppermute | solution.py:32
  425.4 10.1 %collective-permute-start.80 = (bf16[24,1152]{1,0:T(8,128)(2,1)S(1)}, bf16[24,1152]{1,0:T(8,128)(2,1)S(1)}, u32[]{:S(2)}, u32[]{:S(2)}) collective-permute-start(bf16[24,1152]{1,0:T(8,128)(2,1)S(1)} %get-tuple-element.103), channel_id=1, source_target_pairs={{0,1},{1,2},{2,3},{3,0},{4,5},{5,6},{6,7},{7,4},{8,9},{9,10},{10,1... | collective-permute-start | bytes 165896 | tf_op jit(solution)/shard_map/ppermute | solution.py:80
  425.5 11.8 %collective-permute-start.81 = (bf16[24,1152]{1,0:T(8,128)(2,1)S(1)}, bf16[24,1152]{1,0:T(8,128)(2,1)S(1)}, u32[]{:S(2)}, u32[]{:S(2)}) collective-permute-start(bf16[24,1152]{1,0:T(8,128)(2,1)S(1)} %get-tuple-element.105), channel_id=1, source_target_pairs={{0,2},{1,3},{2,0},{3,1},{4,6},{5,7},{6,4},{7,5},{8,10},{9,11},{10,... | collective-permute-start | bytes 165896 | tf_op jit(solution)/shard_map/ppermute | solution.py:80
  428.1 10.8 %collective-permute-start.82 = (bf16[24,1152]{1,0:T(8,128)(2,1)S(1)}, bf16[24,1152]{1,0:T(8,128)(2,1)S(1)}, u32[]{:S(2)}, u32[]{:S(2)}) collective-permute-start(bf16[24,1152]{1,0:T(8,128)(2,1)S(1)} %get-tuple-element.104), channel_id=1, source_target_pairs={{0,3},{1,0},{2,1},{3,2},{4,7},{5,4},{6,5},{7,6},{8,11},{9,8},{10,9... | collective-permute-start | bytes 165896 | tf_op jit(solution)/shard_map/ppermute | solution.py:80
  431.3 23.4 %collective-permute-start.96 = (bf16[2,384,768]{2,1,0:T(8,128)(2,1)S(1)}, bf16[2,384,768]{2,1,0:T(8,128)(2,1)S(1)}, u32[]{:S(2)}, u32[]{:S(2)}) collective-permute-start(bf16[2,384,768]{2,1,0:T(8,128)(2,1)S(1)} %dynamic-slice_bitcast_fusion.2), channel_id=1, source_target_pairs={{0,8},{4,12},{8,0},{12,4},{16,24},{20,28},{24,16},{28,20},{1,9},{5... | collective-permute-start | bytes 3538952 | tf_op jit(solution)/shard_map/ppermute | solution.py:32
  434.7 22.8 %collective-permute-start.90 = (bf16[2,96,3072]{2,1,0:T(8,128)(2,1)S(1)}, bf16[2,96,3072]{2,1,0:T(8,128)(2,1)S(1)}, u32[]{:S(2)}, u32[]{:S(2)}) collective-permute-start(bf16[2,96,3072]{2,1,0:T(8,128)(2,1)S(1)} %dynamic-slice_bitcast_fusion.3), channel_id=1, source_target_pairs={{0,16},{4,20},{8,24},{12,28},{16,0},{20,4},{24,8},{28,12},{1,17},{... | collective-permute-start | bytes 3538952 | tf_op jit(solution)/shard_map/ppermute | solution.py:32
  455.1 15.4 %collective-permute-start.97 = (bf16[384,768]{1,0:T(8,128)(2,1)S(1)}, bf16[384,768]{1,0:T(8,128)(2,1)S(1)}, u32[]{:S(2)}, u32[]{:S(2)}) collective-permute-start(bf16[384,768]{1,0:T(8,128)(2,1)S(1)} %dynamic-slice_bitcast_fusion.7), channel_id=1, source_target_pairs={{0,16},{4,20},{8,24},{12,28},{16,0},{20,4},{24,8},{28,12},{1,17},{... | collective-permute-start | bytes 1769480 | tf_op jit(solution)/shard_map/ppermute | solution.py:32
  457.9 17.7 %collective-permute-start.91 = (bf16[96,3072]{1,0:T(8,128)(2,1)S(1)}, bf16[96,3072]{1,0:T(8,128)(2,1)S(1)}, u32[]{:S(2)}, u32[]{:S(2)}) collective-permute-start(bf16[96,3072]{1,0:T(8,128)(2,1)S(1)} %dynamic-slice_bitcast_fusion.8), channel_id=1, source_target_pairs={{0,8},{4,12},{8,0},{12,4},{16,24},{20,28},{24,16},{28,20},{1,9},{5... | collective-permute-start | bytes 1769480 | tf_op jit(solution)/shard_map/ppermute | solution.py:32
  475.8 13.5 %collective-permute-start.92 = (bf16[24,3072]{1,0:T(8,128)(2,1)S(1)}, bf16[24,3072]{1,0:T(8,128)(2,1)S(1)}, u32[]{:S(2)}, u32[]{:S(2)}) collective-permute-start(bf16[24,3072]{1,0:T(8,128)(2,1)S(1)} %get-tuple-element.97), channel_id=1, source_target_pairs={{0,1},{1,2},{2,3},{3,0},{4,5},{5,6},{6,7},{7,4},{8,9},{9,10},{10,1... | collective-permute-start | bytes 442376 | tf_op jit(solution)/shard_map/ppermute | solution.py:80
  475.9 19.8 %collective-permute-start.93 = (bf16[24,3072]{1,0:T(8,128)(2,1)S(1)}, bf16[24,3072]{1,0:T(8,128)(2,1)S(1)}, u32[]{:S(2)}, u32[]{:S(2)}) collective-permute-start(bf16[24,3072]{1,0:T(8,128)(2,1)S(1)} %get-tuple-element.99), channel_id=1, source_target_pairs={{0,2},{1,3},{2,0},{3,1},{4,6},{5,7},{6,4},{7,5},{8,10},{9,11},{10,... | collective-permute-start | bytes 442376 | tf_op jit(solution)/shard_map/ppermute | solution.py:80
  477.0 19.8 %collective-permute-start.94 = (bf16[24,3072]{1,0:T(8,128)(2,1)S(1)}, bf16[24,3072]{1,0:T(8,128)(2,1)S(1)}, u32[]{:S(2)}, u32[]{:S(2)}) collective-permute-start(bf16[24,3072]{1,0:T(8,128)(2,1)S(1)} %get-tuple-element.98), channel_id=1, source_target_pairs={{0,3},{1,0},{2,1},{3,2},{4,7},{5,4},{6,5},{7,6},{8,11},{9,8},{10,9... | collective-permute-start | bytes 442376 | tf_op jit(solution)/shard_map/ppermute | solution.py:80
  (116 other events, 1835.5 us)

commit v2 on v1

--- a/solution.py
+++ b/solution.py
@@ -32,11 +32,19 @@
     return lax.ppermute(arr, "seq", [(i, i ^ mask) for i in range(size)])
 
 
-def stream_rows(shard, depth):
-    pieces = [shard] + [
+def after(arr, *deps):
+    return lax.optimization_barrier((arr,) + deps)[0]
+
+
+def stream_send(shard, depth):
+    return [shard] + [
         lax.ppermute(shard, "stream", [(i, (i + d) % depth) for i in range(depth)])
         for d in range(1, depth)
     ]
+
+
+def stream_rows(pieces, depth):
+    shard = pieces[0]
     ring = pieces[::-1]
     place = lax.axis_index("stream")
     rows = shard.shape[0]
@@ -44,43 +52,108 @@
     return lax.dynamic_slice_in_dim(both, (depth - 1 - place) * rows, depth * rows, 0)
 
 
-def seq_blocks(block, size, flip):
-    bits = [1 << b for b in range(1, size.bit_length() - 1)]
-    if flip:
-        bits = bits[::-1]
-    found = {0: block}
-    for bit in bits:
-        for r in list(found):
-            found[r ^ bit] = xor_send(found[r], size, bit)
-    for r in list(found):
-        found[r ^ 1] = xor_send(found[r], size, 1)
-    return [found[r] for r in range(size)]
-
-
-def to_owner(grad, size, depth, flip):
-    nbits = size.bit_length() - 1
-    place = lax.axis_index("seq")
-    rest = list(range(nbits))[::-1]
-    cols = grad.shape[1]
-    cur = grad.reshape([2] * nbits + [grad.shape[0] // size, cols])
-    order = [0] + (list(range(1, nbits))[::-1] if flip else list(range(1, nbits)))
-    for bit in order:
-        axis = rest.index(bit)
+class Spread:
+    def __init__(self, block, size, flip):
+        self.size = size
+        bits = [1 << b for b in range(1, size.bit_length() - 1)]
+        self.bits = bits[::-1] if flip else bits
+        self.block = block
+        self.found = {0: block}
+
+    def near(self, *deps):
+        block = after(self.block, *deps) if deps else self.block
+        for bit in self.bits:
+            self.found[bit] = xor_send(block, self.size, bit)
+        return self
+
+    def far(self, *deps):
+        for bit in self.bits:
+            for r in list(self.found):
+                if r ^ bit not in self.found and r < 2 * max(self.bits):
+                    src = self.found[r]
+                    self.found[r ^ bit] = xor_send(after(src, *deps) if deps else src, self.size, bit)
+        return self
+
+    def far_halves(self):
+        one, two = self.bits[:2]
+        half = self.block.shape[1] // 2
+        self.cuts = [self.found[one][:, :half], self.found[two][:, half:]]
+        left = xor_send(self.cuts[0], self.size, two)
+        right = xor_send(self.cuts[1], self.size, one)
+        self.found[one ^ two] = jnp.concatenate([left, right], axis=1)
+        return self.far()
+
+    def cores(self, *deps):
+        parts = [self.found[2 * r] for r in range(self.size // 2)]
+        stack = jnp.stack(parts)
+        if deps:
+            stack = after(stack, *deps)
+        return [stack, xor_send(stack, self.size, 1)]
+
+
+def beside(parts):
+    return parts[0] if len(parts) == 1 else jnp.concatenate(parts, axis=-1)
+
+
+class Reduce:
+    def __init__(self, grads, size, depth, order=None, rest=None):
+        self.size, self.depth = size, depth
+        nbits = size.bit_length() - 1
+        self.rest = list(range(nbits))[::-1] if rest is None else list(rest)
+        self.order = list(range(nbits)) if order is None else list(order)
+        self.cur = [
+            g.reshape([2] * len(self.rest) + [g.shape[0] // 2 ** len(self.rest), g.shape[1]])
+            if g.ndim == 2
+            else g
+            for g in grads
+        ]
+
+    def send(self):
+        place = lax.axis_index("seq")
+        bit = self.order.pop(0)
+        axis = self.rest.index(bit)
         own = (place >> bit) & 1
-        send = lax.dynamic_index_in_dim(cur, 1 - own, axis, False)
-        keep = lax.dynamic_index_in_dim(cur, own, axis, False)
-        got = xor_send(send, size, 1 << bit)
-        cur = (keep.astype(f32) + got.astype(f32)).astype(bf16)
-        rest.pop(axis)
-    level = lax.axis_index("stream")
-    cur = cur.reshape(depth, cur.shape[0] // depth, cols)
-    total = lax.dynamic_index_in_dim(cur, level, 0, False).astype(f32)
-    for d in range(1, depth):
-        piece = lax.dynamic_index_in_dim(cur, (level + d) % depth, 0, False)
-        total = total + lax.ppermute(
-            piece, "stream", [(i, (i + d) % depth) for i in range(depth)]
-        ).astype(f32)
-    return total
+        self.out = beside([lax.dynamic_index_in_dim(c, 1 - own, axis, False) for c in self.cur])
+        self.kept = [lax.dynamic_index_in_dim(c, own, axis, False) for c in self.cur]
+        self.flight = xor_send(self.out, self.size, 1 << bit)
+        self.rest.pop(axis)
+        return self
+
+    def add(self, *deps):
+        got = after(self.flight, *deps) if deps else self.flight
+        self.cur = [(beside(self.kept).astype(f32) + got.astype(f32)).astype(bf16)]
+        return self
+
+    def cut(self, at):
+        (cur,) = self.cur
+        parts = [
+            Reduce([cur[..., :at]], self.size, self.depth, self.order, self.rest),
+            Reduce([cur[..., at:]], self.size, self.depth, self.order[::-1], self.rest),
+        ]
+        return parts
+
+    def send_stream(self):
+        while self.order:
+            self.send().add()
+        depth = self.depth
+        level = lax.axis_index("stream")
+        cur = beside(self.cur)
+        self.out = cur
+        cur = cur.reshape(depth, cur.shape[0] // depth, cur.shape[1])
+        self.total = lax.dynamic_index_in_dim(cur, level, 0, False).astype(f32)
+        self.flights = []
+        for d in range(1, depth):
+            piece = lax.dynamic_index_in_dim(cur, (level + d) % depth, 0, False)
+            self.flights.append(
+                lax.ppermute(piece, "stream", [(i, (i + d) % depth) for i in range(depth)])
+            )
+        return self
+
+    def done(self, *deps):
+        total = self.total
+        for f in self.flights:
+            total = total + (after(f, *deps) if deps else f).astype(f32)
+        return total
 
 
 def lanes(shape):
@@ -93,15 +166,21 @@
     return jnp.where(r == c, 1.0, 0.0).astype(bf16)
 
 
-def fetch_start(blocks, dest, me, sems, col=0, width=None):
-    rows = dest.shape[0] // len(blocks)
+def fetch_start(stacks, dest, me, sems, col=0, width=None, at=0):
+    half = stacks[0].shape[0]
+    rows = dest.shape[0] // (2 * half)
+    width = width or stacks[0].shape[2]
     copies = []
-    for r, ref in enumerate(blocks):
-        off = pl.multiple_of((me ^ r) * rows, 8)
-        src = ref if width is None else ref.at[:, pl.ds(col, width)]
-        copy = pltpu.make_async_copy(src, dest.at[pl.ds(off, rows), :], sems.at[r])
-        copy.start()
-        copies.append(copy)
+    for c, ref in enumerate(stacks):
+        for r in range(half):
+            off = pl.multiple_of((me ^ (2 * r + c)) * rows, 8)
+            copy = pltpu.make_async_copy(
+                ref.at[r, :, pl.ds(col, width)],
+                dest.at[pl.ds(off, rows), pl.ds(at, width)],
+                sems.at[2 * r + c],
+            )
+            copy.start()
+            copies.append(copy)
     return copies
 
 
@@ -157,28 +236,38 @@
     dest[pairs] = zt.astype(bf16)
 
 
-def unpack_states(coef_ref, blocks, put, pairs, split):
+def unpack_states(me, keep_ref, blocks, put, base, count, pairs, back):
     shape = (128, 128)
     lane = lanes(shape)
     low = lane < 64
+    size = 2 * blocks.shape[1]
+    coefs = [None]
+    for r in range(1, size):
+        j = me ^ r
+        c = jnp.where(j > me if back else j < me, 1.0, 0.0)
+        for i in range(size):
+            between = ((i > me) & (i < j)) if back else ((i > j) & (i < me))
+            c = c * jnp.where(between, keep_ref[i], 1.0)
+        coefs.append(c)
 
     def total(i):
         acc = jnp.zeros(shape, f32)
-        for r in range(1, len(blocks)):
-            acc = acc + coef_ref[r] * blocks[r][i].astype(f32)
+        for r in range(1, size):
+            acc = acc + coefs[r] * blocks[r % 2, r // 2, i].astype(f32)
         return acc
 
     zt = total(pairs)
-    for p in range(pairs):
+    for q in range(count):
+        p = base + q
         two = total(p)
         za = jnp.sum(jnp.where(lane == 64 + 2 * p, zt, 0.0), axis=1, keepdims=True)
         zb = jnp.sum(jnp.where(lane == 2 * p + 1, zt, 0.0), axis=1, keepdims=True)
-        if split:
-            put(2 * p, jnp.where(low, two, jnp.where(lane == 64, za, 0.0)))
-            put(2 * p + 1, jnp.where(low, jnp.where(lane == 0, zb, 0.0), two))
+        if back:
+            put(2 * q, jnp.where(low, two, jnp.where(lane == 64, za, 0.0)))
+            put(2 * q + 1, jnp.where(low, jnp.where(lane == 0, zb, 0.0), two))
         else:
-            put(2 * p, jnp.where(low, two, za))
-            put(2 * p + 1, jnp.where(low, zb, two))
+            put(2 * q, jnp.where(low, two, za))
+            put(2 * q + 1, jnp.where(low, zb, two))
 
 
 def normed(values, gain, bias):
@@ -200,19 +289,19 @@
 
 def keys_body(n_seq, pairs, me_ref, cend_ref, x_ref, cnt_ref, *refs):
     width = x_ref.shape[1]
-    wa, wb = refs[:n_seq], refs[n_seq : 2 * n_seq]
-    (h_ref, k_ref, v_ref, phi_ref, st_ref, gb_ref, w1, w2, maps, state, sems) = refs[2 * n_seq :]
+    wl = refs[:2]
+    (h_ref, k_ref, v_ref, phi_ref, st_ref, gb_ref, feat_ref, w1, maps, state, sems) = refs[2:]
     step = pl.program_id(0)
 
     @pl.when(step == 0)
     def _():
         me = me_ref[0]
-        copies = fetch_start(wa, w1, me, sems.at[0])
-        copies += fetch_start(wb, w2, me, sems.at[1])
+        copies = fetch_start(wl, w1, me, sems.at[0], width, 2 * width + 256)
         for c in copies:
             c.wait()
-        gb_ref[...] = w1[:, pl.ds(width + 128, 128)].astype(f32).T[:8]
-        pair_maps(w1.at[:, pl.ds(width, 128)], maps, pairs, 1)
+        gb_ref[...] = w1[:, pl.ds(2 * width + 128, 128)].astype(f32).T[:8]
+        feat_ref[...] = w1[:, pl.ds(2 * width, 128)]
+        pair_maps(feat_ref, maps, pairs, 1)
         state[...] = jnp.zeros_like(state)
 
     gb = gb_ref[...]
@@ -220,7 +309,7 @@
     h1 = out.astype(bf16)
     h_ref[...] = h1
     keys = mm(h1, w1[:, pl.ds(0, width)]).astype(bf16)
-    vals = mm(h1, w2[...]).astype(bf16)
+    vals = mm(h1, w1[:, pl.ds(width, width)]).astype(bf16)
     k_ref[...] = keys
     v_ref[...] = vals
     ones = block_ones(256, 64)
@@ -239,25 +328,29 @@
         pack_states(lambda h: state[h], st_ref, pairs, False)
 
 
-def local_body(n_seq, pairs, me_ref, cend_ref, h_ref, phik_ref, v_ref, cnt_ref, row_ref, feat_ref, *refs):
-    wq = refs[:n_seq]
-    (q_ref, phiq_ref, num_ref, den_ref, srel_ref, w1, maps, state, sems) = refs[n_seq:]
+def local_body(base, pairs, me_ref, cend_ref, h_ref, phik_ref, v_ref, cnt_ref, row_ref, feat_ref, *refs):
+    wq = refs[:2]
+    (q_ref, phiq_ref, num_ref, den_ref, srel_ref, state, w1, maps, sems) = refs[-9:]
     step = pl.program_id(0)
     width = h_ref.shape[1]
 
     @pl.when(step == 0)
     def _():
-        for c in fetch_start(wq, w1, me_ref[0], sems, 0, width):
+        copies = fetch_start(wq, w1, me_ref[0], sems, 0, width)
+        pair_maps(feat_ref, maps, pairs, 0)
+        if base:
+            state[...] = refs[2][...]
+        else:
+            state[...] = jnp.zeros_like(state)
+        for c in copies:
             c.wait()
-        pair_maps(feat_ref, maps, pairs, 0)
-        state[...] = jnp.zeros_like(state)
 
     queries = mm(h_ref[...], w1[...]).astype(bf16)
     q_ref[...] = queries
     ones = block_ones(256, 64)
     size = h_ref.shape[0]
     cnt = cnt_ref[...]
-    first, last = cend_ref[step], cend_ref[step + 1]
+    first, last = cend_ref[base + step], cend_ref[base + step + 1]
     row_id = lax.broadcasted_iota(jnp.int32, (size, size), 0)
     mask = (row_id >= lanes((size, size))) & (cnt == row_ref[...])
     before = jnp.where(cnt == first, 1.0, 0.0)
@@ -284,28 +377,28 @@
 
 
 def middle_body(
-    n_seq, pairs, me_ref, coef_ref, x_ref, dy_ref, num_ref, den_ref, phiq_ref, cnt_ref, gb_ref, *refs
+    n_seq, pairs, me_ref, keep_ref, x_ref, dy_ref, num_ref, den_ref, phiq_ref, cnt_ref, gb_ref, *refs
 ):
     width = x_ref.shape[1]
-    wo, wf, wp, sts = (refs[i * n_seq : (i + 1) * n_seq] for i in range(4))
+    wf, wp, sts = (refs[2 * i : 2 * i + 2] for i in range(3))
     (
         y_ref, o_ref, h_ref, a_ref, df_ref, dat_ref, dr_ref, dd_ref, sin_ref, gst_ref, sum_ref,
         w_out, w_fc, w_proj, rden, state, stv, sems,
-    ) = refs[4 * n_seq :]
+    ) = refs[6:]
     step = pl.program_id(0)
     chunk = 768
+    hidden = w_fc.shape[1]
     size = x_ref.shape[0]
 
     @pl.when(step == 0)
     def _():
         me = me_ref[0]
         st_copies = []
-        for r in range(1, n_seq):
-            c = pltpu.make_async_copy(sts[r], stv.at[r], sems.at[3, r])
-            c.start()
-            st_copies.append(c)
-        copies = fetch_start(wo, w_out, me, sems.at[0], width, width)
-        copies += fetch_start(wf, w_fc, me, sems.at[1])
+        for c in range(2):
+            st_copies.append(pltpu.make_async_copy(sts[c], stv.at[c], sems.at[3, c]))
+            st_copies[c].start()
+        copies = fetch_start(wf, w_out, me, sems.at[0], hidden, width)
+        copies += fetch_start(wf, w_fc, me, sems.at[1], 0, hidden)
         copies += fetch_start(wp, w_proj, me, sems.at[2])
         for c in st_copies:
             c.wait()
@@ -313,7 +406,7 @@
         def put(h, value):
             sin_ref[h] = value.astype(bf16)
 
-        unpack_states(coef_ref, [stv.at[r] for r in range(n_seq)], put, pairs, False)
+        unpack_states(me, keep_ref, stv, put, 0, pairs, pairs, False)
         state[...] = jnp.zeros_like(state)
         sum_ref[...] = jnp.zeros_like(sum_ref)
         for c in copies:
@@ -397,11 +490,11 @@
 
 
 def back_body(
-    n_seq, pairs, coef_ref, cend_ref, q_ref, k_ref, v_ref, phiq_ref, phik_ref, dd_ref, srel_ref, sin_ref,
+    base, pairs, all_pairs, me_ref, keep_ref, cend_ref, q_ref, k_ref, v_ref, phiq_ref, phik_ref, dd_ref, srel_ref, sin_ref,
     cnt_ref, row_ref, feat_ref, *refs
 ):
-    sts = refs[:n_seq]
-    (dqkv_ref, gfeat_ref, mapq, mapk, state, gq, gk, stv, sems) = refs[n_seq:]
+    sts = refs[:2]
+    (dqkv_ref, gfeat_ref, mapq, mapk, state, gq, gk, stv, sems) = refs[2:]
     step = pl.program_id(0)
     nblk = pl.num_programs(0)
     here = nblk - 1 - step
@@ -409,10 +502,9 @@
     @pl.when(step == 0)
     def _():
         copies = []
-        for r in range(1, n_seq):
-            c = pltpu.make_async_copy(sts[r], stv.at[r], sems.at[r])
-            c.start()
-            copies.append(c)
+        for c in range(2):
+            copies.append(pltpu.make_async_copy(sts[c], stv.at[c], sems.at[c]))
+            copies[c].start()
         pair_maps(feat_ref, mapq, pairs, 0)
         pair_maps(feat_ref, mapk, pairs, 1)
         gq[...] = jnp.zeros_like(gq)
@@ -423,7 +515,7 @@
         def put(h, value):
             state[h] = value
 
-        unpack_states(coef_ref, [stv.at[r] for r in range(n_seq)], put, pairs, True)
+        unpack_states(me_ref[0], keep_ref, stv, put, base, pairs, all_pairs, True)
 
     size = q_ref.shape[0]
     width = q_ref.shape[1]
@@ -482,28 +574,27 @@
             gfeat_ref[pl.ds(p * 128, 128), :] = jnp.where(lane < 64, outs[0], -outs[1]).astype(bf16)
 
 
-def enter_body(n_seq, me_ref, x_ref, dr_ref, dqkv_ref, gb_ref, *refs):
+def enter_body(groups, me_ref, x_ref, dr_ref, gb_ref, *refs):
     width = x_ref.shape[1]
-    wq, wk, wv = (refs[i * n_seq : (i + 1) * n_seq] for i in range(3))
-    (dx_ref, sum_ref, w1, w2, w3, sems) = refs[3 * n_seq :]
+    grads = refs[:groups]
+    wl = refs[groups : groups + 2]
+    (dx_ref, sum_ref, w1, sems) = refs[groups + 2 :]
 
     @pl.when(pl.program_id(0) == 0)
     def _():
         me = me_ref[0]
-        copies = fetch_start(wq, w1, me, sems.at[0], 0, width)
-        copies += fetch_start(wk, w2, me, sems.at[1], 0, width)
-        copies += fetch_start(wv, w3, me, sems.at[2])
+        copies = fetch_start(wl, w1, me, sems.at[0], 0, 3 * width)
         sum_ref[...] = jnp.zeros_like(sum_ref)
         for c in copies:
             c.wait()
 
     gb = gb_ref[...]
     _, hat, rstd = normed(x_ref[...].astype(f32), gb[0:1], gb[2:3])
-    dh = (
-        mm_t(dqkv_ref[:, pl.ds(0, width)], w1[...])
-        + mm_t(dqkv_ref[:, pl.ds(width, width)], w2[...])
-        + mm_t(dqkv_ref[:, pl.ds(2 * width, width)], w3[...])
-    )
+    part = width // groups
+    dh = jnp.zeros(x_ref.shape, f32)
+    for g in range(groups):
+        for i in range(3):
+            dh = dh + mm_t(grads[g][:, pl.ds(i * part, part)], w1[:, pl.ds(i * width + g * part, part)])
     dx_ref[...] = dr_ref[...] + normed_back(dh, hat, rstd, gb[0:1])
     sum_ref[0:1] += jnp.sum(dh * hat, axis=0, keepdims=True)
     sum_ref[1:2] += jnp.sum(dh, axis=0, keepdims=True)
@@ -535,6 +626,12 @@
 def cparams():
     return pltpu.CompilerParams(
         dimension_semantics=("arbitrary",), vmem_limit_bytes=58 * 1024 * 1024
+    )
+
+
+def cost(micros):
+    return pl.CostEstimate(
+        flops=int(micros * 5e8), transcendentals=0, bytes_accessed=int(micros * 1e6)
     )
 
 
@@ -554,19 +651,8 @@
     me = lax.axis_index("seq")
     me_arr = me.reshape(1).astype(jnp.int32)
 
-    norms = jnp.concatenate(
-        [norm_gains, norm_biases, jnp.zeros((rows, 124), bf16)], axis=1
-    )
-    first = jnp.concatenate([w_qkv[:, width : 2 * width], w_feat, norms], axis=1)
-    values_w = w_qkv[:, 2 * width :]
-    second = jnp.concatenate([w_qkv[:, :width], w_out], axis=1)
-    keys_blocks = seq_blocks(stream_rows(first, depth), n_seq, False)
-    vals_blocks = seq_blocks(stream_rows(values_w, depth), n_seq, True)
-    second_blocks = seq_blocks(stream_rows(second, depth), n_seq, False)
-    fc_blocks = seq_blocks(stream_rows(w_fc, depth), n_seq, True)
-    proj_blocks = seq_blocks(stream_rows(w_proj, depth), n_seq, False)
-
     marks = resets[0].reshape(nblk, BT).astype(bf16)
+    flag = jnp.where(jnp.max(resets) == 0, 1.0, 0.0).astype(bf16)
     upper = jnp.triu(jnp.ones((BT, BT), bf16))
     inner = jnp.dot(marks, upper, preferred_element_type=f32)
     ends = jnp.cumsum(inner[:, -1])
@@ -574,74 +660,111 @@
     counts = inner + cend[:-1, None]
     cnt_col = counts.reshape(tokens, 1)
     cnt_row = counts.reshape(1, tokens)
-    keep_dev = jnp.where(ends[-1] == 0.0, 1.0, 0.0).astype(f32)
-    tile = jnp.full((8, 128), keep_dev, f32)
-    keeps = jnp.stack([xor_send(tile, n_seq, r)[0, 0] if r else keep_dev for r in range(n_seq)])
-    index = jnp.arange(n_seq) ^ me
-    i_abs, j_abs = index[None, :], index[:, None]
-    ahead = jnp.where((i_abs > j_abs) & (i_abs < me), keeps[None, :], 1.0)
-    coef_f = jnp.where(index < me, jnp.prod(ahead, axis=1), 0.0)
-    behind = jnp.where((i_abs < j_abs) & (i_abs > me), keeps[None, :], 1.0)
-    coef_b = jnp.where(index > me, jnp.prod(behind, axis=1), 0.0)
+
+    norms = jnp.concatenate(
+        [norm_gains, norm_biases, jnp.broadcast_to(flag, (rows, 1)), jnp.zeros((rows, 123), bf16)],
+        axis=1,
+    )
+    first = stream_rows(stream_send(jnp.concatenate([w_qkv, w_feat, norms], axis=1), depth), depth)
+    first = Spread(first, n_seq, False).near()
+    up = jnp.concatenate([w_fc, w_out], axis=1)
+    first.far_halves()
+    up = stream_send(after(up, *first.cuts), depth)
+    first_blocks = first.cores()
+    up = stream_rows([after(a, first_blocks[0]) for a in up], depth)
+    up = Spread(up, n_seq, True).near(first_blocks[0])
+    proj_pieces = stream_send(after(w_proj, first_blocks[1], up.block), depth)
+    me_first = after(me_arr, up.block)
 
     packed = (pairs + 1, 128, 128)
     full = (heads, 128, 128)
-    h_one, keys, vals, phi_k, state, gb = pl.pallas_call(
+    h_one, keys, vals, phi_k, state, gb, feat_all = pl.pallas_call(
         functools.partial(keys_body, n_seq, pairs),
         name="keys",
+        cost_estimate=cost(22),
         grid=(tokens // TM,),
-        in_specs=[smem(), smem(), rows_spec(TM, width), rows_spec(TM, 1)] + [whole()] * (2 * n_seq),
+        in_specs=[smem(), smem(), rows_spec(TM, width), rows_spec(TM, 1)] + [whole()] * 2,
         out_specs=[rows_spec(TM, width)] * 3
-        + [rows_spec(TM, 2 * width), full_spec(packed), full_spec((8, width))],
+        + [rows_spec(TM, 2 * width), full_spec(packed), full_spec((8, width)), full_spec((width, 128))],
         out_shape=[sds((tokens, width), bf16)] * 3
-        + [sds((tokens, 2 * width), bf16), sds(packed, bf16), sds((8, width), f32)],
+        + [sds((tokens, 2 * width), bf16), sds(packed, bf16), sds((8, width), f32), sds((width, 128), bf16)],
         scratch_shapes=[
-            pltpu.VMEM((width, width + 256), bf16),
-            pltpu.VMEM((width, width), bf16),
+            pltpu.VMEM((width, 2 * width + 256), bf16),
             pltpu.VMEM((pairs, 128, 256), bf16),
             pltpu.VMEM(full, f32),
             dma(2, n_seq),
         ],
         compiler_params=cparams(),
-    )(me_arr, cend, x, cnt_col, *keys_blocks, *vals_blocks)
-    feat_full = assembled([b[:, width : width + 128] for b in keys_blocks], me)
-    states = seq_blocks(state, n_seq, False)
-
-    queries, phi_q, num, den, srel = pl.pallas_call(
-        functools.partial(local_body, n_seq, pairs),
-        name="local",
-        grid=(nblk,),
-        in_specs=[
-            smem(), smem(), rows_spec(BT, width), rows_spec(BT, 2 * width), rows_spec(BT, width),
-            rows_spec(BT, 1), pl.BlockSpec((1, BT), lambda i: (0, i)), full_spec((width, 128)),
-        ]
-        + [whole()] * n_seq,
-        out_specs=[
-            rows_spec(BT, width), rows_spec(BT, 2 * width), rows_spec(BT, width), rows_spec(BT, width),
-            pl.BlockSpec((1,) + full, lambda i: (i, 0, 0, 0)),
-        ],
-        out_shape=[
+    )(me_first, cend, x, cnt_col, *first_blocks)
+    level = lax.axis_index("stream")
+    flags = gb[4].reshape(n_seq, depth, rows)[:, :, 0]
+    keeps = lax.dynamic_index_in_dim(flags, level, 1, False)
+    spread = Spread(state, n_seq, False)
+    spread.near()
+    up.far(gb)
+    proj = Spread(stream_rows([after(a, gb) for a in proj_pieces], depth), n_seq, False).near()
+    part_blk = nblk // 2
+    local = []
+    for part in range(2):
+        base = part * part_blk
+
+        def here(size, cols):
+            return pl.BlockSpec((size, cols), lambda i: (base + i, 0))
+
+        blocks_out = [
             sds((tokens, width), bf16), sds((tokens, 2 * width), bf16), sds((tokens, width), f32),
             sds((tokens, width), f32), sds((nblk,) + full, bf16),
-        ],
-        scratch_shapes=[
-            pltpu.VMEM((width, width), bf16),
-            pltpu.VMEM((pairs, 128, 256), bf16),
-            pltpu.VMEM(full, f32),
-            dma(n_seq),
-        ],
-        compiler_params=cparams(),
-    )(me_arr, cend, h_one, phi_k, vals, cnt_col, cnt_row, feat_full, *second_blocks)
+        ]
+        if part:
+            me_two = after(me_arr, up_blocks[0], *[proj.found[b] for b in proj.bits], *spread.found.values())
+        else:
+            me_two = after(me_arr, proj.block, state, after(up.found[up.bits[0]], gb))
+        local = pl.pallas_call(
+            functools.partial(local_body, base, pairs),
+            name="local",
+            cost_estimate=cost(19),
+            grid=(part_blk,),
+            in_specs=[
+                smem(), smem(), here(BT, width), here(BT, 2 * width), here(BT, width), here(BT, 1),
+                pl.BlockSpec((1, BT), lambda i: (0, base + i)), full_spec((width, 128)),
+            ]
+            + [whole()] * 2
+            + ([full_spec(full)] + [whole()] * 5 if part else []),
+            out_specs=[
+                here(BT, width), here(BT, 2 * width), here(BT, width), here(BT, width),
+                pl.BlockSpec((1,) + full, lambda i: (base + i, 0, 0, 0)), full_spec(full),
+            ],
+            out_shape=blocks_out + [sds(full, f32)],
+            scratch_shapes=[
+                pltpu.VMEM((width, width), bf16),
+                pltpu.VMEM((pairs, 128, 256), bf16),
+                dma(n_seq),
+            ],
+            input_output_aliases={11 + i: i for i in range(5)} if part else {},
+            compiler_params=cparams(),
+        )(
+            me_two, cend, h_one, phi_k, vals, cnt_col, cnt_row, feat_all, *first_blocks,
+            *([local[5]] + list(local[:5]) if part else []),
+        )
+        if part == 0:
+            event = local[5]
+            proj.far(event)
+            spread.far(event)
+            up_blocks = up.cores(event)
+    queries, phi_q, num, den, srel, event = local
+    proj_blocks = proj.cores(event)
+    states = spread.cores(event)
 
     y, att, h_two, act, d_fc, d_att, d_mid, dd, s_in, g_state, sums = pl.pallas_call(
         functools.partial(middle_body, n_seq, pairs),
         name="middle",
+        cost_estimate=cost(43),
         grid=(tokens // TM,),
         in_specs=[
             smem(), smem(), rows_spec(TM, width), rows_spec(TM, width), rows_spec(TM, width),
             rows_spec(TM, width), rows_spec(TM, 2 * width), rows_spec(TM, 1), full_spec((8, width)),
         ]
-        + [whole()] * (4 * n_seq),
+        + [whole()] * 6,
         out_specs=[
             rows_spec(TM, width), rows_spec(TM, width), rows_spec(TM, width), rows_spec(TM, hidden),
             rows_spec(TM, hidden), rows_spec(TM, width), rows_spec(TM, width), rows_spec(TM, 2 * width),
@@ -659,96 +782,146 @@
             pltpu.VMEM((hidden, width), bf16),
             pltpu.VMEM((TM, width), f32),
             pltpu.VMEM(full, f32),
-            pltpu.VMEM((n_seq,) + packed, bf16),
+            pltpu.VMEM((2, n_seq // 2) + packed, bf16),
             dma(4, n_seq),
         ],
         compiler_params=cparams(),
     )(
-        me_arr, coef_f, x, dy, num, den, phi_q, cnt_col, gb,
-        *second_blocks, *fc_blocks, *proj_blocks, *states,
+        me_arr, keeps, x, dy, num, den, phi_q, cnt_col, gb,
+        *up_blocks, *proj_blocks, *states,
     )
 
-    g_states = seq_blocks(g_state, n_seq, True)
+    spread = Spread(g_state, n_seq, True).near()
     squares = jnp.sum(sums[:3], axis=1)
-    for b in range(n_seq.bit_length() - 1):
-        squares = squares + xor_send(squares, n_seq, 1 << b)
-    branch_rms = jnp.sqrt(squares / (tokens * n_seq * width)).reshape(1, 3)
-
-    grad_proj = to_owner(mm_f(act, dy).astype(bf16), n_seq, depth, False)
-    grad_fc = to_owner(mm_f(h_two, d_fc).astype(bf16), n_seq, depth, True)
-    g_out = mm_f(att, d_att).astype(bf16)
-
-    spec = functools.partial(rows_spec, BT, back=nblk)
-    d_qkv, g_feat = pl.pallas_call(
-        functools.partial(back_body, n_seq, pairs),
-        name="back",
-        grid=(nblk,),
-        in_specs=[
-            smem(), smem(), spec(width), spec(width), spec(width), spec(2 * width), spec(2 * width),
-            spec(2 * width), pl.BlockSpec((1,) + full, lambda i: (nblk - 1 - i, 0, 0, 0)), full_spec(full),
-            spec(1), pl.BlockSpec((1, BT), lambda i: (0, nblk - 1 - i)), full_spec((width, 128)),
-        ]
-        + [whole()] * n_seq,
-        out_specs=[spec(3 * width), full_spec((width, 128))],
-        out_shape=[sds((tokens, 3 * width), bf16), sds((width, 128), bf16)],
-        scratch_shapes=[
-            pltpu.VMEM((pairs, 128, 256), bf16),
-            pltpu.VMEM((pairs, 128, 256), bf16),
-            pltpu.VMEM(full, f32),
-            pltpu.VMEM((pairs, 128, 256), f32),
-            pltpu.VMEM((pairs, 128, 256), f32),
-            pltpu.VMEM((n_seq,) + packed, bf16),
-            dma(n_seq),
-        ],
-        compiler_params=cparams(),
-    )(
-        coef_b, cend, queries, keys, vals, phi_q, phi_k, dd, srel, s_in, cnt_col, cnt_row, feat_full,
-        *g_states,
-    )
-
-    cut = 3 * width // 2
-    grad_left = to_owner(mm_f(h_one, d_qkv[:, :cut]).astype(bf16), n_seq, depth, False)
-    grad_right = to_owner(
-        jnp.concatenate([mm_f(h_one, d_qkv[:, cut:]).astype(bf16), g_feat], axis=1), n_seq, depth, True
-    )
+    norm_two = jnp.stack([sums[3], sums[4]], axis=1).astype(bf16)
+    norm_two = jnp.concatenate([norm_two, jnp.zeros((width, 126), bf16)], axis=1)
+
+    g_proj = mm_f(act, dy).astype(bf16)
+    spread.far(g_proj)
+    red_proj = Reduce([g_proj], n_seq, depth).send()
+    h_late = after(h_two, red_proj.out, *[spread.found[b] for b in spread.bits])
+    g_fc = mm_f(h_late, d_fc).astype(bf16)
+    g_states = spread.cores()
+    red_fc = Reduce([g_fc], n_seq, depth).send()
+    g_out = mm_f(after(att, red_fc.out, g_states[0]), d_att).astype(bf16)
+    red_proj.add(red_fc.out).send()
+    me_back = after(me_arr, red_proj.out, g_out)
+
+    groups = 2
+    some = pairs // groups
+    part = some * 128
+    d_qkv, g_feat = [], []
+    for g in range(groups):
+
+        def spec(cols):
+            return pl.BlockSpec((BT, cols), lambda i: (nblk - 1 - i, g))
+
+        def one_group(shape):
+            return pl.BlockSpec(shape, lambda i: (g,) + (0,) * (len(shape) - 1))
+
+        one = (2 * some, 128, 128)
+        d_one, g_one = pl.pallas_call(
+            functools.partial(back_body, g * some, some, pairs),
+            name="back",
+            cost_estimate=cost(22),
+            grid=(nblk,),
+            in_specs=[
+                smem(), smem(), smem(), spec(part), spec(part), spec(part), spec(2 * part), spec(2 * part),
+                spec(2 * part), pl.BlockSpec((1,) + one, lambda i: (nblk - 1 - i, g, 0, 0)), one_group(one),
+                rows_spec(BT, 1, nblk), pl.BlockSpec((1, BT), lambda i: (0, nblk - 1 - i)),
+                one_group((part, 128)),
+            ]
+            + [whole()] * 2,
+            out_specs=[rows_spec(BT, 3 * part, nblk), full_spec((part, 128))],
+            out_shape=[sds((tokens, 3 * part), bf16), sds((part, 128), bf16)],
+            scratch_shapes=[
+                pltpu.VMEM((some, 128, 256), bf16),
+                pltpu.VMEM((some, 128, 256), bf16),
+                pltpu.VMEM(one, f32),
+                pltpu.VMEM((some, 128, 256), f32),
+                pltpu.VMEM((some, 128, 256), f32),
+                pltpu.VMEM((2, n_seq // 2) + packed, bf16),
+                dma(n_seq),
+            ],
+            compiler_params=cparams(),
+        )(
+            me_back, keeps, cend, queries, keys, vals, phi_q, phi_k, dd, srel, s_in, cnt_col, cnt_row,
+            feat_all, *g_states,
+        )
+        d_qkv.append(d_one)
+        g_feat.append(g_one)
+        if g == 0:
+            red_fc.add(d_one).send()
+            g_one = mm_f(after(h_one, red_fc.out), d_one).astype(bf16)
+            red_one = Reduce([g_one, g_out, norm_two], n_seq, depth).send()
+            red_proj.add(red_one.out).send()
+            me_back = after(me_arr, red_proj.out, red_one.out)
+        squares = squares + xor_send(squares, n_seq, 1 << g)
+        squares = after(squares, d_one)
+
+    last = d_qkv[-1]
+    g_two = mm_f(h_one, last).astype(bf16)
+    red_two = Reduce([g_two, jnp.concatenate(g_feat, axis=0)], n_seq, depth).send()
+    red_fc.add(red_two.out).send()
+    red_one.add(red_fc.out).send()
+    red_proj.add(red_one.out).send_stream()
+    me_late = after(me_arr, red_proj.out, red_one.out, red_fc.out)
     dx, sums_one = pl.pallas_call(
-        functools.partial(enter_body, n_seq),
+        functools.partial(enter_body, groups),
         name="enter",
+        cost_estimate=cost(11),
         grid=(tokens // TM,),
-        in_specs=[
-            smem(), rows_spec(TM, width), rows_spec(TM, width), rows_spec(TM, 3 * width), full_spec((8, width)),
-        ]
-        + [whole()] * (3 * n_seq),
+        in_specs=[smem(), rows_spec(TM, width), rows_spec(TM, width), full_spec((8, width))]
+        + [rows_spec(TM, 3 * part)] * groups
+        + [whole()] * 2,
         out_specs=[rows_spec(TM, width), full_spec((8, width))],
         out_shape=[sds((tokens, width), f32), sds((8, width), f32)],
-        scratch_shapes=[pltpu.VMEM((width, width), bf16)] * 3 + [dma(3, n_seq)],
+        scratch_shapes=[pltpu.VMEM((width, 3 * width), bf16), dma(2, n_seq)],
         compiler_params=cparams(),
-    )(me_arr, x, d_mid, d_qkv, gb, *second_blocks, *keys_blocks, *vals_blocks)
-    norm_cols = jnp.stack([sums_one[0], sums[3], sums_one[1], sums[4]], axis=1).astype(bf16)
-    last = to_owner(
-        jnp.concatenate([g_out, norm_cols, jnp.zeros((width, 124), bf16)], axis=1), n_seq, depth, False
+    )(me_late, x, d_mid, gb, *d_qkv, *first_blocks)
+    for bit in range(groups, n_seq.bit_length() - 1):
+        squares = squares + xor_send(squares, n_seq, 1 << bit)
+    branch_rms = jnp.sqrt(squares / (tokens * n_seq * width)).reshape(1, 3)
+    norm_one = jnp.stack([sums_one[0], sums_one[1]], axis=1).astype(bf16)
+    norm_one = jnp.concatenate([norm_one, jnp.zeros((width, 126), bf16)], axis=1)
+    red_norm = Reduce([norm_one], n_seq, depth).send()
+    red_a, red_b = red_two.add(dx).cut((3 * part + 128) // 2)
+    red_a.send()
+    red_norm.add(red_a.out)
+    red_b.cur = red_b.cur + red_norm.cur
+    red_b.send()
+    grad_proj = red_proj.done(red_a.out, red_b.out)
+    red_fc.add(red_a.out, red_b.out).send_stream()
+    red_one.add(red_fc.out).send()
+    red_a.add(red_one.out).send()
+    red_b.add(red_one.out).send()
+    for red in (red_one, red_a, red_b):
+        while red.order:
+            red.add().send()
+    grad_fc = red_fc.done(red_a.out, red_b.out)
+    for red in (red_one, red_a, red_b):
+        red.add()
+    tail = Reduce(red_one.cur + red_a.cur + red_b.cur, n_seq, depth, [], []).send_stream().done()
+    first_cols = 3 * part + width + 128
+    grads = [tail[:, : 3 * part], tail[:, first_cols : first_cols + 3 * part]]
+    grad_out = tail[:, 3 * part : first_cols]
+    grad_feat = tail[:, first_cols + 3 * part : first_cols + 3 * part + 128]
+    norm_one = tail[:, first_cols + 3 * part + 128 :]
+    grad_qkv = jnp.concatenate(
+        [grads[g][:, i * part : (i + 1) * part] for i in range(3) for g in range(groups)], axis=1
     )
     return (
         y[None],
         dx[None],
-        last[:, width : width + 2],
-        last[:, width + 2 : width + 4],
-        jnp.concatenate([grad_left, grad_right[:, : 3 * width - cut]], axis=1),
-        grad_right[:, 3 * width - cut :],
-        last[:, :width],
+        jnp.concatenate([norm_one[:, 0:1], grad_out[:, width : width + 1]], axis=1),
+        jnp.concatenate([norm_one[:, 1:2], grad_out[:, width + 1 : width + 2]], axis=1),
+        grad_qkv,
+        grad_feat,
+        grad_out[:, :width],
         grad_fc,
         grad_proj,
         branch_rms,
     )
-
-
-def assembled(blocks, me):
-    size = len(blocks)
-    rows = blocks[0].shape[0]
-    out = jnp.zeros((size * rows, blocks[0].shape[1]), blocks[0].dtype)
-    for r, block in enumerate(blocks):
-        out = lax.dynamic_update_slice_in_dim(out, block, (me ^ r) * rows, 0)
-    return out
 
 
 def solution(mesh):

time: 506 us -> 385 us (0.76)
  waiting for transfers between devices: 140 us -> 59.1 us
  starting transfers between devices: 113 us -> 62.5 us
  other arithmetic: 16.5 us -> 33.5 us
  local copies, waits for them, and re-layouts: 40.4 us -> 28 us
  Pallas kernels: 160 us -> 171 us
    ppermute x74 -> x39, waiting for transfers between devices: 86.1 us -> 13.4 us  [xor_send(): return lax.ppermute(arr, 'seq', [(i, i ^ mask) for i in range(size)])]
    ppermute x74 -> x39, starting transfers between devices: 72.7 us -> 42.2 us  [xor_send(): return lax.ppermute(arr, 'seq', [(i, i ^ mask) for i in range(size)])]
    ppermute x30 -> x18, starting transfers between devices: 40.4 us -> 20.3 us  [the longest x9 11.4 us: send_stream(): lax.ppermute(piece, 'stream', [(i, (i + d) % depth) for i in range(depth)])]
    pallas_call x4 -> x6, Pallas kernels: 117 us -> 127 us  [the longest x2 50.4 us: shards(): pl.pallas_call(functools.partial(back_body, g * some, some, pairs), name=...]
    slice x15 -> x11, local copies, waits for them, and re-layouts: 11.8 us -> 2.5 us  [the longest x1 0.75 us: shards(): flags = gb[4].reshape(n_seq, depth, rows)[:, :, 0]]
    another operation x4 -> x12, other arithmetic: 0.89 us -> 9.78 us  [the longest x6 8.12 us: cores(): stack = jnp.stack(parts)]
    ppermute x30 -> x18, waiting for transfers between devices: 54 us -> 45.7 us  [the longest x9 28.3 us: send_stream(): lax.ppermute(piece, 'stream', [(i, (i + d) % depth) for i in range(depth)])]
    convert_element_type x15, other arithmetic: 8.84 us -> 16.4 us  [add(): self.cur = [(beside(self.kept).astype(f32) + got.astype(f32)).astype(bf16)]]
  transfers between devices with their start and end apart: 104 -> 57, of which waited for: 42 -> 14; matrix products, arithmetic and copies ran while one was open for 15% -> 19% of each run, Pallas kernels for 23% -> 33%
where the time goes in v2:
time: 385 us; the launch traced here: 381 us
  Pallas kernels  171 us (44%)
  starting transfers between devices  62.5 us (16%)
  waiting for transfers between devices  59.1 us (15%)
  other arithmetic  33.5 us (9%)
  local copies, waits for them, and re-layouts  28 us (7%)
  matrix products  24.3 us (6%)
    pallas_call x2, Pallas kernels, shards(): pl.pallas_call(functools.partial(back_body, g * some, some, pairs), name=...  50.4 us
    pallas_call x1, Pallas kernels, shards(): pl.pallas_call(functools.partial(middle_body, n_seq, pairs), name='middle...  43.3 us
    pallas_call x2, Pallas kernels, shards(): pl.pallas_call(functools.partial(local_body, base, pairs), name='local',...  43 us
    ppermute x39, starting transfers between devices, xor_send(): return lax.ppermute(arr, 'seq', [(i, i ^ mask) for i in range(size)])  42.2 us
    ppermute x9, waiting for transfers between devices, send_stream(): lax.ppermute(piece, 'stream', [(i, (i + d) % depth) for i in range(depth)])  28.3 us
    dot_general x5, matrix products, mm_f(): lax.dot_general(a, b, (((0,), (0,)), ((), ())), preferred_element_type=f32)  24.1 us
    pallas_call x1, Pallas kernels, shards(): pl.pallas_call(functools.partial(keys_body, n_seq, pairs), name='keys', c...  21.9 us
    ppermute x9, waiting for transfers between devices, stream_send(): lax.ppermute(shard, 'stream', [(i, (i + d) % depth) for i in range(depth)])  17.5 us
  transfers between devices with their start and end apart: 57, of which 14 were waited for; matrix products, arithmetic and copies ran while one was open for 19% of the time, Pallas kernels for 33%

profile of v2, /device:TPU:9, one launch (start us, length us, event | category | flops | bytes accessed | tf_op | source)
XLA Modules:
  0.0 380.7 jit_solution(10261344869243908101)
XLA Ops:
  2.1 1.3 reduce_max.9
  5.2 2.5 collective-permute-start.1
  7.7 2.2 collective-permute-start.2
  11.1 3.6 collective-permute-done.1
  14.7 3.2 collective-permute-done.2
  18.0 1.3 collective-permute-start.3
  19.3 1.2 collective-permute-start.4
  21.7 8.0 %collective-permute-done.3 = bf16[96,2560]{1,0:T(8,128)(2,1)S(1)} collective-permute-done((bf16[96,2560]{1,0:T(8,128)(2,1)S(1)}, bf16[96,2560]{1,0:T(8,128)(2,1)S(1)}, u32[]{:S(2)}, u32[]{:S(2)}) %collective-permute-start.3) | collective-permute-done | bytes 491552 | tf_op jit(solution)/shard_map/ppermute | solution.py:32
  29.7 1.3 collective-permute-start.6
  31.0 1.3 collective-permute-start.7
  32.4 3.4 collective-permute-start.5
  36.7 3.3 collective-permute-start.10
  40.0 10.7 %collective-permute-done.5 = bf16[24,3840]{1,0:T(8,128)(2,1)S(1)} collective-permute-done((bf16[24,3840]{1,0:T(8,128)(2,1)S(1)}, bf16[24,3840]{1,0:T(8,128)(2,1)S(1)}, u32[]{:S(2)}, u32[]{:S(2)}) %collective-permute-start.5) | collective-permute-done | bytes 184352 | tf_op jit(solution)/shard_map/ppermute | solution.py:41
  52.2 1.3 copy-done.26
  54.2 21.9 %keys.1 = (bf16[1024,768]{1,0:T(8,128)(2,1)}, bf16[1024,768]{1,0:T(8,128)(2,1)}, bf16[1024,768]{1,0:T(8,128)(2,1)}, bf16[1024,1536]{1,0:T(8,128)(2,1)}, bf16[7,1...) custom-call(s32[1]{0:T(128)} %bitcast.me_ref, f32[9]{0:T(128)} %copy-done.25, ...), custom_call_target="tpu_custom_call" | custom-call | flops 11000000512 | bytes 22000000 | tf_op jit(solution)/shard_map/keys/pallas_call | solution.py:681
  79.4 1.2 collective-permute-start.18
  80.6 21.4 %local.2 = (bf16[1024,768]{1,0:T(8,128)(2,1)}, bf16[1024,1536]{1,0:T(8,128)(2,1)}, f32[1024,768]{1,0:T(8,128)}, f32[1024,768]{1,0:T(8,128)}, bf16[8,12,128,128]{3,2,1,0:T(8,128)(2,1)}, /*index=5*/f32[12,128,128]{2,1,0:T(8,128)}) custom-call(s32[1]{0:T(128)} %bitcast.me_ref, f32[9]{0:T(128)} %copy-done.25, bf16[1024,768]{1,0:T(8,128)(2,1)} %get-tuple-element.148.h_ref, ...), custom_call_target="tpu_custom_call" | custom-call | flops 9500000256 | bytes 19000000 | tf_op jit(solution)/shard_map/local/pallas_call | solution.py:722
  102.4 1.2 collective-permute-start.21
  104.5 1.5 pad_maximum_fusion.refs_0_
  106.0 6.0 %collective-permute-start.22 = (bf16[4,96,3840]{2,1,0:T(8,128)(2,1)S(1)}, bf16[4,96,3840]{2,1,0:T(8,128)(2,1)}, u32[]{:S(2)}, u32[]{:S(2)}) collective-permute-start(bf16[4,96,3840]{2,1,0:T(8,128)(2,1)S(1)} %pad_maximum_fusion.refs_0_), channel_id=1, source_target_pairs={{0,4},{4,0},{8,12},{12,8},{16,20},{20,16},{24,28},{28,24},{1,5},{5... | collective-permute-start | bytes 8847368 | tf_op jit(solution)/shard_map/ppermute | solution.py:32
  112.9 21.7 %local.3 = (bf16[1024,768]{1,0:T(8,128)(2,1)}, bf16[1024,1536]{1,0:T(8,128)(2,1)}, f32[1024,768]{1,0:T(8,128)}, f32[1024,768]{1,0:T(8,128)}, bf16[8,12,128,128]{3,2,1,0:T(8,128)(2,1)}, /*index=5*/f32[12,128,128]{2,1,0:T(8,128)}) custom-call(s32[1]{0:T(128)} %bitcast.me_ref, ...), custom_call_target="tpu_custom_call", output_to_operand_aliasing={{0}: (11, {}), {1}: (12, {}), {2}: (13, {}), {3}: (14, {}),... | custom-call | flops 9500000256 | bytes 19000000 | tf_op jit(solution)/shard_map/local/pallas_call | solution.py:722
  134.6 3.0 pad_maximum_fusion.1.refs_2_
  137.6 4.0 %collective-permute-start.24 = (bf16[4,384,768]{2,1,0:T(8,128)(2,1)}, bf16[4,384,768]{2,1,0:T(8,128)(2,1)}, u32[]{:S(2)}, u32[]{:S(2)}) collective-permute-start(bf16[4,384,768]{2,1,0:T(8,128)(2,1)} %pad_maximum_fusion.1.refs_2_), channel_id=1, source_target_pairs={{0,4},{4,0},{8,12},{12,8},{16,20},{20,16},{24,28},{28,24},{1,5},{5... | collective-permute-start | bytes 7077896 | tf_op jit(solution)/shard_map/ppermute | solution.py:32
  141.6 2.1 pad_maximum_fusion.6.refs_4_
  145.1 2.3 collective-permute-done.25.refs_5_
  147.4 43.3 %middle.1 = (bf16[1024,768]{1,0:T(8,128)(2,1)}, bf16[1024,768]{1,0:T(8,128)(2,1)}, bf16[1024,768]{1,0:T(8,128)(2,1)}, bf16[1024,3072]{1,0:T(8,128)(2,1)}, bf16[1...) custom-call(s32[1]{0:T(128)} %bitcast.me_ref, ...), custom_call_target="tpu_custom_call" | custom-call | flops 21500000256 | bytes 43000000 | tf_op jit(solution)/shard_map/middle/pallas_call | solution.py:758
  190.7 1.3 collective-permute-start.28
  194.8 8.7 %convolution_convert_fusion.1 = bf16[3072,768]{1,0:T(8,128)(2,1)S(1)} fusion(bf16[1024,3072]{1,0:T(8,128)(2,1)} %get-tuple-element.130, bf16[1,1024,768]{2,1,0:T(8,128)(2,1)S(1)} %copy-done.27), kind=kOutput, calls=%fused_computation.1 | convolution fusion | flops 4834197504 | bytes 12582912 | tf_op jit(solution)/shard_map/dot_general | solution.py:28
  203.7 2.0 copy-done.1
  205.7 1.3 collective-permute-start.31
  207.0 5.6 %convolution_convert_fusion = bf16[768,3072]{1,0:T(8,128)(2,1)S(1)} fusion(bf16[1024,768]{1,0:T(8,128)(2,1)S(1)} %copy-done.32, bf16[1024,3072]{1,0:T(8,128)(2,1)S(1)} %copy-done.29), kind=kOutput, calls=%fused_computation | convolution fusion | flops 4834197504 | bytes 12582912 | tf_op jit(solution)/shard_map/dot_general | solution.py:28
  212.6 1.5 dynamic-slice_bitcast_fusion
  214.1 1.3 copy-done
  216.5 1.3 pad_maximum_fusion.7.refs_0_
  218.0 3.2 convolution_convert_fusion.4
  222.1 2.2 fusion.1
  226.7 25.1 %back.2 = (bf16[1024,1152]{1,0:T(8,128)(2,1)}, bf16[384,128]{1,0:T(8,128)(2,1)}) custom-call(s32[1]{0:T(128)} %bitcast.me_ref, f32[8]{0:T(128)} %bitcast.240, f32[9]{0:T(128)} %copy-done.25, bf16[1024,768]{1,0:T(8,128)(2,1)} %get-tuple-element.141.q_ref, bf16[1024,768]{1,0:T(8,128)(2,1)} %get-tuple-element.142.k_ref, ...), custom_call_target="tpu_custom_call" | custom-call | flops 11000000512 | bytes 22000000 | tf_op jit(solution)/shard_map/back/pallas_call | solution.py:823
  251.8 1.3 collective-permute-start.55
  254.3 3.4 fusion
  258.9 1.2 collective-permute-start.35
  260.1 2.3 convolution_convert_fusion.3
  263.5 1.4 pad_maximum_fusion.3
  264.9 1.9 collective-permute-start.34
  266.8 1.5 fusion.3
  269.7 25.4 %back.3 = (bf16[1024,1152]{1,0:T(8,128)(2,1)}, bf16[384,128]{1,0:T(8,128)(2,1)}) custom-call(s32[1]{0:T(128)} %bitcast.me_ref, f32[8]{0:T(128)} %bitcast.241, f32[9]{0:T(128)} %copy-done.25, bf16[1024,768]{1,0:T(8,128)(2,1)} %get-tuple-element.141.q_ref, bf16[1024,768]{1,0:T(8,128)(2,1)} %get-tuple-element.142.k_ref, ...), custom_call_target="tpu_custom_call" | custom-call | flops 11000000512 | bytes 22000000 | tf_op jit(solution)/shard_map/back/pallas_call | solution.py:823
  295.1 4.4 %convolution_convert_fusion.2 = bf16[768,1152]{1,0:T(8,128)(2,1)S(1)} fusion(bf16[1024,768]{1,0:T(8,128)(2,1)} %get-tuple-element.148.h_ref, bf16[1024,1152]{1,0:T(8,128)(2,1)} %get-tuple-element.152.refs_1_), kind=kOutput, calls=%fused_computation.6 | convolution fusion | flops 1812824064 | bytes 5701632 | tf_op jit(solution)/shard_map/dot_general | solution.py:28
  299.5 1.2 collective-permute-start.56
  304.7 1.7 fusion.2
  307.7 1.9 add_convert_fusion
  312.5 11.9 %enter.1 = (f32[1024,768]{1,0:T(8,128)}, f32[8,768]{1,0:T(8,128)}) custom-call(s32[1]{0:T(128)} %bitcast.me_ref, bf16[1024,768]{1,0:T(8,128)(2,1)} %bitcast.245, f32[1024,768]{1,0:T(8,128)} %get-tuple-element.159.dr_ref, f32[8,768]{1,0:T(8,128)} %get-tuple-element.99.gb_ref, bf16[1024,1152]{1,0:T(8,128)(2,1)} %get-tuple-element.146.refs_0_, ...), custom_call_target="tpu_custom_call" | custom-call | flops 5500000256 | bytes 11000000 | tf_op jit(solution)/shard_map/enter/pallas_call | solution.py:869
  327.1 4.2 %collective-permute-start.52 = (bf16[96,768]{1,0:T(8,128)(2,1)S(1)}, bf16[96,768]{1,0:T(8,128)(2,1)S(1)}, u32[]{:S(2)}, u32[]{:S(2)}) collective-permute-start(bf16[96,768]{1,0:T(8,128)(2,1)S(1)} %get-tuple-element.219), channel_id=1, source_target_pairs={{0,2},{1,3},{2,0},{3,1},{4,6},{5,7},{6,4},{7,5},{8,10},{9,11},{10,... | collective-permute-start | bytes 442376 | tf_op jit(solution)/shard_map/ppermute | solution.py:148
  331.3 1.5 add_convert_fusion.1
  334.0 1.2 fusion.5
  336.4 4.3 %collective-permute-done.52 = bf16[96,768]{1,0:T(8,128)(2,1)S(1)} collective-permute-done((bf16[96,768]{1,0:T(8,128)(2,1)S(1)}, bf16[96,768]{1,0:T(8,128)(2,1)S(1)}, u32[]{:S(2)}, u32[]{:S(2)}) %collective-permute-start.52) | collective-permute-done | bytes 147488 | tf_op jit(solution)/shard_map/ppermute | solution.py:148
  340.6 3.3 collective-permute-done.53
  344.9 1.4 collective-permute-start.50
  346.3 1.4 fusion.4
  350.4 5.7 %collective-permute-done.49 = bf16[24,3072]{1,0:T(8,128)(2,1)S(1)} collective-permute-done((bf16[24,3072]{1,0:T(8,128)(2,1)S(1)}, bf16[24,3072]{1,0:T(8,128)(2,1)S(1)}, u32[]{:S(2)}, u32[]{:S(2)}) %collective-permute-start.49) | collective-permute-done | bytes 147488 | tf_op jit(solution)/shard_map/ppermute | solution.py:148
  356.1 2.0 collective-permute-done.50
  358.1 1.2 collective-permute-done.42
  359.7 1.5 collective-permute-start.45
  361.2 3.1 collective-permute-start.46
  365.1 9.8 %collective-permute-done.46 = bf16[24,3456]{1,0:T(8,128)(2,1)S(1)} collective-permute-done((bf16[24,3456]{1,0:T(8,128)(2,1)S(1)}, bf16[24,3456]{1,0:T(8,128)(2,1)S(1)}, u32[]{:S(2)}, u32[]{:S(2)}) %collective-permute-start.46) | collective-permute-done | bytes 165920 | tf_op jit(solution)/shard_map/ppermute | solution.py:148
  374.9 3.2 collective-permute-done.47
  (268 shorter events, 47.5 us)
Async XLA Ops:
  5.1 5.9 %collective-permute-start = (bf16[24,2560]{1,0:T(8,128)(2,1)S(1)}, bf16[24,2560]{1,0:T(8,128)(2,1)S(1)}, u32[]{:S(2)}, u32[]{:S(2)}) collective-permute-start(bf16[24,2560]{1,0:T(8,128)(2,1)S(1)} %concatenate.61), channel_id=1, source_target_pairs={{0,3},{1,0},{2,1},{3,2},{4,7},{5,4},{6,5},{7,6},{8,11},{9,8},{10,9... | collective-permute-start | bytes 368648 | tf_op jit(solution)/shard_map/ppermute | solution.py:41
  5.2 9.5 %collective-permute-start.1 = (bf16[24,2560]{1,0:T(8,128)(2,1)S(1)}, bf16[24,2560]{1,0:T(8,128)(2,1)S(1)}, u32[]{:S(2)}, u32[]{:S(2)}) collective-permute-start(bf16[24,2560]{1,0:T(8,128)(2,1)S(1)} %concatenate.61), channel_id=1, source_target_pairs={{0,2},{1,3},{2,0},{3,1},{4,6},{5,7},{6,4},{7,5},{8,10},{9,11},{10,... | collective-permute-start | bytes 368648 | tf_op jit(solution)/shard_map/ppermute | solution.py:41
  7.7 10.2 %collective-permute-start.2 = (bf16[24,2560]{1,0:T(8,128)(2,1)S(1)}, bf16[24,2560]{1,0:T(8,128)(2,1)S(1)}, u32[]{:S(2)}, u32[]{:S(2)}) collective-permute-start(bf16[24,2560]{1,0:T(8,128)(2,1)S(1)} %concatenate.61), channel_id=1, source_target_pairs={{0,1},{1,2},{2,3},{3,0},{4,5},{5,6},{6,7},{7,4},{8,9},{9,10},{10,1... | collective-permute-start | bytes 368648 | tf_op jit(solution)/shard_map/ppermute | solution.py:41
  11.1 10.6 %copy-start.25 = (f32[9]{0:T(128)}, f32[9]{0:T(128)S(1)}, u32[]{:S(2)}) copy-start(f32[9]{0:T(128)S(1)} %pad_maximum_fusion.16.cend_ref) | copy-start | bytes 112
  11.1 10.6 %copy-start.19 = (bf16[24,3072]{1,0:T(8,128)(2,1)S(1)}, bf16[24,3072]{1,0:T(8,128)(2,1)}, u32[]{:S(2)}) copy-start(bf16[24,3072]{1,0:T(8,128)(2,1)} %param.17) | copy-start | bytes 442372
  18.0 11.6 %collective-permute-start.3 = (bf16[96,2560]{1,0:T(8,128)(2,1)S(1)}, bf16[96,2560]{1,0:T(8,128)(2,1)S(1)}, u32[]{:S(2)}, u32[]{:S(2)}) collective-permute-start(bf16[96,2560]{1,0:T(8,128)(2,1)S(1)} %constant_dynamic-slice_fusion.3), channel_id=1, source_target_pairs={{0,8},{4,12},{8,0},{12,4},{16,24},{20,28},{24,16},{28,20},{1,9},{5... | collective-permute-start | bytes 1474568 | tf_op jit(solution)/shard_map/ppermute | solution.py:32
  19.3 11.7 %collective-permute-start.4 = (bf16[96,2560]{1,0:T(8,128)(2,1)S(1)}, bf16[96,2560]{1,0:T(8,128)(2,1)S(1)}, u32[]{:S(2)}, u32[]{:S(2)}) collective-permute-start(bf16[96,2560]{1,0:T(8,128)(2,1)S(1)} %constant_dynamic-slice_fusion.3), channel_id=1, source_target_pairs={{0,16},{4,20},{8,24},{12,28},{16,0},{20,4},{24,8},{28,12},{1,17},{... | collective-permute-start | bytes 1474568 | tf_op jit(solution)/shard_map/ppermute | solution.py:32
  20.6 15.8 %copy-start.23 = (f32[8,128]{1,0:T(8,128)}, f32[8,128]{1,0:T(8,128)S(1)}, u32[]{:S(2)}) copy-start(f32[8,128]{1,0:T(8,128)S(1)} %broadcast_add_fusion) | copy-start | bytes 12292
  29.7 6.1 %collective-permute-start.6 = (bf16[96,1280]{1,0:T(8,128)(2,1)S(1)}, bf16[96,1280]{1,0:T(8,128)(2,1)S(1)}, u32[]{:S(2)}, u32[]{:S(2)}) collective-permute-start(bf16[96,1280]{1,0:T(8,128)(2,1)S(1)} %slice.119), channel_id=1, source_target_pairs={{0,16},{4,20},{8,24},{12,28},{16,0},{20,4},{24,8},{28,12},{1,17},{... | collective-permute-start | bytes 737288 | tf_op jit(solution)/shard_map/ppermute | solution.py:32
  31.0 5.4 %collective-permute-start.7 = (bf16[96,1280]{1,0:T(8,128)(2,1)S(1)}, bf16[96,1280]{1,0:T(8,128)(2,1)S(1)}, u32[]{:S(2)}, u32[]{:S(2)}) collective-permute-start(bf16[96,1280]{1,0:T(8,128)(2,1)S(1)} %slice.120), channel_id=1, source_target_pairs={{0,8},{4,12},{8,0},{12,4},{16,24},{20,28},{24,16},{28,20},{1,9},{5... | collective-permute-start | bytes 737288 | tf_op jit(solution)/shard_map/ppermute | solution.py:32
  32.3 18.4 %collective-permute-start.8 = (bf16[24,3840]{1,0:T(8,128)(2,1)S(1)}, bf16[24,3840]{1,0:T(8,128)(2,1)S(1)}, u32[]{:S(2)}, u32[]{:S(2)}) collective-permute-start(bf16[24,3840]{1,0:T(8,128)(2,1)S(1)} %pad_maximum_fusion.11), channel_id=1, source_target_pairs={{0,2},{1,3},{2,0},{3,1},{4,6},{5,7},{6,4},{7,5},{8,10},{9,11},{10,... | collective-permute-start | bytes 552968 | tf_op jit(solution)/shard_map/ppermute | solution.py:41
  32.4 18.3 %collective-permute-start.5 = (bf16[24,3840]{1,0:T(8,128)(2,1)S(1)}, bf16[24,3840]{1,0:T(8,128)(2,1)S(1)}, u32[]{:S(2)}, u32[]{:S(2)}) collective-permute-start(bf16[24,3840]{1,0:T(8,128)(2,1)S(1)} %pad_maximum_fusion.11), channel_id=1, source_target_pairs={{0,3},{1,0},{2,1},{3,2},{4,7},{5,4},{6,5},{7,6},{8,11},{9,8},{10,9... | collective-permute-start | bytes 552968 | tf_op jit(solution)/shard_map/ppermute | solution.py:41
  35.8 15.0 %collective-permute-start.9 = (bf16[24,3840]{1,0:T(8,128)(2,1)S(1)}, bf16[24,3840]{1,0:T(8,128)(2,1)S(1)}, u32[]{:S(2)}, u32[]{:S(2)}) collective-permute-start(bf16[24,3840]{1,0:T(8,128)(2,1)S(1)} %pad_maximum_fusion.11), channel_id=1, source_target_pairs={{0,1},{1,2},{2,3},{3,0},{4,5},{5,6},{6,7},{7,4},{8,9},{9,10},{10,1... | collective-permute-start | bytes 552968 | tf_op jit(solution)/shard_map/ppermute | solution.py:41
  36.7 14.3 %copy-start.8 = (bf16[4,96,2560]{2,1,0:T(8,128)(2,1)}, bf16[4,96,2560]{2,1,0:T(8,128)(2,1)S(1)}, u32[]{:S(2)}) copy-start(bf16[4,96,2560]{2,1,0:T(8,128)(2,1)S(1)} %pad_maximum_fusion.2.refs_0_.refs_2_) | copy-start | bytes 5898244
  36.7 15.4 %collective-permute-start.10 = (bf16[4,96,2560]{2,1,0:T(8,128)(2,1)S(1)}, bf16[4,96,2560]{2,1,0:T(8,128)(2,1)S(1)}, u32[]{:S(2)}, u32[]{:S(2)}) collective-permute-start(bf16[4,96,2560]{2,1,0:T(8,128)(2,1)S(1)} %pad_maximum_fusion.2.refs_0_.refs_2_), channel_id=1, source_target_pairs={{0,4},{4,0},{8,12},{12,8},{16,20},{20,16},{24,28},{28,24},{1,5},{5... | collective-permute-start | bytes 5898248 | tf_op jit(solution)/shard_map/ppermute | solution.py:32
  51.0 25.1 %collective-permute-start.11 = (bf16[96,3840]{1,0:T(8,128)(2,1)S(1)}, bf16[96,3840]{1,0:T(8,128)(2,1)S(1)}, u32[]{:S(2)}, u32[]{:S(2)}) collective-permute-start(bf16[96,3840]{1,0:T(8,128)(2,1)S(1)} %constant_dynamic-slice_fusion.2), channel_id=1, source_target_pairs={{0,8},{4,12},{8,0},{12,4},{16,24},{20,28},{24,16},{28,20},{1,9},{5... | collective-permute-start | bytes 2211848 | tf_op jit(solution)/shard_map/ppermute | solution.py:32
  51.3 51.1 %collective-permute-start.12 = (bf16[96,3840]{1,0:T(8,128)(2,1)S(1)}, bf16[96,3840]{1,0:T(8,128)(2,1)S(1)}, u32[]{:S(2)}, u32[]{:S(2)}) collective-permute-start(bf16[96,3840]{1,0:T(8,128)(2,1)S(1)} %constant_dynamic-slice_fusion.2), channel_id=1, source_target_pairs={{0,16},{4,20},{8,24},{12,28},{16,0},{20,4},{24,8},{28,12},{1,17},{... | collective-permute-start | bytes 2211848 | tf_op jit(solution)/shard_map/ppermute | solution.py:32
  52.2 24.7 %collective-permute-start.16 = (bf16[96,768]{1,0:T(8,128)(2,1)S(1)}, bf16[96,768]{1,0:T(8,128)(2,1)S(1)}, u32[]{:S(2)}, u32[]{:S(2)}) collective-permute-start(bf16[96,768]{1,0:T(8,128)(2,1)S(1)} %copy-done.14), channel_id=1, source_target_pairs={{0,1},{1,2},{2,3},{3,0},{4,5},{5,6},{6,7},{7,4},{8,9},{9,10},{10,1... | collective-permute-start | bytes 442376 | tf_op jit(solution)/shard_map/ppermute | solution.py:41
  53.5 24.2 %collective-permute-start.15 = (bf16[96,768]{1,0:T(8,128)(2,1)S(1)}, bf16[96,768]{1,0:T(8,128)(2,1)S(1)}, u32[]{:S(2)}, u32[]{:S(2)}) collective-permute-start(bf16[96,768]{1,0:T(8,128)(2,1)S(1)} %copy-done.14), channel_id=1, source_target_pairs={{0,2},{1,3},{2,0},{3,1},{4,6},{5,7},{6,4},{7,5},{8,10},{9,11},{10,... | collective-permute-start | bytes 442376 | tf_op jit(solution)/shard_map/ppermute | solution.py:41
  53.5 24.2 %collective-permute-start.14 = (bf16[96,768]{1,0:T(8,128)(2,1)S(1)}, bf16[96,768]{1,0:T(8,128)(2,1)S(1)}, u32[]{:S(2)}, u32[]{:S(2)}) collective-permute-start(bf16[96,768]{1,0:T(8,128)(2,1)S(1)} %copy-done.14), channel_id=1, source_target_pairs={{0,3},{1,0},{2,1},{3,2},{4,7},{5,4},{6,5},{7,6},{8,11},{9,8},{10,9... | collective-permute-start | bytes 442376 | tf_op jit(solution)/shard_map/ppermute | solution.py:41
  76.1 25.9 %collective-permute-start.20 = (bf16[7,128,128]{2,1,0:T(8,128)(2,1)}, bf16[7,128,128]{2,1,0:T(8,128)(2,1)}, u32[]{:S(2)}, u32[]{:S(2)}) collective-permute-start(bf16[7,128,128]{2,1,0:T(8,128)(2,1)} %get-tuple-element.107), channel_id=1, source_target_pairs={{0,16},{4,20},{8,24},{12,28},{16,0},{20,4},{24,8},{28,12},{1,17},{... | collective-permute-start | bytes 688136 | tf_op jit(solution)/shard_map/ppermute | solution.py:32
  76.9 26.7 %collective-permute-start.13 = (bf16[96,3840]{1,0:T(8,128)(2,1)S(1)}, bf16[96,3840]{1,0:T(8,128)(2,1)S(1)}, u32[]{:S(2)}, u32[]{:S(2)}) collective-permute-start(bf16[96,3840]{1,0:T(8,128)(2,1)S(1)} %collective-permute-done.11), channel_id=1, source_target_pairs={{0,16},{4,20},{8,24},{12,28},{16,0},{20,4},{24,8},{28,12},{1,17},{... | collective-permute-start | bytes 2211848 | tf_op jit(solution)/shard_map/ppermute | solution.py:32
  78.7 33.3 %collective-permute-start.17 = (bf16[384,768]{1,0:T(8,128)(2,1)}, bf16[384,768]{1,0:T(8,128)(2,1)}, u32[]{:S(2)}, u32[]{:S(2)}) collective-permute-start(bf16[384,768]{1,0:T(8,128)(2,1)} %constant_dynamic-slice_fusion), channel_id=1, source_target_pairs={{0,8},{4,12},{8,0},{12,4},{16,24},{20,28},{24,16},{28,20},{1,9},{5... | collective-permute-start | bytes 1769480 | tf_op jit(solution)/shard_map/ppermute | solution.py:32
  79.4 33.3 %collective-permute-start.18 = (bf16[384,768]{1,0:T(8,128)(2,1)}, bf16[384,768]{1,0:T(8,128)(2,1)}, u32[]{:S(2)}, u32[]{:S(2)}) collective-permute-start(bf16[384,768]{1,0:T(8,128)(2,1)} %constant_dynamic-slice_fusion), channel_id=1, source_target_pairs={{0,16},{4,20},{8,24},{12,28},{16,0},{20,4},{24,8},{28,12},{1,17},{... | collective-permute-start | bytes 1769480 | tf_op jit(solution)/shard_map/ppermute | solution.py:32
  102.1 9.9 %collective-permute-start.19 = (bf16[7,128,128]{2,1,0:T(8,128)(2,1)}, bf16[7,128,128]{2,1,0:T(8,128)(2,1)S(1)}, u32[]{:S(2)}, u32[]{:S(2)}) collective-permute-start(bf16[7,128,128]{2,1,0:T(8,128)(2,1)} %get-tuple-element.107), channel_id=1, source_target_pairs={{0,8},{4,12},{8,0},{12,4},{16,24},{20,28},{24,16},{28,20},{1,9},{5... | collective-permute-start | bytes 688136 | tf_op jit(solution)/shard_map/ppermute | solution.py:32
  102.4 9.6 %collective-permute-start.21 = (bf16[7,128,128]{2,1,0:T(8,128)(2,1)}, bf16[7,128,128]{2,1,0:T(8,128)(2,1)S(1)}, u32[]{:S(2)}, u32[]{:S(2)}) collective-permute-start(bf16[7,128,128]{2,1,0:T(8,128)(2,1)} %collective-permute-done.20), channel_id=1, source_target_pairs={{0,8},{4,12},{8,0},{12,4},{16,24},{20,28},{24,16},{28,20},{1,9},{5... | collective-permute-start | bytes 688136 | tf_op jit(solution)/shard_map/ppermute | solution.py:32
  106.0 28.6 %copy-start.6 = (bf16[4,96,3840]{2,1,0:T(8,128)(2,1)}, bf16[4,96,3840]{2,1,0:T(8,128)(2,1)S(1)}, u32[]{:S(2)}) copy-start(bf16[4,96,3840]{2,1,0:T(8,128)(2,1)S(1)} %pad_maximum_fusion.refs_0_) | copy-start | bytes 8847364
  106.0 41.4 %collective-permute-start.22 = (bf16[4,96,3840]{2,1,0:T(8,128)(2,1)S(1)}, bf16[4,96,3840]{2,1,0:T(8,128)(2,1)}, u32[]{:S(2)}, u32[]{:S(2)}) collective-permute-start(bf16[4,96,3840]{2,1,0:T(8,128)(2,1)S(1)} %pad_maximum_fusion.refs_0_), channel_id=1, source_target_pairs={{0,4},{4,0},{8,12},{12,8},{16,20},{20,16},{24,28},{28,24},{1,5},{5... | collective-permute-start | bytes 8847368 | tf_op jit(solution)/shard_map/ppermute | solution.py:32
  112.7 21.9 %collective-permute-start.23 = (bf16[384,768]{1,0:T(8,128)(2,1)}, bf16[384,768]{1,0:T(8,128)(2,1)S(1)}, u32[]{:S(2)}, u32[]{:S(2)}) collective-permute-start(bf16[384,768]{1,0:T(8,128)(2,1)} %collective-permute-done.18), channel_id=1, source_target_pairs={{0,8},{4,12},{8,0},{12,4},{16,24},{20,28},{24,16},{28,20},{1,9},{5... | collective-permute-start | bytes 1769480 | tf_op jit(solution)/shard_map/ppermute | solution.py:32
  137.6 9.8 %collective-permute-start.24 = (bf16[4,384,768]{2,1,0:T(8,128)(2,1)}, bf16[4,384,768]{2,1,0:T(8,128)(2,1)}, u32[]{:S(2)}, u32[]{:S(2)}) collective-permute-start(bf16[4,384,768]{2,1,0:T(8,128)(2,1)} %pad_maximum_fusion.1.refs_2_), channel_id=1, source_target_pairs={{0,4},{4,0},{8,12},{12,8},{16,20},{20,16},{24,28},{28,24},{1,5},{5... | collective-permute-start | bytes 7077896 | tf_op jit(solution)/shard_map/ppermute | solution.py:32
  143.7 3.7 collective-permute-start.25
  147.4 47.4 %copy-start.27 = (bf16[1,1024,768]{2,1,0:T(8,128)(2,1)S(1)}, bf16[1,1024,768]{2,1,0:T(8,128)(2,1)}, u32[]{:S(2)}) copy-start(bf16[1,1024,768]{2,1,0:T(8,128)(2,1)} %param.19) | copy-start | bytes 4718596
  190.7 14.9 %collective-permute-start.28 = (bf16[7,128,128]{2,1,0:T(8,128)(2,1)}, bf16[7,128,128]{2,1,0:T(8,128)(2,1)S(1)}, u32[]{:S(2)}, u32[]{:S(2)}) collective-permute-start(bf16[7,128,128]{2,1,0:T(8,128)(2,1)} %get-tuple-element.132), channel_id=1, source_target_pairs={{0,8},{4,12},{8,0},{12,4},{16,24},{20,28},{24,16},{28,20},{1,9},{5... | collective-permute-start | bytes 688136 | tf_op jit(solution)/shard_map/ppermute | solution.py:32
  192.0 14.9 %collective-permute-start.27 = (bf16[7,128,128]{2,1,0:T(8,128)(2,1)}, bf16[7,128,128]{2,1,0:T(8,128)(2,1)S(1)}, u32[]{:S(2)}, u32[]{:S(2)}) collective-permute-start(bf16[7,128,128]{2,1,0:T(8,128)(2,1)} %get-tuple-element.132), channel_id=1, source_target_pairs={{0,16},{4,20},{8,24},{12,28},{16,0},{20,4},{24,8},{28,12},{1,17},{... | collective-permute-start | bytes 688136 | tf_op jit(solution)/shard_map/ppermute | solution.py:32
  193.9 22.6 %collective-permute-start.54 = (f32[3]{0:T(128)S(1)}, f32[3]{0:T(128)S(1)}, u32[]{:S(2)}, u32[]{:S(2)}) collective-permute-start(f32[3]{0:T(128)S(1)} %slice_reduce_fusion), channel_id=1, source_target_pairs={{0,4},{4,0},{8,12},{12,8},{16,20},{20,16},{24,28},{28,24},{1,5},{5... | collective-permute-start | bytes 44 | tf_op jit(solution)/shard_map/ppermute | solution.py:32
  194.8 12.2 %copy-start.29 = (bf16[1024,3072]{1,0:T(8,128)(2,1)S(1)}, bf16[1024,3072]{1,0:T(8,128)(2,1)}, u32[]{:S(2)}) copy-start(bf16[1024,3072]{1,0:T(8,128)(2,1)} %get-tuple-element.134) | copy-start | bytes 18874372
  205.6 16.5 %collective-permute-start.26 = (bf16[2,2,384,768]{3,2,1,0:T(8,128)(2,1)S(1)}, bf16[2,2,384,768]{3,2,1,0:T(8,128)(2,1)}, u32[]{:S(2)}, u32[]{:S(2)}) collective-permute-start(bf16[2,2,384,768]{3,2,1,0:T(8,128)(2,1)S(1)} %dynamic-slice_bitcast_fusion.1), channel_id=1, source_target_pairs={{0,4},{4,0},{8,12},{12,8},{16,20},{20,16},{24,28},{28,24},{1,5},{5... | collective-permute-start | bytes 7077896 | tf_op jit(solution)/shard_map/ppermute | solution.py:32
  205.7 10.8 %collective-permute-start.31 = (bf16[7,128,128]{2,1,0:T(8,128)(2,1)S(1)}, bf16[7,128,128]{2,1,0:T(8,128)(2,1)}, u32[]{:S(2)}, u32[]{:S(2)}) collective-permute-start(bf16[7,128,128]{2,1,0:T(8,128)(2,1)S(1)} %collective-permute-done.28), channel_id=1, source_target_pairs={{0,16},{4,20},{8,24},{12,28},{16,0},{20,4},{24,8},{28,12},{1,17},{... | collective-permute-start | bytes 688136 | tf_op jit(solution)/shard_map/ppermute | solution.py:32
  215.4 38.9 %collective-permute-start.30 = (bf16[2,2,96,3072]{3,2,1,0:T(8,128)(2,1)}, bf16[2,2,96,3072]{3,2,1,0:T(8,128)(2,1)}, u32[]{:S(2)}, u32[]{:S(2)}) collective-permute-start(bf16[2,2,96,3072]{3,2,1,0:T(8,128)(2,1)} %dynamic-slice_bitcast_fusion), channel_id=1, source_target_pairs={{0,4},{4,0},{8,12},{12,8},{16,20},{20,16},{24,28},{28,24},{1,5},{5... | collective-permute-start | bytes 7077896 | tf_op jit(solution)/shard_map/ppermute | solution.py:32
  217.8 7.9 %collective-permute-start.32 = (bf16[4,7,128,128]{3,2,1,0:T(8,128)(2,1)S(1)}, bf16[4,7,128,128]{3,2,1,0:T(8,128)(2,1)S(1)}, u32[]{:S(2)}, u32[]{:S(2)}) collective-permute-start(bf16[4,7,128,128]{3,2,1,0:T(8,128)(2,1)S(1)} %pad_maximum_fusion.7.refs_0_), channel_id=1, source_target_pairs={{0,4},{4,0},{8,12},{12,8},{16,20},{20,16},{24,28},{28,24},{1,5},{5... | collective-permute-start | bytes 2752520 | tf_op jit(solution)/shard_map/ppermute | solution.py:32
  225.5 41.3 %collective-permute-start.29 = (bf16[2,384,768]{2,1,0:T(8,128)(2,1)}, bf16[2,384,768]{2,1,0:T(8,128)(2,1)}, u32[]{:S(2)}, u32[]{:S(2)}) collective-permute-start(bf16[2,384,768]{2,1,0:T(8,128)(2,1)} %dynamic-slice_bitcast_fusion.3), channel_id=1, source_target_pairs={{0,8},{4,12},{8,0},{12,4},{16,24},{20,28},{24,16},{28,20},{1,9},{5... | collective-permute-start | bytes 3538952 | tf_op jit(solution)/shard_map/ppermute | solution.py:32
  251.8 2.5 collective-permute-start.55
  258.9 45.9 %collective-permute-start.35 = (bf16[2,96,3072]{2,1,0:T(8,128)(2,1)}, bf16[2,96,3072]{2,1,0:T(8,128)(2,1)}, u32[]{:S(2)}, u32[]{:S(2)}) collective-permute-start(bf16[2,96,3072]{2,1,0:T(8,128)(2,1)} %dynamic-slice_bitcast_fusion.2), channel_id=1, source_target_pairs={{0,8},{4,12},{8,0},{12,4},{16,24},{20,28},{24,16},{28,20},{1,9},{5... | collective-permute-start | bytes 3538952 | tf_op jit(solution)/shard_map/ppermute | solution.py:32
  264.9 42.8 %collective-permute-start.34 = (bf16[2,2,96,2048]{3,2,1,0:T(8,128)(2,1)}, bf16[2,2,96,2048]{3,2,1,0:T(8,128)(2,1)}, u32[]{:S(2)}, u32[]{:S(2)}) collective-permute-start(bf16[2,2,96,2048]{3,2,1,0:T(8,128)(2,1)} %pad_maximum_fusion.3), channel_id=1, source_target_pairs={{0,4},{4,0},{8,12},{12,8},{16,20},{20,16},{24,28},{28,24},{1,5},{5... | collective-permute-start | bytes 4718600 | tf_op jit(solution)/shard_map/ppermute | solution.py:32
  269.4 41.9 %collective-permute-start.33 = (bf16[384,768]{1,0:T(8,128)(2,1)S(1)}, bf16[384,768]{1,0:T(8,128)(2,1)}, u32[]{:S(2)}, u32[]{:S(2)}) collective-permute-start(bf16[384,768]{1,0:T(8,128)(2,1)S(1)} %dynamic-slice_bitcast_fusion.11), channel_id=1, source_target_pairs={{0,16},{4,20},{8,24},{12,28},{16,0},{20,4},{24,8},{28,12},{1,17},{... | collective-permute-start | bytes 1769480 | tf_op jit(solution)/shard_map/ppermute | solution.py:32
  299.5 4.7 %collective-permute-start.56 = (f32[3]{0:T(128)S(1)}, f32[3]{0:T(128)S(1)}, u32[]{:S(2)}, u32[]{:S(2)}) collective-permute-start(f32[3]{0:T(128)S(1)} %add.281), channel_id=1, source_target_pairs={{0,16},{4,20},{8,24},{12,28},{16,0},{20,4},{24,8},{28,12},{1,17},{... | collective-permute-start | bytes 44 | tf_op jit(solution)/shard_map/ppermute | solution.py:32
  303.6 23.5 %collective-permute-start.38 = (bf16[2,2,96,1280]{3,2,0,1:T(8,128)(2,1)}, bf16[2,2,96,1280]{3,2,0,1:T(8,128)(2,1)}, u32[]{:S(2)}, u32[]{:S(2)}) collective-permute-start(bf16[2,2,96,1280]{3,2,0,1:T(8,128)(2,1)} %copy.112), channel_id=1, source_target_pairs={{0,4},{4,0},{8,12},{12,8},{16,20},{20,16},{24,28},{28,24},{1,5},{5... | collective-permute-start | bytes 2949128 | tf_op jit(solution)/shard_map/ppermute | solution.py:32
  307.4 25.8 %collective-permute-start.37 = (bf16[96,3072]{1,0:T(8,128)(2,1)}, bf16[96,3072]{1,0:T(8,128)(2,1)}, u32[]{:S(2)}, u32[]{:S(2)}) collective-permute-start(bf16[96,3072]{1,0:T(8,128)(2,1)} %dynamic-slice_bitcast_fusion.9), channel_id=1, source_target_pairs={{0,16},{4,20},{8,24},{12,28},{16,0},{20,4},{24,8},{28,12},{1,17},{... | collective-permute-start | bytes 1769480 | tf_op jit(solution)/shard_map/ppermute | solution.py:32
  310.5 34.4 %collective-permute-start.36 = (bf16[2,96,2048]{2,1,0:T(8,128)(2,1)}, bf16[2,96,2048]{2,1,0:T(8,128)(2,1)}, u32[]{:S(2)}, u32[]{:S(2)}) collective-permute-start(bf16[2,96,2048]{2,1,0:T(8,128)(2,1)} %dynamic-slice_bitcast_fusion.8), channel_id=1, source_target_pairs={{0,8},{4,12},{8,0},{12,4},{16,24},{20,28},{24,16},{28,20},{1,9},{5... | collective-permute-start | bytes 2359304 | tf_op jit(solution)/shard_map/ppermute | solution.py:32
  325.4 7.5 %collective-permute-start.39 = (bf16[2,2,96,128]{3,2,1,0:T(8,128)(2,1)S(1)}, bf16[2,2,96,128]{3,2,1,0:T(8,128)(2,1)S(1)}, u32[]{:S(2)}, u32[]{:S(2)}) collective-permute-start(bf16[2,2,96,128]{3,2,1,0:T(8,128)(2,1)S(1)} %dynamic-slice_bitcast_fusion.28), channel_id=1, source_target_pairs={{0,4},{4,0},{8,12},{12,8},{16,20},{20,16},{24,28},{28,24},{1,5},{5... | collective-permute-start | bytes 294920 | tf_op jit(solution)/shard_map/ppermute | solution.py:32
  326.1 9.1 %collective-permute-start.51 = (bf16[96,768]{1,0:T(8,128)(2,1)S(1)}, bf16[96,768]{1,0:T(8,128)(2,1)S(1)}, u32[]{:S(2)}, u32[]{:S(2)}) collective-permute-start(bf16[96,768]{1,0:T(8,128)(2,1)S(1)} %get-tuple-element.217), channel_id=1, source_target_pairs={{0,1},{1,2},{2,3},{3,0},{4,5},{5,6},{6,7},{7,4},{8,9},{9,10},{10,1... | collective-permute-start | bytes 442376 | tf_op jit(solution)/shard_map/ppermute | solution.py:148
  327.1 13.5 %collective-permute-start.52 = (bf16[96,768]{1,0:T(8,128)(2,1)S(1)}, bf16[96,768]{1,0:T(8,128)(2,1)S(1)}, u32[]{:S(2)}, u32[]{:S(2)}) collective-permute-start(bf16[96,768]{1,0:T(8,128)(2,1)S(1)} %get-tuple-element.219), channel_id=1, source_target_pairs={{0,2},{1,3},{2,0},{3,1},{4,6},{5,7},{6,4},{7,5},{8,10},{9,11},{10,... | collective-permute-start | bytes 442376 | tf_op jit(solution)/shard_map/ppermute | solution.py:148
  332.9 11.0 %collective-permute-start.53 = (bf16[96,768]{1,0:T(8,128)(2,1)S(1)}, bf16[96,768]{1,0:T(8,128)(2,1)S(1)}, u32[]{:S(2)}, u32[]{:S(2)}) collective-permute-start(bf16[96,768]{1,0:T(8,128)(2,1)S(1)} %get-tuple-element.218), channel_id=1, source_target_pairs={{0,3},{1,0},{2,1},{3,2},{4,7},{5,4},{6,5},{7,6},{8,11},{9,8},{10,9... | collective-permute-start | bytes 442376 | tf_op jit(solution)/shard_map/ppermute | solution.py:148
  333.2 14.5 %collective-permute-start.41 = (bf16[2,96,640]{2,1,0:T(8,128)(2,1)S(1)}, bf16[2,96,640]{2,1,0:T(8,128)(2,1)S(1)}, u32[]{:S(2)}, u32[]{:S(2)}) collective-permute-start(bf16[2,96,640]{2,1,0:T(8,128)(2,1)S(1)} %dynamic-slice_bitcast_fusion.16), channel_id=1, source_target_pairs={{0,8},{4,12},{8,0},{12,4},{16,24},{20,28},{24,16},{28,20},{1,9},{5... | collective-permute-start | bytes 737288 | tf_op jit(solution)/shard_map/ppermute | solution.py:32
  335.3 13.6 %collective-permute-start.43 = (bf16[2,96,768]{2,1,0:T(8,128)(2,1)S(1)}, bf16[2,96,768]{2,1,0:T(8,128)(2,1)S(1)}, u32[]{:S(2)}, u32[]{:S(2)}) collective-permute-start(bf16[2,96,768]{2,1,0:T(8,128)(2,1)S(1)} %pad_maximum_fusion.9), channel_id=1, source_target_pairs={{0,16},{4,20},{8,24},{12,28},{16,0},{20,4},{24,8},{28,12},{1,17},{... | collective-permute-start | bytes 884744 | tf_op jit(solution)/shard_map/ppermute | solution.py:32
  343.9 5.6 %collective-permute-start.48 = (bf16[24,3072]{1,0:T(8,128)(2,1)S(1)}, bf16[24,3072]{1,0:T(8,128)(2,1)S(1)}, u32[]{:S(2)}, u32[]{:S(2)}) collective-permute-start(bf16[24,3072]{1,0:T(8,128)(2,1)S(1)} %get-tuple-element.220), channel_id=1, source_target_pairs={{0,1},{1,2},{2,3},{3,0},{4,5},{5,6},{6,7},{7,4},{8,9},{9,10},{10,1... | collective-permute-start | bytes 442376 | tf_op jit(solution)/shard_map/ppermute | solution.py:148
  344.0 12.1 %collective-permute-start.49 = (bf16[24,3072]{1,0:T(8,128)(2,1)S(1)}, bf16[24,3072]{1,0:T(8,128)(2,1)S(1)}, u32[]{:S(2)}, u32[]{:S(2)}) collective-permute-start(bf16[24,3072]{1,0:T(8,128)(2,1)S(1)} %get-tuple-element.222), channel_id=1, source_target_pairs={{0,2},{1,3},{2,0},{3,1},{4,6},{5,7},{6,4},{7,5},{8,10},{9,11},{10,... | collective-permute-start | bytes 442376 | tf_op jit(solution)/shard_map/ppermute | solution.py:148
  344.9 13.2 %collective-permute-start.50 = (bf16[24,3072]{1,0:T(8,128)(2,1)S(1)}, bf16[24,3072]{1,0:T(8,128)(2,1)S(1)}, u32[]{:S(2)}, u32[]{:S(2)}) collective-permute-start(bf16[24,3072]{1,0:T(8,128)(2,1)S(1)} %get-tuple-element.221), channel_id=1, source_target_pairs={{0,3},{1,0},{2,1},{3,2},{4,7},{5,4},{6,5},{7,6},{8,11},{9,8},{10,9... | collective-permute-start | bytes 442376 | tf_op jit(solution)/shard_map/ppermute | solution.py:148
  347.7 11.7 %collective-permute-start.40 = (bf16[96,2048]{1,0:T(8,128)(2,1)S(1)}, bf16[96,2048]{1,0:T(8,128)(2,1)S(1)}, u32[]{:S(2)}, u32[]{:S(2)}) collective-permute-start(bf16[96,2048]{1,0:T(8,128)(2,1)S(1)} %dynamic-slice_bitcast_fusion.13), channel_id=1, source_target_pairs={{0,16},{4,20},{8,24},{12,28},{16,0},{20,4},{24,8},{28,12},{1,17},{... | collective-permute-start | bytes 1179656 | tf_op jit(solution)/shard_map/ppermute | solution.py:32
  348.9 10.4 %collective-permute-start.42 = (bf16[96,640]{1,0:T(8,128)(2,1)S(1)}, bf16[96,640]{1,0:T(8,128)(2,1)S(1)}, u32[]{:S(2)}, u32[]{:S(2)}) collective-permute-start(bf16[96,640]{1,0:T(8,128)(2,1)S(1)} %dynamic-slice_bitcast_fusion.27), channel_id=1, source_target_pairs={{0,16},{4,20},{8,24},{12,28},{16,0},{20,4},{24,8},{28,12},{1,17},{... | collective-permute-start | bytes 368648 | tf_op jit(solution)/shard_map/ppermute | solution.py:32
  349.5 9.8 %collective-permute-start.44 = (bf16[96,768]{1,0:T(8,128)(2,1)S(1)}, bf16[96,768]{1,0:T(8,128)(2,1)S(1)}, u32[]{:S(2)}, u32[]{:S(2)}) collective-permute-start(bf16[96,768]{1,0:T(8,128)(2,1)S(1)} %dynamic-slice_bitcast_fusion.26), channel_id=1, source_target_pairs={{0,8},{4,12},{8,0},{12,4},{16,24},{20,28},{24,16},{28,20},{1,9},{5... | collective-permute-start | bytes 442376 | tf_op jit(solution)/shard_map/ppermute | solution.py:32
  359.7 5.4 %collective-permute-start.45 = (bf16[24,3456]{1,0:T(8,128)(2,1)S(1)}, bf16[24,3456]{1,0:T(8,128)(2,1)S(1)}, u32[]{:S(2)}, u32[]{:S(2)}) collective-permute-start(bf16[24,3456]{1,0:T(8,128)(2,1)S(1)} %get-tuple-element.214), channel_id=1, source_target_pairs={{0,1},{1,2},{2,3},{3,0},{4,5},{5,6},{6,7},{7,4},{8,9},{9,10},{10,1... | collective-permute-start | bytes 497672 | tf_op jit(solution)/shard_map/ppermute | solution.py:148
  361.2 13.7 %collective-permute-start.46 = (bf16[24,3456]{1,0:T(8,128)(2,1)S(1)}, bf16[24,3456]{1,0:T(8,128)(2,1)S(1)}, u32[]{:S(2)}, u32[]{:S(2)}) collective-permute-start(bf16[24,3456]{1,0:T(8,128)(2,1)S(1)} %get-tuple-element.216), channel_id=1, source_target_pairs={{0,2},{1,3},{2,0},{3,1},{4,6},{5,7},{6,4},{7,5},{8,10},{9,11},{10,... | collective-permute-start | bytes 497672 | tf_op jit(solution)/shard_map/ppermute | solution.py:148
  364.3 13.8 %collective-permute-start.47 = (bf16[24,3456]{1,0:T(8,128)(2,1)S(1)}, bf16[24,3456]{1,0:T(8,128)(2,1)S(1)}, u32[]{:S(2)}, u32[]{:S(2)}) collective-permute-start(bf16[24,3456]{1,0:T(8,128)(2,1)S(1)} %get-tuple-element.215), channel_id=1, source_target_pairs={{0,3},{1,0},{2,1},{3,2},{4,7},{5,4},{6,5},{7,6},{8,11},{9,8},{10,9... | collective-permute-start | bytes 497672 | tf_op jit(solution)/shard_map/ppermute | solution.py:148
  (29 other events, 93.7 us)

commit v3 on v2

--- a/solution.py
+++ b/solution.py
@@ -7,7 +7,9 @@
 from jax.experimental.pallas import tpu as pltpu
 from jax.sharding import PartitionSpec as P
 
-BT = 128
+BT = 256
+GF = 6
+TK = 512
 TM = 256
 epsilon = 1e-05
 f32 = jnp.float32
@@ -200,16 +202,20 @@
         dest[p, :, pl.ds(width, width)] = jnp.where(row >= half, signed, 0.0).astype(bf16)
 
 
-def features(logits, ones):
-    parts = []
-    for j in range(2):
-        one = logits[:, j * 128 : (j + 1) * 128]
-        low = lanes(one.shape) < 64
-        top_a = jnp.max(jnp.where(low, one, -jnp.inf), axis=1, keepdims=True)
-        top_b = jnp.max(jnp.where(low, -jnp.inf, one), axis=1, keepdims=True)
-        parts.append(jnp.exp(one - jnp.where(low, top_a, top_b)))
-    exps = jnp.concatenate(parts, axis=1)
-    return (exps / mm(exps.astype(bf16), ones)).astype(bf16)
+def features(logits_of, ones):
+    halves = [one[:, j * 128 : (j + 1) * 128] for one in logits_of for j in range(2)]
+    low = lanes(halves[0].shape) < 64
+    tops = [
+        (
+            jnp.max(jnp.where(low, one, -jnp.inf), axis=1, keepdims=True),
+            jnp.max(jnp.where(low, -jnp.inf, one), axis=1, keepdims=True),
+        )
+        for one in halves
+    ]
+    exps = [jnp.exp(one - jnp.where(low, *top)) for one, top in zip(halves, tops)]
+    exps = [jnp.concatenate(exps[2 * i : 2 * i + 2], axis=1) for i in range(len(logits_of))]
+    sums = [mm(e.astype(bf16), ones) for e in exps]
+    return [(e / t).astype(bf16) for e, t in zip(exps, sums)]
 
 
 def augmented(two):
@@ -315,13 +321,14 @@
     ones = block_ones(256, 64)
     last = cend_ref[cend_ref.shape[0] - 1]
     used = jnp.where(cnt_ref[...] == last, 1.0, 0.0).astype(bf16)
-    for p in range(pairs):
-        two = slice(p * 128, (p + 1) * 128)
-        phi = features(mm(keys[:, two], maps[p]), ones)
-        phi_ref[:, pl.ds(p * 256, 256)] = phi
-        va, vb = augmented(vals[:, two])
-        state[2 * p] += mm_f(phi[:, :128], va * used)
-        state[2 * p + 1] += mm_f(phi[:, 128:], vb * used)
+    for g in range(0, pairs, GF):
+        group = range(g, min(g + GF, pairs))
+        phis = features([mm(keys[:, p * 128 : (p + 1) * 128], maps[p]) for p in group], ones)
+        for p, phi in zip(group, phis):
+            phi_ref[:, pl.ds(p * 256, 256)] = phi
+            va, vb = augmented(vals[:, p * 128 : (p + 1) * 128])
+            state[2 * p] += mm_f(phi[:, :128], va * used)
+            state[2 * p + 1] += mm_f(phi[:, 128:], vb * used)
 
     @pl.when(step == pl.num_programs(0) - 1)
     def _():
@@ -357,23 +364,27 @@
     after = jnp.where(cnt == last, 1.0, 0.0).astype(bf16)
     keep = jnp.where(first == last, 1.0, 0.0)
     low = lanes((size, 128)) < 64
-    for p in range(pairs):
-        two = slice(p * 128, (p + 1) * 128)
-        phi = features(mm(queries[:, two], maps[p]), ones)
-        phiq_ref[:, pl.ds(p * 256, 256)] = phi
+    for g in range(0, pairs, GF):
+        group = range(g, min(g + GF, pairs))
+        phis = features([mm(queries[:, p * 128 : (p + 1) * 128], maps[p]) for p in group], ones)
+        for p, phi in zip(group, phis):
+            phiq_ref[:, pl.ds(p * 256, 256)] = phi
+        pqs = [phi[:, j * 128 : (j + 1) * 128] for phi in phis for j in range(2)]
+        heads = [2 * p + j for p in group for j in range(2)]
+        pks = [phik_ref[:, pl.ds(h * 128, 128)] for h in heads]
+        scores = [jnp.where(mask, mm_t(pq, pk), 0.0).astype(bf16) for pq, pk in zip(pqs, pks)]
+        val_of = [v for p in group for v in augmented(v_ref[:, p * 128 : (p + 1) * 128])]
         res = []
-        for j, val in enumerate(augmented(v_ref[:, two])):
-            h = 2 * p + j
-            pq = phi[:, j * 128 : (j + 1) * 128]
-            pk = phik_ref[:, pl.ds(h * 128, 128)]
-            scores = jnp.where(mask, mm_t(pq, pk), 0.0).astype(bf16)
+        for h, pq, pk, sc, val in zip(heads, pqs, pks, scores, val_of):
             st = state[h]
             st_b = st.astype(bf16)
             srel_ref[0, h] = st_b
-            res.append(mm(scores, val) + before * mm(pq, st_b))
+            res.append(mm(sc, val) + before * mm(pq, st_b))
             state[h] = keep * st + mm_f(pk, val * after)
-        num_ref[:, two] = jnp.where(low, res[0], res[1])
-        den_ref[:, two] = pltpu.roll(jnp.where(low, res[1], res[0]), 64, 1)
+        for i, p in enumerate(group):
+            two = pl.ds(p * 128, 128)
+            num_ref[:, two] = jnp.where(low, res[2 * i], res[2 * i + 1])
+            den_ref[:, two] = pltpu.roll(jnp.where(low, res[2 * i + 1], res[2 * i]), 64, 1)
 
 
 def middle_body(
@@ -416,10 +427,10 @@
     low = lanes((size, 128)) < 64
     start = jnp.where(cnt_ref[...] == 0.0, 1.0, 0.0)
     start_b = start.astype(bf16)
+    res = [mm(phiq_ref[:, pl.ds(h * 128, 128)], sin_ref[h]) for h in range(2 * pairs)]
     for p in range(pairs):
         two = pl.ds(p * 128, 128)
-        ra = mm(phiq_ref[:, pl.ds(p * 256, 128)], sin_ref[2 * p])
-        rb = mm(phiq_ref[:, pl.ds(p * 256 + 128, 128)], sin_ref[2 * p + 1])
+        ra, rb = res[2 * p], res[2 * p + 1]
         num = num_ref[:, two] + start * jnp.where(low, ra, rb)
         den = den_ref[:, two] + start * pltpu.roll(jnp.where(low, rb, ra), 64, 1)
         inv = 1.0 / den
@@ -461,28 +472,27 @@
     d_o = mm_t(dat, w_out[...])
     ones = block_ones(256, 64)
     lane = lanes((size, 128))
-    for q in range(pairs // 2):
-        four = pl.ds(q * 256, 256)
-        inv = rden[:, four]
-        d_q = d_o[:, q * 256 : (q + 1) * 256]
-        prod = d_q * o_ref[:, four].astype(f32)
-        hi = prod.astype(bf16)
-        lo = (prod - hi.astype(f32)).astype(bf16)
-        dden = -(mm(hi, ones) + mm(lo, ones)) * inv
-        dnum = (d_q * inv).astype(bf16)
-        for i in range(2):
-            p = 2 * q + i
-            sub = slice(i * 128, (i + 1) * 128)
-            dd = pltpu.roll(dden[:, sub], 64, 1)
-            dhi = dd.astype(bf16)
-            dlo = (dd - dhi.astype(f32)).astype(bf16)
-            near = lane & 63
-            aux = jnp.where(near == 0, dhi.astype(f32), jnp.where(near == 1, dlo.astype(f32), 0.0)).astype(bf16)
-            dn = dnum[:, sub]
-            for j, both in enumerate((jnp.where(low, dn, aux), jnp.where(low, aux, dn))):
-                h = 2 * p + j
-                dd_ref[:, pl.ds(h * 128, 128)] = both
-                state[h] += mm_f(phiq_ref[:, pl.ds(h * 128, 128)], both * start_b)
+    quads = range(pairs // 2)
+    fours = [pl.ds(q * 256, 256) for q in quads]
+    d_os = [d_o[:, q * 256 : (q + 1) * 256] for q in quads]
+    prods = [d * o_ref[:, c].astype(f32) for d, c in zip(d_os, fours)]
+    his = [a.astype(bf16) for a in prods]
+    los = [(a - hi.astype(f32)).astype(bf16) for a, hi in zip(prods, his)]
+    ddens = [-(mm(hi, ones) + mm(lo, ones)) * rden[:, c] for hi, lo, c in zip(his, los, fours)]
+    dnums = [(d * rden[:, c]).astype(bf16) for d, c in zip(d_os, fours)]
+    near = lane & 63
+    for p in range(pairs):
+        sub = slice((p % 2) * 128, (p % 2 + 1) * 128)
+        dd = pltpu.roll(ddens[p // 2][:, sub], 64, 1)
+        dhi = dd.astype(bf16)
+        dlo = (dd - dhi.astype(f32)).astype(bf16)
+        aux = jnp.where(near == 0, dhi.astype(f32), jnp.where(near == 1, dlo.astype(f32), 0.0)).astype(bf16)
+        dn = dnums[p // 2][:, sub]
+        dd_ref[:, pl.ds(p * 256, 128)] = jnp.where(low, dn, aux)
+        dd_ref[:, pl.ds(p * 256 + 128, 128)] = jnp.where(low, aux, dn)
+    for h in range(2 * pairs):
+        own = pl.ds(h * 128, 128)
+        state[h] += mm_f(phiq_ref[:, own], dd_ref[:, own] * start_b)
 
     @pl.when(step == pl.num_programs(0) - 1)
     def _():
@@ -532,35 +542,38 @@
     opened = jnp.where(first == 0.0, 1.0, 0.0)
     ones = block_ones(256, 64)
     low = lanes((size, 128)) < 64
+    heads = range(2 * pairs)
+    cols = [pl.ds(h * 128, 128) for h in heads]
+    vals = [v for p in range(pairs) for v in augmented(v_ref[:, pl.ds(p * 128, 128)])]
+    scores_t = [
+        jnp.where(mask_t, mm_t(phik_ref[:, c], phiq_ref[:, c]), 0.0).astype(bf16) for c in cols
+    ]
+    dsc = [jnp.where(mask, mm_t(dd_ref[:, c], v), 0.0).astype(bf16) for c, v in zip(cols, vals)]
+    dsc_t = [jnp.where(mask_t, mm_t(v, dd_ref[:, c]), 0.0).astype(bf16) for c, v in zip(cols, vals)]
+    sts = [
+        (srel_ref[0, h].astype(f32) + opened * sin_ref[h].astype(f32)).astype(bf16) for h in heads
+    ]
+    dsts = [state[h].astype(bf16) for h in heads]
+    ddws = [dd_ref[:, c] * before for c in cols]
+    dphi_q = [mm(dsc[h], phik_ref[:, cols[h]]) + mm_t(ddws[h], sts[h]) for h in heads]
+    dphi_k = [mm(dsc_t[h], phiq_ref[:, cols[h]]) + mm_t(vals[h] * after, dsts[h]) for h in heads]
+    dvs = [mm(scores_t[h], dd_ref[:, cols[h]]) + mm(phik_ref[:, cols[h]] * after, dsts[h]) for h in heads]
+    for h in heads:
+        state[h] = keep * state[h] + mm_f(phiq_ref[:, cols[h]], ddws[h])
     for p in range(pairs):
-        two = pl.ds(p * 128, 128)
-        dphi_q, dphi_k, dvs = [], [], []
-        for j, val in enumerate(augmented(v_ref[:, two])):
-            h = 2 * p + j
-            own = pl.ds(h * 128, 128)
-            pq, pk, dd = phiq_ref[:, own], phik_ref[:, own], dd_ref[:, own]
-            scores_t = jnp.where(mask_t, mm_t(pk, pq), 0.0).astype(bf16)
-            dsc = jnp.where(mask, mm_t(dd, val), 0.0).astype(bf16)
-            dsc_t = jnp.where(mask_t, mm_t(val, dd), 0.0).astype(bf16)
-            st = (srel_ref[0, h].astype(f32) + opened * sin_ref[h].astype(f32)).astype(bf16)
-            dst = state[h]
-            dst_b = dst.astype(bf16)
-            ddw = dd * before
-            dphi_q.append(mm(dsc, pk) + mm_t(ddw, st))
-            dphi_k.append(mm(dsc_t, pq) + mm_t(val * after, dst_b))
-            dvs.append(mm(scores_t, dd) + mm(pk * after, dst_b))
-            state[h] = keep * dst + mm_f(pq, ddw)
-        dqkv_ref[:, pl.ds(2 * width + p * 128, 128)] = jnp.where(low, dvs[0], dvs[1]).astype(bf16)
-        for phi_ref, dphi, rows_ref, maps, acc, base in (
-            (phiq_ref, dphi_q, q_ref, mapq, gq, 0),
-            (phik_ref, dphi_k, k_ref, mapk, gk, width),
-        ):
-            phi = phi_ref[:, pl.ds(p * 256, 256)].astype(f32)
-            dphi = jnp.concatenate(dphi, axis=1)
-            total = mm((phi * dphi).astype(bf16), ones)
-            dlog = (phi * (dphi - total)).astype(bf16)
-            dqkv_ref[:, pl.ds(base + p * 128, 128)] = mm_t(dlog, maps[p]).astype(bf16)
-            acc[p] += mm_f(rows_ref[:, two], dlog)
+        dqkv_ref[:, pl.ds(2 * width + p * 128, 128)] = jnp.where(low, dvs[2 * p], dvs[2 * p + 1]).astype(bf16)
+    for phi_ref, dphi, rows_ref, maps, acc, base_col in (
+        (phiq_ref, dphi_q, q_ref, mapq, gq, 0),
+        (phik_ref, dphi_k, k_ref, mapk, gk, width),
+    ):
+        phis = [phi_ref[:, pl.ds(p * 256, 256)].astype(f32) for p in range(pairs)]
+        dphis = [jnp.concatenate(dphi[2 * p : 2 * p + 2], axis=1) for p in range(pairs)]
+        totals = [mm((phi * d).astype(bf16), ones) for phi, d in zip(phis, dphis)]
+        dlogs = [(phi * (d - t)).astype(bf16) for phi, d, t in zip(phis, dphis, totals)]
+        for p in range(pairs):
+            two = pl.ds(p * 128, 128)
+            dqkv_ref[:, pl.ds(base_col + p * 128, 128)] = mm_t(dlogs[p], maps[p]).astype(bf16)
+            acc[p] += mm_f(rows_ref[:, two], dlogs[p])
 
     @pl.when(step == nblk - 1)
     def _():
@@ -682,10 +695,10 @@
         functools.partial(keys_body, n_seq, pairs),
         name="keys",
         cost_estimate=cost(22),
-        grid=(tokens // TM,),
-        in_specs=[smem(), smem(), rows_spec(TM, width), rows_spec(TM, 1)] + [whole()] * 2,
-        out_specs=[rows_spec(TM, width)] * 3
-        + [rows_spec(TM, 2 * width), full_spec(packed), full_spec((8, width)), full_spec((width, 128))],
+        grid=(tokens // TK,),
+        in_specs=[smem(), smem(), rows_spec(TK, width), rows_spec(TK, 1)] + [whole()] * 2,
+        out_specs=[rows_spec(TK, width)] * 3
+        + [rows_spec(TK, 2 * width), full_spec(packed), full_spec((8, width)), full_spec((width, 128))],
         out_shape=[sds((tokens, width), bf16)] * 3
         + [sds((tokens, 2 * width), bf16), sds(packed, bf16), sds((8, width), f32), sds((width, 128), bf16)],
         scratch_shapes=[
@@ -722,7 +735,7 @@
         local = pl.pallas_call(
             functools.partial(local_body, base, pairs),
             name="local",
-            cost_estimate=cost(19),
+            cost_estimate=cost(15),
             grid=(part_blk,),
             in_specs=[
                 smem(), smem(), here(BT, width), here(BT, 2 * width), here(BT, width), here(BT, 1),
@@ -823,7 +836,7 @@
         d_one, g_one = pl.pallas_call(
             functools.partial(back_body, g * some, some, pairs),
             name="back",
-            cost_estimate=cost(22),
+            cost_estimate=cost(19),
             grid=(nblk,),
             in_specs=[
                 smem(), smem(), smem(), spec(part), spec(part), spec(part), spec(2 * part), spec(2 * part),
@@ -870,11 +883,11 @@
         functools.partial(enter_body, groups),
         name="enter",
         cost_estimate=cost(11),
-        grid=(tokens // TM,),
-        in_specs=[smem(), rows_spec(TM, width), rows_spec(TM, width), full_spec((8, width))]
-        + [rows_spec(TM, 3 * part)] * groups
+        grid=(tokens // TK,),
+        in_specs=[smem(), rows_spec(TK, width), rows_spec(TK, width), full_spec((8, width))]
+        + [rows_spec(TK, 3 * part)] * groups
         + [whole()] * 2,
-        out_specs=[rows_spec(TM, width), full_spec((8, width))],
+        out_specs=[rows_spec(TK, width), full_spec((8, width))],
         out_shape=[sds((tokens, width), f32), sds((8, width), f32)],
         scratch_shapes=[pltpu.VMEM((width, 3 * width), bf16), dma(2, n_seq)],
         compiler_params=cparams(),

time: 385 us -> 358 us (0.930)
  Pallas kernels: 171 us -> 121 us
  waiting for transfers between devices: 59.1 us -> 76.4 us
  starting transfers between devices: 62.5 us -> 67.7 us
    pallas_call x2, Pallas kernels: 43 us -> 21.2 us  [shards(): pl.pallas_call(functools.partial(local_body, base, pairs), name='local',...]
    pallas_call x2, Pallas kernels: 50.4 us -> 29.9 us  [shards(): pl.pallas_call(functools.partial(back_body, g * some, some, pairs), name=...]
    ppermute x39, waiting for transfers between devices: 13.4 us -> 30.8 us  [xor_send(): return lax.ppermute(arr, 'seq', [(i, i ^ mask) for i in range(size)])]
    pallas_call x1, Pallas kernels: 21.9 us -> 13.7 us  [shards(): pl.pallas_call(functools.partial(keys_body, n_seq, pairs), name='keys', c...]
    ppermute x39, starting transfers between devices: 42.2 us -> 47.3 us  [xor_send(): return lax.ppermute(arr, 'seq', [(i, i ^ mask) for i in range(size)])]
    unnamed x103 -> x105, local copies, waits for them, and re-layouts: 11.1 us -> 12.3 us
  transfers between devices with their start and end apart: 57 -> 57, of which waited for: 14 -> 16; matrix products, arithmetic and copies ran while one was open for 19% -> 20% of each run, Pallas kernels for 33% -> 22%
where the time goes in v3:
time: 358 us; the launch traced here: 354 us
  Pallas kernels  121 us (34%)
  waiting for transfers between devices  76.4 us (21%)
  starting transfers between devices  67.7 us (19%)
  other arithmetic  33.7 us (9%)
  local copies, waits for them, and re-layouts  28.1 us (8%)
  matrix products  24.1 us (7%)
    ppermute x39, starting transfers between devices, xor_send(): return lax.ppermute(arr, 'seq', [(i, i ^ mask) for i in range(size)])  47.3 us
    pallas_call x1, Pallas kernels, shards(): pl.pallas_call(functools.partial(middle_body, n_seq, pairs), name='middle...  43.2 us
    ppermute x39, waiting for transfers between devices, xor_send(): return lax.ppermute(arr, 'seq', [(i, i ^ mask) for i in range(size)])  30.8 us
    pallas_call x2, Pallas kernels, shards(): pl.pallas_call(functools.partial(back_body, g * some, some, pairs), name=...  29.9 us
    ppermute x9, waiting for transfers between devices, send_stream(): lax.ppermute(piece, 'stream', [(i, (i + d) % depth) for i in range(depth)])  28.2 us
    dot_general x5, matrix products, mm_f(): lax.dot_general(a, b, (((0,), (0,)), ((), ())), preferred_element_type=f32)  23.9 us
    pallas_call x2, Pallas kernels, shards(): pl.pallas_call(functools.partial(local_body, base, pairs), name='local',...  21.2 us
    ppermute x9, waiting for transfers between devices, stream_send(): lax.ppermute(shard, 'stream', [(i, (i + d) % depth) for i in range(depth)])  17.4 us
  transfers between devices with their start and end apart: 57, of which 16 were waited for; matrix products, arithmetic and copies ran while one was open for 20% of the time, Pallas kernels for 22%

profile of v3, /device:TPU:9, one launch (start us, length us, event | category | flops | bytes accessed | tf_op | source)
XLA Modules:
  0.0 354.0 jit_solution(825685459520811998)
XLA Ops:
  2.1 1.3 reduce_max.9
  5.2 2.5 collective-permute-start.1
  7.7 2.2 collective-permute-start.2
  11.2 3.5 collective-permute-done.1
  14.7 3.2 collective-permute-done.2
  18.0 1.3 collective-permute-start.3
  19.3 1.2 collective-permute-start.4
  21.7 8.0 %collective-permute-done.3 = bf16[96,2560]{1,0:T(8,128)(2,1)S(1)} collective-permute-done((bf16[96,2560]{1,0:T(8,128)(2,1)S(1)}, bf16[96,2560]{1,0:T(8,128)(2,1)S(1)}, u32[]{:S(2)}, u32[]{:S(2)}) %collective-permute-start.3) | collective-permute-done | bytes 491552 | tf_op jit(solution)/shard_map/ppermute | solution.py:34
  29.7 1.3 collective-permute-start.6
  31.0 1.3 collective-permute-start.7
  32.4 3.4 collective-permute-start.5
  36.7 3.3 collective-permute-start.10
  40.0 10.7 %collective-permute-done.5 = bf16[24,3840]{1,0:T(8,128)(2,1)S(1)} collective-permute-done((bf16[24,3840]{1,0:T(8,128)(2,1)S(1)}, bf16[24,3840]{1,0:T(8,128)(2,1)S(1)}, u32[]{:S(2)}, u32[]{:S(2)}) %collective-permute-start.5) | collective-permute-done | bytes 184352 | tf_op jit(solution)/shard_map/ppermute | solution.py:43
  52.2 1.2 copy-done.26
  54.2 13.7 %keys.1 = (bf16[1024,768]{1,0:T(8,128)(2,1)}, bf16[1024,768]{1,0:T(8,128)(2,1)}, bf16[1024,768]{1,0:T(8,128)(2,1)}, bf16[1024,1536]{1,0:T(8,128)(2,1)}, bf16[7,1...) custom-call(s32[1]{0:T(128)} %bitcast.me_ref, f32[5]{0:T(128)} %copy-done.25, ...), custom_call_target="tpu_custom_call" | custom-call | flops 11000000512 | bytes 22000000 | tf_op jit(solution)/shard_map/keys/pallas_call | solution.py:694
  71.2 1.2 collective-permute-start.18
  72.4 10.2 %local.2 = (bf16[1024,768]{1,0:T(8,128)(2,1)}, bf16[1024,1536]{1,0:T(8,128)(2,1)}, f32[1024,768]{1,0:T(8,128)}, f32[1024,768]{1,0:T(8,128)}, bf16[4,12,128,128]{3,2,1,0:T(8,128)(2,1)}, /*index=5*/f32[12,128,128]{2,1,0:T(8,128)}) custom-call(s32[1]{0:T(128)} %bitcast.me_ref, f32[5]{0:T(128)} %copy-done.25, bf16[1024,768]{1,0:T(8,128)(2,1)} %get-tuple-element.148.h_ref, ...), custom_call_target="tpu_custom_call" | custom-call | flops 7500000256 | bytes 15000000 | tf_op jit(solution)/shard_map/local/pallas_call | solution.py:735
  83.0 1.2 collective-permute-start.21
  84.2 2.7 collective-permute-done.13
  87.8 1.5 pad_maximum_fusion.refs_0_
  89.3 10.0 %collective-permute-start.22 = (bf16[4,96,3840]{2,1,0:T(8,128)(2,1)S(1)}, bf16[4,96,3840]{2,1,0:T(8,128)(2,1)}, u32[]{:S(2)}, u32[]{:S(2)}) collective-permute-start(bf16[4,96,3840]{2,1,0:T(8,128)(2,1)S(1)} %pad_maximum_fusion.refs_0_), channel_id=1, source_target_pairs={{0,4},{4,0},{8,12},{12,8},{16,20},{20,16},{24,28},{28,24},{1,5},{5... | collective-permute-start | bytes 8847368 | tf_op jit(solution)/shard_map/ppermute | solution.py:34
  100.6 11.0 %local.3 = (bf16[1024,768]{1,0:T(8,128)(2,1)}, bf16[1024,1536]{1,0:T(8,128)(2,1)}, f32[1024,768]{1,0:T(8,128)}, f32[1024,768]{1,0:T(8,128)}, bf16[4,12,128,128]{3,2,1,0:T(8,128)(2,1)}, /*index=5*/f32[12,128,128]{2,1,0:T(8,128)}) custom-call(s32[1]{0:T(128)} %bitcast.me_ref, ...), custom_call_target="tpu_custom_call", output_to_operand_aliasing={{0}: (11, {}), {1}: (12, {}), {2}: (13, {}), {3}: (14, {}),... | custom-call | flops 7500000256 | bytes 15000000 | tf_op jit(solution)/shard_map/local/pallas_call | solution.py:735
  111.7 3.0 pad_maximum_fusion.1.refs_2_
  114.7 5.1 %collective-permute-start.24 = (bf16[4,384,768]{2,1,0:T(8,128)(2,1)}, bf16[4,384,768]{2,1,0:T(8,128)(2,1)}, u32[]{:S(2)}, u32[]{:S(2)}) collective-permute-start(bf16[4,384,768]{2,1,0:T(8,128)(2,1)} %pad_maximum_fusion.1.refs_2_), channel_id=1, source_target_pairs={{0,4},{4,0},{8,12},{12,8},{16,20},{20,16},{24,28},{28,24},{1,5},{5... | collective-permute-start | bytes 7077896 | tf_op jit(solution)/shard_map/ppermute | solution.py:34
  119.8 2.1 pad_maximum_fusion.6.refs_4_
  123.4 2.3 collective-permute-done.25.refs_5_
  125.7 43.2 %middle.1 = (bf16[1024,768]{1,0:T(8,128)(2,1)}, bf16[1024,768]{1,0:T(8,128)(2,1)}, bf16[1024,768]{1,0:T(8,128)(2,1)}, bf16[1024,3072]{1,0:T(8,128)(2,1)}, bf16[1...) custom-call(s32[1]{0:T(128)} %bitcast.me_ref, ...), custom_call_target="tpu_custom_call" | custom-call | flops 21500000256 | bytes 43000000 | tf_op jit(solution)/shard_map/middle/pallas_call | solution.py:771
  173.0 8.7 %convolution_convert_fusion.1 = bf16[3072,768]{1,0:T(8,128)(2,1)S(1)} fusion(bf16[1024,3072]{1,0:T(8,128)(2,1)} %get-tuple-element.130, bf16[1,1024,768]{2,1,0:T(8,128)(2,1)S(1)} %copy-done.27), kind=kOutput, calls=%fused_computation.1 | convolution fusion | flops 4834197504 | bytes 12582912 | tf_op jit(solution)/shard_map/dot_general | solution.py:30
  181.8 2.0 copy-done.1
  184.2 5.5 %convolution_convert_fusion = bf16[768,3072]{1,0:T(8,128)(2,1)S(1)} fusion(bf16[1024,768]{1,0:T(8,128)(2,1)S(1)} %copy-done.33, bf16[1024,3072]{1,0:T(8,128)(2,1)S(1)} %copy-done.29), kind=kOutput, calls=%fused_computation | convolution fusion | flops 4834197504 | bytes 12582912 | tf_op jit(solution)/shard_map/dot_general | solution.py:30
  189.8 1.6 dynamic-slice_bitcast_fusion
  191.4 1.3 copy-done
  194.0 5.8 %collective-permute-done.31 = bf16[7,128,128]{2,1,0:T(8,128)(2,1)} collective-permute-done((bf16[7,128,128]{2,1,0:T(8,128)(2,1)S(1)}, bf16[7,128,128]{2,1,0:T(8,128)(2,1)}, u32[]{:S(2)}, u32[]{:S(2)}) %collective-permute-start.31) | collective-permute-done | bytes 229408 | tf_op jit(solution)/shard_map/ppermute | solution.py:34
  200.9 1.3 collective-permute-start.32
  202.2 3.0 convolution_convert_fusion.4
  206.2 2.2 fusion.1
  209.5 1.2 collective-permute-start.29
  211.7 15.0 %back.2 = (bf16[1024,1152]{1,0:T(8,128)(2,1)}, bf16[384,128]{1,0:T(8,128)(2,1)}) custom-call(s32[1]{0:T(128)} %bitcast.me_ref, f32[8]{0:T(128)} %bitcast.250, f32[5]{0:T(128)} %copy-done.25, bf16[1024,768]{1,0:T(8,128)(2,1)} %get-tuple-element.141.q_ref, bf16[1024,768]{1,0:T(8,128)(2,1)} %get-tuple-element.142.k_ref, ...), custom_call_target="tpu_custom_call" | custom-call | flops 9500000256 | bytes 19000000 | tf_op jit(solution)/shard_map/back/pallas_call | solution.py:836
  227.0 10.2 %collective-permute-done.55 = f32[3]{0:T(128)S(1)} collective-permute-done((f32[3]{0:T(128)S(1)}, f32[3]{0:T(128)S(1)}, u32[]{:S(2)}, u32[]{:S(2)}) %collective-permute-start.55) | collective-permute-done | bytes 44 | tf_op jit(solution)/shard_map/ppermute | solution.py:34
  237.2 3.4 fusion
  241.8 1.2 collective-permute-start.35
  243.0 2.3 convolution_convert_fusion.3
  246.3 1.4 pad_maximum_fusion.3
  247.8 1.3 collective-permute-start.34
  249.1 1.5 fusion.3
  252.0 14.9 %back.3 = (bf16[1024,1152]{1,0:T(8,128)(2,1)}, bf16[384,128]{1,0:T(8,128)(2,1)}) custom-call(s32[1]{0:T(128)} %bitcast.me_ref, f32[8]{0:T(128)} %bitcast.251, f32[5]{0:T(128)} %copy-done.25, bf16[1024,768]{1,0:T(8,128)(2,1)} %get-tuple-element.141.q_ref, bf16[1024,768]{1,0:T(8,128)(2,1)} %get-tuple-element.142.k_ref, ...), custom_call_target="tpu_custom_call" | custom-call | flops 9500000256 | bytes 19000000 | tf_op jit(solution)/shard_map/back/pallas_call | solution.py:836
  266.9 4.4 %convolution_convert_fusion.2 = bf16[768,1152]{1,0:T(8,128)(2,1)S(1)} fusion(bf16[1024,768]{1,0:T(8,128)(2,1)} %get-tuple-element.148.h_ref, bf16[1024,1152]{1,0:T(8,128)(2,1)} %get-tuple-element.152.refs_1_), kind=kOutput, calls=%fused_computation.6 | convolution fusion | flops 1812824064 | bytes 5701632 | tf_op jit(solution)/shard_map/dot_general | solution.py:30
  271.3 1.3 collective-permute-start.56
  276.6 1.7 fusion.2
  279.5 1.9 add_convert_fusion
  284.3 13.3 %enter.1 = (f32[1024,768]{1,0:T(8,128)}, f32[8,768]{1,0:T(8,128)}) custom-call(s32[1]{0:T(128)} %bitcast.me_ref, bf16[1024,768]{1,0:T(8,128)(2,1)} %bitcast.255, f32[1024,768]{1,0:T(8,128)} %get-tuple-element.159.dr_ref, f32[8,768]{1,0:T(8,128)} %get-tuple-element.99.gb_ref, bf16[1024,1152]{1,0:T(8,128)(2,1)} %get-tuple-element.146.refs_0_, ...), custom_call_target="tpu_custom_call" | custom-call | flops 5500000256 | bytes 11000000 | tf_op jit(solution)/shard_map/enter/pallas_call | solution.py:882
  300.4 4.2 %collective-permute-start.52 = (bf16[96,768]{1,0:T(8,128)(2,1)S(1)}, bf16[96,768]{1,0:T(8,128)(2,1)S(1)}, u32[]{:S(2)}, u32[]{:S(2)}) collective-permute-start(bf16[96,768]{1,0:T(8,128)(2,1)S(1)} %get-tuple-element.219), channel_id=1, source_target_pairs={{0,2},{1,3},{2,0},{3,1},{4,6},{5,7},{6,4},{7,5},{8,10},{9,11},{10,... | collective-permute-start | bytes 442376 | tf_op jit(solution)/shard_map/ppermute | solution.py:150
  304.6 1.5 add_convert_fusion.1
  309.7 4.2 %collective-permute-done.52 = bf16[96,768]{1,0:T(8,128)(2,1)S(1)} collective-permute-done((bf16[96,768]{1,0:T(8,128)(2,1)S(1)}, bf16[96,768]{1,0:T(8,128)(2,1)S(1)}, u32[]{:S(2)}, u32[]{:S(2)}) %collective-permute-start.52) | collective-permute-done | bytes 147488 | tf_op jit(solution)/shard_map/ppermute | solution.py:150
  313.9 3.3 collective-permute-done.53
  318.2 1.4 collective-permute-start.50
  319.5 1.4 fusion.4
  323.7 5.7 %collective-permute-done.49 = bf16[24,3072]{1,0:T(8,128)(2,1)S(1)} collective-permute-done((bf16[24,3072]{1,0:T(8,128)(2,1)S(1)}, bf16[24,3072]{1,0:T(8,128)(2,1)S(1)}, u32[]{:S(2)}, u32[]{:S(2)}) %collective-permute-start.49) | collective-permute-done | bytes 147488 | tf_op jit(solution)/shard_map/ppermute | solution.py:150
  329.3 2.0 collective-permute-done.50
  331.4 1.2 collective-permute-done.42
  332.9 1.5 collective-permute-start.45
  334.5 3.1 collective-permute-start.46
  338.3 9.8 %collective-permute-done.46 = bf16[24,3456]{1,0:T(8,128)(2,1)S(1)} collective-permute-done((bf16[24,3456]{1,0:T(8,128)(2,1)S(1)}, bf16[24,3456]{1,0:T(8,128)(2,1)S(1)}, u32[]{:S(2)}, u32[]{:S(2)}) %collective-permute-start.46) | collective-permute-done | bytes 165920 | tf_op jit(solution)/shard_map/ppermute | solution.py:150
  348.1 3.2 collective-permute-done.47
  (270 shorter events, 50.8 us)
Async XLA Ops:
  5.1 6.0 %collective-permute-start = (bf16[24,2560]{1,0:T(8,128)(2,1)S(1)}, bf16[24,2560]{1,0:T(8,128)(2,1)S(1)}, u32[]{:S(2)}, u32[]{:S(2)}) collective-permute-start(bf16[24,2560]{1,0:T(8,128)(2,1)S(1)} %concatenate.61), channel_id=1, source_target_pairs={{0,3},{1,0},{2,1},{3,2},{4,7},{5,4},{6,5},{7,6},{8,11},{9,8},{10,9... | collective-permute-start | bytes 368648 | tf_op jit(solution)/shard_map/ppermute | solution.py:43
  5.2 9.5 %collective-permute-start.1 = (bf16[24,2560]{1,0:T(8,128)(2,1)S(1)}, bf16[24,2560]{1,0:T(8,128)(2,1)S(1)}, u32[]{:S(2)}, u32[]{:S(2)}) collective-permute-start(bf16[24,2560]{1,0:T(8,128)(2,1)S(1)} %concatenate.61), channel_id=1, source_target_pairs={{0,2},{1,3},{2,0},{3,1},{4,6},{5,7},{6,4},{7,5},{8,10},{9,11},{10,... | collective-permute-start | bytes 368648 | tf_op jit(solution)/shard_map/ppermute | solution.py:43
  7.7 10.2 %collective-permute-start.2 = (bf16[24,2560]{1,0:T(8,128)(2,1)S(1)}, bf16[24,2560]{1,0:T(8,128)(2,1)S(1)}, u32[]{:S(2)}, u32[]{:S(2)}) collective-permute-start(bf16[24,2560]{1,0:T(8,128)(2,1)S(1)} %concatenate.61), channel_id=1, source_target_pairs={{0,1},{1,2},{2,3},{3,0},{4,5},{5,6},{6,7},{7,4},{8,9},{9,10},{10,1... | collective-permute-start | bytes 368648 | tf_op jit(solution)/shard_map/ppermute | solution.py:43
  11.1 10.6 %copy-start.25 = (f32[5]{0:T(128)}, f32[5]{0:T(128)S(1)}, u32[]{:S(2)}) copy-start(f32[5]{0:T(128)S(1)} %pad_maximum_fusion.16.cend_ref) | copy-start | bytes 64
  11.1 10.5 %copy-start.19 = (bf16[24,3072]{1,0:T(8,128)(2,1)S(1)}, bf16[24,3072]{1,0:T(8,128)(2,1)}, u32[]{:S(2)}) copy-start(bf16[24,3072]{1,0:T(8,128)(2,1)} %param.17) | copy-start | bytes 442372
  18.0 11.6 %collective-permute-start.3 = (bf16[96,2560]{1,0:T(8,128)(2,1)S(1)}, bf16[96,2560]{1,0:T(8,128)(2,1)S(1)}, u32[]{:S(2)}, u32[]{:S(2)}) collective-permute-start(bf16[96,2560]{1,0:T(8,128)(2,1)S(1)} %constant_dynamic-slice_fusion.3), channel_id=1, source_target_pairs={{0,8},{4,12},{8,0},{12,4},{16,24},{20,28},{24,16},{28,20},{1,9},{5... | collective-permute-start | bytes 1474568 | tf_op jit(solution)/shard_map/ppermute | solution.py:34
  19.3 11.7 %collective-permute-start.4 = (bf16[96,2560]{1,0:T(8,128)(2,1)S(1)}, bf16[96,2560]{1,0:T(8,128)(2,1)S(1)}, u32[]{:S(2)}, u32[]{:S(2)}) collective-permute-start(bf16[96,2560]{1,0:T(8,128)(2,1)S(1)} %constant_dynamic-slice_fusion.3), channel_id=1, source_target_pairs={{0,16},{4,20},{8,24},{12,28},{16,0},{20,4},{24,8},{28,12},{1,17},{... | collective-permute-start | bytes 1474568 | tf_op jit(solution)/shard_map/ppermute | solution.py:34
  20.6 15.8 %copy-start.23 = (f32[1,1,4,256]{3,1,2,0:T(1,128)}, f32[1,1,4,256]{3,1,2,0:T(1,128)S(1)}, u32[]{:S(2)}) copy-start(f32[1,1,4,256]{3,1,2,0:T(1,128)S(1)} %copy.126) | copy-start | bytes 12292
  29.7 6.1 %collective-permute-start.6 = (bf16[96,1280]{1,0:T(8,128)(2,1)S(1)}, bf16[96,1280]{1,0:T(8,128)(2,1)S(1)}, u32[]{:S(2)}, u32[]{:S(2)}) collective-permute-start(bf16[96,1280]{1,0:T(8,128)(2,1)S(1)} %slice.119), channel_id=1, source_target_pairs={{0,16},{4,20},{8,24},{12,28},{16,0},{20,4},{24,8},{28,12},{1,17},{... | collective-permute-start | bytes 737288 | tf_op jit(solution)/shard_map/ppermute | solution.py:34
  31.0 5.4 %collective-permute-start.7 = (bf16[96,1280]{1,0:T(8,128)(2,1)S(1)}, bf16[96,1280]{1,0:T(8,128)(2,1)S(1)}, u32[]{:S(2)}, u32[]{:S(2)}) collective-permute-start(bf16[96,1280]{1,0:T(8,128)(2,1)S(1)} %slice.120), channel_id=1, source_target_pairs={{0,8},{4,12},{8,0},{12,4},{16,24},{20,28},{24,16},{28,20},{1,9},{5... | collective-permute-start | bytes 737288 | tf_op jit(solution)/shard_map/ppermute | solution.py:34
  32.3 18.4 %collective-permute-start.8 = (bf16[24,3840]{1,0:T(8,128)(2,1)S(1)}, bf16[24,3840]{1,0:T(8,128)(2,1)S(1)}, u32[]{:S(2)}, u32[]{:S(2)}) collective-permute-start(bf16[24,3840]{1,0:T(8,128)(2,1)S(1)} %pad_maximum_fusion.11), channel_id=1, source_target_pairs={{0,2},{1,3},{2,0},{3,1},{4,6},{5,7},{6,4},{7,5},{8,10},{9,11},{10,... | collective-permute-start | bytes 552968 | tf_op jit(solution)/shard_map/ppermute | solution.py:43
  32.4 18.3 %collective-permute-start.5 = (bf16[24,3840]{1,0:T(8,128)(2,1)S(1)}, bf16[24,3840]{1,0:T(8,128)(2,1)S(1)}, u32[]{:S(2)}, u32[]{:S(2)}) collective-permute-start(bf16[24,3840]{1,0:T(8,128)(2,1)S(1)} %pad_maximum_fusion.11), channel_id=1, source_target_pairs={{0,3},{1,0},{2,1},{3,2},{4,7},{5,4},{6,5},{7,6},{8,11},{9,8},{10,9... | collective-permute-start | bytes 552968 | tf_op jit(solution)/shard_map/ppermute | solution.py:43
  35.8 15.0 %collective-permute-start.9 = (bf16[24,3840]{1,0:T(8,128)(2,1)S(1)}, bf16[24,3840]{1,0:T(8,128)(2,1)S(1)}, u32[]{:S(2)}, u32[]{:S(2)}) collective-permute-start(bf16[24,3840]{1,0:T(8,128)(2,1)S(1)} %pad_maximum_fusion.11), channel_id=1, source_target_pairs={{0,1},{1,2},{2,3},{3,0},{4,5},{5,6},{6,7},{7,4},{8,9},{9,10},{10,1... | collective-permute-start | bytes 552968 | tf_op jit(solution)/shard_map/ppermute | solution.py:43
  36.7 14.3 %copy-start.8 = (bf16[4,96,2560]{2,1,0:T(8,128)(2,1)}, bf16[4,96,2560]{2,1,0:T(8,128)(2,1)S(1)}, u32[]{:S(2)}) copy-start(bf16[4,96,2560]{2,1,0:T(8,128)(2,1)S(1)} %pad_maximum_fusion.2.refs_0_.refs_2_) | copy-start | bytes 5898244
  36.7 15.4 %collective-permute-start.10 = (bf16[4,96,2560]{2,1,0:T(8,128)(2,1)S(1)}, bf16[4,96,2560]{2,1,0:T(8,128)(2,1)S(1)}, u32[]{:S(2)}, u32[]{:S(2)}) collective-permute-start(bf16[4,96,2560]{2,1,0:T(8,128)(2,1)S(1)} %pad_maximum_fusion.2.refs_0_.refs_2_), channel_id=1, source_target_pairs={{0,4},{4,0},{8,12},{12,8},{16,20},{20,16},{24,28},{28,24},{1,5},{5... | collective-permute-start | bytes 5898248 | tf_op jit(solution)/shard_map/ppermute | solution.py:34
  51.0 17.0 %collective-permute-start.11 = (bf16[96,3840]{1,0:T(8,128)(2,1)S(1)}, bf16[96,3840]{1,0:T(8,128)(2,1)S(1)}, u32[]{:S(2)}, u32[]{:S(2)}) collective-permute-start(bf16[96,3840]{1,0:T(8,128)(2,1)S(1)} %constant_dynamic-slice_fusion.2), channel_id=1, source_target_pairs={{0,8},{4,12},{8,0},{12,4},{16,24},{20,28},{24,16},{28,20},{1,9},{5... | collective-permute-start | bytes 2211848 | tf_op jit(solution)/shard_map/ppermute | solution.py:34
  51.3 31.7 %collective-permute-start.12 = (bf16[96,3840]{1,0:T(8,128)(2,1)S(1)}, bf16[96,3840]{1,0:T(8,128)(2,1)S(1)}, u32[]{:S(2)}, u32[]{:S(2)}) collective-permute-start(bf16[96,3840]{1,0:T(8,128)(2,1)S(1)} %constant_dynamic-slice_fusion.2), channel_id=1, source_target_pairs={{0,16},{4,20},{8,24},{12,28},{16,0},{20,4},{24,8},{28,12},{1,17},{... | collective-permute-start | bytes 2211848 | tf_op jit(solution)/shard_map/ppermute | solution.py:34
  52.2 16.5 %collective-permute-start.16 = (bf16[96,768]{1,0:T(8,128)(2,1)S(1)}, bf16[96,768]{1,0:T(8,128)(2,1)S(1)}, u32[]{:S(2)}, u32[]{:S(2)}) collective-permute-start(bf16[96,768]{1,0:T(8,128)(2,1)S(1)} %copy-done.14), channel_id=1, source_target_pairs={{0,1},{1,2},{2,3},{3,0},{4,5},{5,6},{6,7},{7,4},{8,9},{9,10},{10,1... | collective-permute-start | bytes 442376 | tf_op jit(solution)/shard_map/ppermute | solution.py:43
  53.5 16.0 %collective-permute-start.15 = (bf16[96,768]{1,0:T(8,128)(2,1)S(1)}, bf16[96,768]{1,0:T(8,128)(2,1)S(1)}, u32[]{:S(2)}, u32[]{:S(2)}) collective-permute-start(bf16[96,768]{1,0:T(8,128)(2,1)S(1)} %copy-done.14), channel_id=1, source_target_pairs={{0,2},{1,3},{2,0},{3,1},{4,6},{5,7},{6,4},{7,5},{8,10},{9,11},{10,... | collective-permute-start | bytes 442376 | tf_op jit(solution)/shard_map/ppermute | solution.py:43
  53.5 16.0 %collective-permute-start.14 = (bf16[96,768]{1,0:T(8,128)(2,1)S(1)}, bf16[96,768]{1,0:T(8,128)(2,1)S(1)}, u32[]{:S(2)}, u32[]{:S(2)}) collective-permute-start(bf16[96,768]{1,0:T(8,128)(2,1)S(1)} %copy-done.14), channel_id=1, source_target_pairs={{0,3},{1,0},{2,1},{3,2},{4,7},{5,4},{6,5},{7,6},{8,11},{9,8},{10,9... | collective-permute-start | bytes 442376 | tf_op jit(solution)/shard_map/ppermute | solution.py:43
  68.0 14.7 %collective-permute-start.20 = (bf16[7,128,128]{2,1,0:T(8,128)(2,1)}, bf16[7,128,128]{2,1,0:T(8,128)(2,1)}, u32[]{:S(2)}, u32[]{:S(2)}) collective-permute-start(bf16[7,128,128]{2,1,0:T(8,128)(2,1)} %get-tuple-element.107), channel_id=1, source_target_pairs={{0,16},{4,20},{8,24},{12,28},{16,0},{20,4},{24,8},{28,12},{1,17},{... | collective-permute-start | bytes 688136 | tf_op jit(solution)/shard_map/ppermute | solution.py:34
  68.7 18.2 %collective-permute-start.13 = (bf16[96,3840]{1,0:T(8,128)(2,1)S(1)}, bf16[96,3840]{1,0:T(8,128)(2,1)S(1)}, u32[]{:S(2)}, u32[]{:S(2)}) collective-permute-start(bf16[96,3840]{1,0:T(8,128)(2,1)S(1)} %collective-permute-done.11), channel_id=1, source_target_pairs={{0,16},{4,20},{8,24},{12,28},{16,0},{20,4},{24,8},{28,12},{1,17},{... | collective-permute-start | bytes 2211848 | tf_op jit(solution)/shard_map/ppermute | solution.py:34
  70.5 28.8 %collective-permute-start.17 = (bf16[384,768]{1,0:T(8,128)(2,1)}, bf16[384,768]{1,0:T(8,128)(2,1)}, u32[]{:S(2)}, u32[]{:S(2)}) collective-permute-start(bf16[384,768]{1,0:T(8,128)(2,1)} %constant_dynamic-slice_fusion), channel_id=1, source_target_pairs={{0,8},{4,12},{8,0},{12,4},{16,24},{20,28},{24,16},{28,20},{1,9},{5... | collective-permute-start | bytes 1769480 | tf_op jit(solution)/shard_map/ppermute | solution.py:34
  71.2 28.8 %collective-permute-start.18 = (bf16[384,768]{1,0:T(8,128)(2,1)}, bf16[384,768]{1,0:T(8,128)(2,1)}, u32[]{:S(2)}, u32[]{:S(2)}) collective-permute-start(bf16[384,768]{1,0:T(8,128)(2,1)} %constant_dynamic-slice_fusion), channel_id=1, source_target_pairs={{0,16},{4,20},{8,24},{12,28},{16,0},{20,4},{24,8},{28,12},{1,17},{... | collective-permute-start | bytes 1769480 | tf_op jit(solution)/shard_map/ppermute | solution.py:34
  82.7 16.6 %collective-permute-start.19 = (bf16[7,128,128]{2,1,0:T(8,128)(2,1)}, bf16[7,128,128]{2,1,0:T(8,128)(2,1)S(1)}, u32[]{:S(2)}, u32[]{:S(2)}) collective-permute-start(bf16[7,128,128]{2,1,0:T(8,128)(2,1)} %get-tuple-element.107), channel_id=1, source_target_pairs={{0,8},{4,12},{8,0},{12,4},{16,24},{20,28},{24,16},{28,20},{1,9},{5... | collective-permute-start | bytes 688136 | tf_op jit(solution)/shard_map/ppermute | solution.py:34
  83.0 16.3 %collective-permute-start.21 = (bf16[7,128,128]{2,1,0:T(8,128)(2,1)}, bf16[7,128,128]{2,1,0:T(8,128)(2,1)S(1)}, u32[]{:S(2)}, u32[]{:S(2)}) collective-permute-start(bf16[7,128,128]{2,1,0:T(8,128)(2,1)} %collective-permute-done.20), channel_id=1, source_target_pairs={{0,8},{4,12},{8,0},{12,4},{16,24},{20,28},{24,16},{28,20},{1,9},{5... | collective-permute-start | bytes 688136 | tf_op jit(solution)/shard_map/ppermute | solution.py:34
  89.3 22.3 %copy-start.6 = (bf16[4,96,3840]{2,1,0:T(8,128)(2,1)}, bf16[4,96,3840]{2,1,0:T(8,128)(2,1)S(1)}, u32[]{:S(2)}) copy-start(bf16[4,96,3840]{2,1,0:T(8,128)(2,1)S(1)} %pad_maximum_fusion.refs_0_) | copy-start | bytes 8847364
  89.3 36.3 %collective-permute-start.22 = (bf16[4,96,3840]{2,1,0:T(8,128)(2,1)S(1)}, bf16[4,96,3840]{2,1,0:T(8,128)(2,1)}, u32[]{:S(2)}, u32[]{:S(2)}) collective-permute-start(bf16[4,96,3840]{2,1,0:T(8,128)(2,1)S(1)} %pad_maximum_fusion.refs_0_), channel_id=1, source_target_pairs={{0,4},{4,0},{8,12},{12,8},{16,20},{20,16},{24,28},{28,24},{1,5},{5... | collective-permute-start | bytes 8847368 | tf_op jit(solution)/shard_map/ppermute | solution.py:34
  100.0 11.6 %collective-permute-start.23 = (bf16[384,768]{1,0:T(8,128)(2,1)}, bf16[384,768]{1,0:T(8,128)(2,1)S(1)}, u32[]{:S(2)}, u32[]{:S(2)}) collective-permute-start(bf16[384,768]{1,0:T(8,128)(2,1)} %collective-permute-done.18), channel_id=1, source_target_pairs={{0,8},{4,12},{8,0},{12,4},{16,24},{20,28},{24,16},{28,20},{1,9},{5... | collective-permute-start | bytes 1769480 | tf_op jit(solution)/shard_map/ppermute | solution.py:34
  114.7 10.9 %collective-permute-start.24 = (bf16[4,384,768]{2,1,0:T(8,128)(2,1)}, bf16[4,384,768]{2,1,0:T(8,128)(2,1)}, u32[]{:S(2)}, u32[]{:S(2)}) collective-permute-start(bf16[4,384,768]{2,1,0:T(8,128)(2,1)} %pad_maximum_fusion.1.refs_2_), channel_id=1, source_target_pairs={{0,4},{4,0},{8,12},{12,8},{16,20},{20,16},{24,28},{28,24},{1,5},{5... | collective-permute-start | bytes 7077896 | tf_op jit(solution)/shard_map/ppermute | solution.py:34
  121.9 3.7 %collective-permute-start.25 = (bf16[4,7,128,128]{3,2,1,0:T(8,128)(2,1)}, bf16[4,7,128,128]{3,2,1,0:T(8,128)(2,1)}, u32[]{:S(2)}, u32[]{:S(2)}) collective-permute-start(bf16[4,7,128,128]{3,2,1,0:T(8,128)(2,1)} %pad_maximum_fusion.6.refs_4_), channel_id=1, source_target_pairs={{0,4},{4,0},{8,12},{12,8},{16,20},{20,16},{24,28},{28,24},{1,5},{5... | collective-permute-start | bytes 2752520 | tf_op jit(solution)/shard_map/ppermute | solution.py:34
  125.7 47.3 %copy-start.27 = (bf16[1,1024,768]{2,1,0:T(8,128)(2,1)S(1)}, bf16[1,1024,768]{2,1,0:T(8,128)(2,1)}, u32[]{:S(2)}) copy-start(bf16[1,1024,768]{2,1,0:T(8,128)(2,1)} %param.19) | copy-start | bytes 4718596
  168.9 15.0 %collective-permute-start.28 = (bf16[7,128,128]{2,1,0:T(8,128)(2,1)}, bf16[7,128,128]{2,1,0:T(8,128)(2,1)S(1)}, u32[]{:S(2)}, u32[]{:S(2)}) collective-permute-start(bf16[7,128,128]{2,1,0:T(8,128)(2,1)} %get-tuple-element.132), channel_id=1, source_target_pairs={{0,8},{4,12},{8,0},{12,4},{16,24},{20,28},{24,16},{28,20},{1,9},{5... | collective-permute-start | bytes 688136 | tf_op jit(solution)/shard_map/ppermute | solution.py:34
  169.8 14.1 %collective-permute-start.27 = (bf16[7,128,128]{2,1,0:T(8,128)(2,1)}, bf16[7,128,128]{2,1,0:T(8,128)(2,1)S(1)}, u32[]{:S(2)}, u32[]{:S(2)}) collective-permute-start(bf16[7,128,128]{2,1,0:T(8,128)(2,1)} %get-tuple-element.132), channel_id=1, source_target_pairs={{0,16},{4,20},{8,24},{12,28},{16,0},{20,4},{24,8},{28,12},{1,17},{... | collective-permute-start | bytes 688136 | tf_op jit(solution)/shard_map/ppermute | solution.py:34
  172.0 21.9 %collective-permute-start.54 = (f32[3]{0:T(128)S(1)}, f32[3]{0:T(128)S(1)}, u32[]{:S(2)}, u32[]{:S(2)}) collective-permute-start(f32[3]{0:T(128)S(1)} %slice_reduce_fusion), channel_id=1, source_target_pairs={{0,4},{4,0},{8,12},{12,8},{16,20},{20,16},{24,28},{28,24},{1,5},{5... | collective-permute-start | bytes 44 | tf_op jit(solution)/shard_map/ppermute | solution.py:34
  173.0 10.9 %copy-start.29 = (bf16[1024,3072]{1,0:T(8,128)(2,1)S(1)}, bf16[1024,3072]{1,0:T(8,128)(2,1)}, u32[]{:S(2)}) copy-start(bf16[1024,3072]{1,0:T(8,128)(2,1)} %get-tuple-element.134) | copy-start | bytes 18874372
  183.8 22.4 %collective-permute-start.26 = (bf16[2,2,384,768]{3,2,1,0:T(8,128)(2,1)S(1)}, bf16[2,2,384,768]{3,2,1,0:T(8,128)(2,1)}, u32[]{:S(2)}, u32[]{:S(2)}) collective-permute-start(bf16[2,2,384,768]{3,2,1,0:T(8,128)(2,1)S(1)} %dynamic-slice_bitcast_fusion.1), channel_id=1, source_target_pairs={{0,4},{4,0},{8,12},{12,8},{16,20},{20,16},{24,28},{28,24},{1,5},{5... | collective-permute-start | bytes 7077896 | tf_op jit(solution)/shard_map/ppermute | solution.py:34
  192.7 44.6 %collective-permute-start.30 = (bf16[2,2,96,3072]{3,2,1,0:T(8,128)(2,1)}, bf16[2,2,96,3072]{3,2,1,0:T(8,128)(2,1)}, u32[]{:S(2)}, u32[]{:S(2)}) collective-permute-start(bf16[2,2,96,3072]{3,2,1,0:T(8,128)(2,1)} %dynamic-slice_bitcast_fusion), channel_id=1, source_target_pairs={{0,4},{4,0},{8,12},{12,8},{16,20},{20,16},{24,28},{28,24},{1,5},{5... | collective-permute-start | bytes 7077896 | tf_op jit(solution)/shard_map/ppermute | solution.py:34
  192.8 7.0 %collective-permute-start.31 = (bf16[7,128,128]{2,1,0:T(8,128)(2,1)S(1)}, bf16[7,128,128]{2,1,0:T(8,128)(2,1)}, u32[]{:S(2)}, u32[]{:S(2)}) collective-permute-start(bf16[7,128,128]{2,1,0:T(8,128)(2,1)S(1)} %collective-permute-done.28), channel_id=1, source_target_pairs={{0,16},{4,20},{8,24},{12,28},{16,0},{20,4},{24,8},{28,12},{1,17},{... | collective-permute-start | bytes 688136 | tf_op jit(solution)/shard_map/ppermute | solution.py:34
  200.9 9.8 %collective-permute-start.32 = (bf16[4,7,128,128]{3,2,1,0:T(8,128)(2,1)S(1)}, bf16[4,7,128,128]{3,2,1,0:T(8,128)(2,1)S(1)}, u32[]{:S(2)}, u32[]{:S(2)}) collective-permute-start(bf16[4,7,128,128]{3,2,1,0:T(8,128)(2,1)S(1)} %pad_maximum_fusion.7.refs_0_), channel_id=1, source_target_pairs={{0,4},{4,0},{8,12},{12,8},{16,20},{20,16},{24,28},{28,24},{1,5},{5... | collective-permute-start | bytes 2752520 | tf_op jit(solution)/shard_map/ppermute | solution.py:34
  209.5 39.6 %collective-permute-start.29 = (bf16[2,384,768]{2,1,0:T(8,128)(2,1)}, bf16[2,384,768]{2,1,0:T(8,128)(2,1)}, u32[]{:S(2)}, u32[]{:S(2)}) collective-permute-start(bf16[2,384,768]{2,1,0:T(8,128)(2,1)} %dynamic-slice_bitcast_fusion.3), channel_id=1, source_target_pairs={{0,8},{4,12},{8,0},{12,4},{16,24},{20,28},{24,16},{28,20},{1,9},{5... | collective-permute-start | bytes 3538952 | tf_op jit(solution)/shard_map/ppermute | solution.py:34
  226.7 10.5 %collective-permute-start.55 = (f32[3]{0:T(128)S(1)}, f32[3]{0:T(128)S(1)}, u32[]{:S(2)}, u32[]{:S(2)}) collective-permute-start(f32[3]{0:T(128)S(1)} %add.280), channel_id=1, source_target_pairs={{0,8},{4,12},{8,0},{12,4},{16,24},{20,28},{24,16},{28,20},{1,9},{5... | collective-permute-start | bytes 44 | tf_op jit(solution)/shard_map/ppermute | solution.py:34
  241.8 34.8 %collective-permute-start.35 = (bf16[2,96,3072]{2,1,0:T(8,128)(2,1)}, bf16[2,96,3072]{2,1,0:T(8,128)(2,1)}, u32[]{:S(2)}, u32[]{:S(2)}) collective-permute-start(bf16[2,96,3072]{2,1,0:T(8,128)(2,1)} %dynamic-slice_bitcast_fusion.2), channel_id=1, source_target_pairs={{0,8},{4,12},{8,0},{12,4},{16,24},{20,28},{24,16},{28,20},{1,9},{5... | collective-permute-start | bytes 3538952 | tf_op jit(solution)/shard_map/ppermute | solution.py:34
  247.8 31.7 %collective-permute-start.34 = (bf16[2,2,96,2048]{3,2,1,0:T(8,128)(2,1)}, bf16[2,2,96,2048]{3,2,1,0:T(8,128)(2,1)}, u32[]{:S(2)}, u32[]{:S(2)}) collective-permute-start(bf16[2,2,96,2048]{3,2,1,0:T(8,128)(2,1)} %pad_maximum_fusion.3), channel_id=1, source_target_pairs={{0,4},{4,0},{8,12},{12,8},{16,20},{20,16},{24,28},{28,24},{1,5},{5... | collective-permute-start | bytes 4718600 | tf_op jit(solution)/shard_map/ppermute | solution.py:34
  251.7 31.4 %collective-permute-start.33 = (bf16[384,768]{1,0:T(8,128)(2,1)S(1)}, bf16[384,768]{1,0:T(8,128)(2,1)}, u32[]{:S(2)}, u32[]{:S(2)}) collective-permute-start(bf16[384,768]{1,0:T(8,128)(2,1)S(1)} %dynamic-slice_bitcast_fusion.11), channel_id=1, source_target_pairs={{0,16},{4,20},{8,24},{12,28},{16,0},{20,4},{24,8},{28,12},{1,17},{... | collective-permute-start | bytes 1769480 | tf_op jit(solution)/shard_map/ppermute | solution.py:34
  271.3 4.7 %collective-permute-start.56 = (f32[3]{0:T(128)S(1)}, f32[3]{0:T(128)S(1)}, u32[]{:S(2)}, u32[]{:S(2)}) collective-permute-start(f32[3]{0:T(128)S(1)} %add.281), channel_id=1, source_target_pairs={{0,16},{4,20},{8,24},{12,28},{16,0},{20,4},{24,8},{28,12},{1,17},{... | collective-permute-start | bytes 44 | tf_op jit(solution)/shard_map/ppermute | solution.py:34
  275.5 24.9 %collective-permute-start.38 = (bf16[2,2,96,1280]{3,2,0,1:T(8,128)(2,1)}, bf16[2,2,96,1280]{3,2,0,1:T(8,128)(2,1)}, u32[]{:S(2)}, u32[]{:S(2)}) collective-permute-start(bf16[2,2,96,1280]{3,2,0,1:T(8,128)(2,1)} %copy.112), channel_id=1, source_target_pairs={{0,4},{4,0},{8,12},{12,8},{16,20},{20,16},{24,28},{28,24},{1,5},{5... | collective-permute-start | bytes 2949128 | tf_op jit(solution)/shard_map/ppermute | solution.py:34
  279.2 27.2 %collective-permute-start.37 = (bf16[96,3072]{1,0:T(8,128)(2,1)}, bf16[96,3072]{1,0:T(8,128)(2,1)}, u32[]{:S(2)}, u32[]{:S(2)}) collective-permute-start(bf16[96,3072]{1,0:T(8,128)(2,1)} %dynamic-slice_bitcast_fusion.9), channel_id=1, source_target_pairs={{0,16},{4,20},{8,24},{12,28},{16,0},{20,4},{24,8},{28,12},{1,17},{... | collective-permute-start | bytes 1769480 | tf_op jit(solution)/shard_map/ppermute | solution.py:34
  282.3 35.9 %collective-permute-start.36 = (bf16[2,96,2048]{2,1,0:T(8,128)(2,1)}, bf16[2,96,2048]{2,1,0:T(8,128)(2,1)}, u32[]{:S(2)}, u32[]{:S(2)}) collective-permute-start(bf16[2,96,2048]{2,1,0:T(8,128)(2,1)} %dynamic-slice_bitcast_fusion.8), channel_id=1, source_target_pairs={{0,8},{4,12},{8,0},{12,4},{16,24},{20,28},{24,16},{28,20},{1,9},{5... | collective-permute-start | bytes 2359304 | tf_op jit(solution)/shard_map/ppermute | solution.py:34
  298.7 7.5 %collective-permute-start.39 = (bf16[2,2,96,128]{3,2,1,0:T(8,128)(2,1)S(1)}, bf16[2,2,96,128]{3,2,1,0:T(8,128)(2,1)S(1)}, u32[]{:S(2)}, u32[]{:S(2)}) collective-permute-start(bf16[2,2,96,128]{3,2,1,0:T(8,128)(2,1)S(1)} %dynamic-slice_bitcast_fusion.28), channel_id=1, source_target_pairs={{0,4},{4,0},{8,12},{12,8},{16,20},{20,16},{24,28},{28,24},{1,5},{5... | collective-permute-start | bytes 294920 | tf_op jit(solution)/shard_map/ppermute | solution.py:34
  299.3 9.2 %collective-permute-start.51 = (bf16[96,768]{1,0:T(8,128)(2,1)S(1)}, bf16[96,768]{1,0:T(8,128)(2,1)S(1)}, u32[]{:S(2)}, u32[]{:S(2)}) collective-permute-start(bf16[96,768]{1,0:T(8,128)(2,1)S(1)} %get-tuple-element.217), channel_id=1, source_target_pairs={{0,1},{1,2},{2,3},{3,0},{4,5},{5,6},{6,7},{7,4},{8,9},{9,10},{10,1... | collective-permute-start | bytes 442376 | tf_op jit(solution)/shard_map/ppermute | solution.py:150
  300.4 13.5 %collective-permute-start.52 = (bf16[96,768]{1,0:T(8,128)(2,1)S(1)}, bf16[96,768]{1,0:T(8,128)(2,1)S(1)}, u32[]{:S(2)}, u32[]{:S(2)}) collective-permute-start(bf16[96,768]{1,0:T(8,128)(2,1)S(1)} %get-tuple-element.219), channel_id=1, source_target_pairs={{0,2},{1,3},{2,0},{3,1},{4,6},{5,7},{6,4},{7,5},{8,10},{9,11},{10,... | collective-permute-start | bytes 442376 | tf_op jit(solution)/shard_map/ppermute | solution.py:150
  306.2 11.0 %collective-permute-start.53 = (bf16[96,768]{1,0:T(8,128)(2,1)S(1)}, bf16[96,768]{1,0:T(8,128)(2,1)S(1)}, u32[]{:S(2)}, u32[]{:S(2)}) collective-permute-start(bf16[96,768]{1,0:T(8,128)(2,1)S(1)} %get-tuple-element.218), channel_id=1, source_target_pairs={{0,3},{1,0},{2,1},{3,2},{4,7},{5,4},{6,5},{7,6},{8,11},{9,8},{10,9... | collective-permute-start | bytes 442376 | tf_op jit(solution)/shard_map/ppermute | solution.py:150
  306.4 14.5 %collective-permute-start.41 = (bf16[2,96,640]{2,1,0:T(8,128)(2,1)S(1)}, bf16[2,96,640]{2,1,0:T(8,128)(2,1)S(1)}, u32[]{:S(2)}, u32[]{:S(2)}) collective-permute-start(bf16[2,96,640]{2,1,0:T(8,128)(2,1)S(1)} %dynamic-slice_bitcast_fusion.16), channel_id=1, source_target_pairs={{0,8},{4,12},{8,0},{12,4},{16,24},{20,28},{24,16},{28,20},{1,9},{5... | collective-permute-start | bytes 737288 | tf_op jit(solution)/shard_map/ppermute | solution.py:34
  308.6 13.3 %collective-permute-start.43 = (bf16[2,96,768]{2,1,0:T(8,128)(2,1)S(1)}, bf16[2,96,768]{2,1,0:T(8,128)(2,1)S(1)}, u32[]{:S(2)}, u32[]{:S(2)}) collective-permute-start(bf16[2,96,768]{2,1,0:T(8,128)(2,1)S(1)} %pad_maximum_fusion.9), channel_id=1, source_target_pairs={{0,16},{4,20},{8,24},{12,28},{16,0},{20,4},{24,8},{28,12},{1,17},{... | collective-permute-start | bytes 884744 | tf_op jit(solution)/shard_map/ppermute | solution.py:34
  317.2 5.6 %collective-permute-start.48 = (bf16[24,3072]{1,0:T(8,128)(2,1)S(1)}, bf16[24,3072]{1,0:T(8,128)(2,1)S(1)}, u32[]{:S(2)}, u32[]{:S(2)}) collective-permute-start(bf16[24,3072]{1,0:T(8,128)(2,1)S(1)} %get-tuple-element.220), channel_id=1, source_target_pairs={{0,1},{1,2},{2,3},{3,0},{4,5},{5,6},{6,7},{7,4},{8,9},{9,10},{10,1... | collective-permute-start | bytes 442376 | tf_op jit(solution)/shard_map/ppermute | solution.py:150
  317.3 12.1 %collective-permute-start.49 = (bf16[24,3072]{1,0:T(8,128)(2,1)S(1)}, bf16[24,3072]{1,0:T(8,128)(2,1)S(1)}, u32[]{:S(2)}, u32[]{:S(2)}) collective-permute-start(bf16[24,3072]{1,0:T(8,128)(2,1)S(1)} %get-tuple-element.222), channel_id=1, source_target_pairs={{0,2},{1,3},{2,0},{3,1},{4,6},{5,7},{6,4},{7,5},{8,10},{9,11},{10,... | collective-permute-start | bytes 442376 | tf_op jit(solution)/shard_map/ppermute | solution.py:150
  318.2 13.2 %collective-permute-start.50 = (bf16[24,3072]{1,0:T(8,128)(2,1)S(1)}, bf16[24,3072]{1,0:T(8,128)(2,1)S(1)}, u32[]{:S(2)}, u32[]{:S(2)}) collective-permute-start(bf16[24,3072]{1,0:T(8,128)(2,1)S(1)} %get-tuple-element.221), channel_id=1, source_target_pairs={{0,3},{1,0},{2,1},{3,2},{4,7},{5,4},{6,5},{7,6},{8,11},{9,8},{10,9... | collective-permute-start | bytes 442376 | tf_op jit(solution)/shard_map/ppermute | solution.py:150
  321.0 11.7 %collective-permute-start.40 = (bf16[96,2048]{1,0:T(8,128)(2,1)S(1)}, bf16[96,2048]{1,0:T(8,128)(2,1)S(1)}, u32[]{:S(2)}, u32[]{:S(2)}) collective-permute-start(bf16[96,2048]{1,0:T(8,128)(2,1)S(1)} %dynamic-slice_bitcast_fusion.13), channel_id=1, source_target_pairs={{0,16},{4,20},{8,24},{12,28},{16,0},{20,4},{24,8},{28,12},{1,17},{... | collective-permute-start | bytes 1179656 | tf_op jit(solution)/shard_map/ppermute | solution.py:34
  321.9 10.7 %collective-permute-start.42 = (bf16[96,640]{1,0:T(8,128)(2,1)S(1)}, bf16[96,640]{1,0:T(8,128)(2,1)S(1)}, u32[]{:S(2)}, u32[]{:S(2)}) collective-permute-start(bf16[96,640]{1,0:T(8,128)(2,1)S(1)} %dynamic-slice_bitcast_fusion.27), channel_id=1, source_target_pairs={{0,16},{4,20},{8,24},{12,28},{16,0},{20,4},{24,8},{28,12},{1,17},{... | collective-permute-start | bytes 368648 | tf_op jit(solution)/shard_map/ppermute | solution.py:34
  322.8 9.8 %collective-permute-start.44 = (bf16[96,768]{1,0:T(8,128)(2,1)S(1)}, bf16[96,768]{1,0:T(8,128)(2,1)S(1)}, u32[]{:S(2)}, u32[]{:S(2)}) collective-permute-start(bf16[96,768]{1,0:T(8,128)(2,1)S(1)} %dynamic-slice_bitcast_fusion.26), channel_id=1, source_target_pairs={{0,8},{4,12},{8,0},{12,4},{16,24},{20,28},{24,16},{28,20},{1,9},{5... | collective-permute-start | bytes 442376 | tf_op jit(solution)/shard_map/ppermute | solution.py:34
  332.9 5.4 %collective-permute-start.45 = (bf16[24,3456]{1,0:T(8,128)(2,1)S(1)}, bf16[24,3456]{1,0:T(8,128)(2,1)S(1)}, u32[]{:S(2)}, u32[]{:S(2)}) collective-permute-start(bf16[24,3456]{1,0:T(8,128)(2,1)S(1)} %get-tuple-element.214), channel_id=1, source_target_pairs={{0,1},{1,2},{2,3},{3,0},{4,5},{5,6},{6,7},{7,4},{8,9},{9,10},{10,1... | collective-permute-start | bytes 497672 | tf_op jit(solution)/shard_map/ppermute | solution.py:150
  334.5 13.7 %collective-permute-start.46 = (bf16[24,3456]{1,0:T(8,128)(2,1)S(1)}, bf16[24,3456]{1,0:T(8,128)(2,1)S(1)}, u32[]{:S(2)}, u32[]{:S(2)}) collective-permute-start(bf16[24,3456]{1,0:T(8,128)(2,1)S(1)} %get-tuple-element.216), channel_id=1, source_target_pairs={{0,2},{1,3},{2,0},{3,1},{4,6},{5,7},{6,4},{7,5},{8,10},{9,11},{10,... | collective-permute-start | bytes 497672 | tf_op jit(solution)/shard_map/ppermute | solution.py:150
  337.5 13.8 %collective-permute-start.47 = (bf16[24,3456]{1,0:T(8,128)(2,1)S(1)}, bf16[24,3456]{1,0:T(8,128)(2,1)S(1)}, u32[]{:S(2)}, u32[]{:S(2)}) collective-permute-start(bf16[24,3456]{1,0:T(8,128)(2,1)S(1)} %get-tuple-element.215), channel_id=1, source_target_pairs={{0,3},{1,0},{2,1},{3,2},{4,7},{5,4},{6,5},{7,6},{8,11},{9,8},{10,9... | collective-permute-start | bytes 497672 | tf_op jit(solution)/shard_map/ppermute | solution.py:150
  (29 other events, 112.8 us)
